TPU v7x, 256 devices: a whole 4x4x8 slice. The times are simulated.
256 devices in a mesh: freq: 32 (over x, y, core), node: 8 (over z).
Axes of the slice: x: 4, y: 4, z: 8, core: 2. Of those that a mesh axis runs over, the one named last changes fastest.
Arguments:
- pressure: bfloat16 [2, 128, 4, 65536], P(None, 'freq', None, 'node'), may hold values from -6 to 6
- spectrum_amp: float32 [4, 128], replicated, may hold values from 0.03 to 0.3
- phase_code: int32 [4, 128], replicated, may hold values from 0 to 4095
- panel_tile: int32 [32, 8, 256, 1], P('freq'), may hold values from 0 to 255; in each aligned block of 2048 rows (0 to 2047, 2048 to 4095, ..., all dimensions but the last counted through in order) at most 12 rows name the same one
- patch_weight: bfloat16 [32, 8, 256, 128], P('freq'), may hold values from 0 to 0.099609375
Outputs:
- node_loads: bfloat16 [4, 4096, 32768], P(None, 'node', 'freq')
Inputs may be any that keep to these rules, and one draw needn't show every extreme that they name: Within each block panel_tile[g] (2048 panels), no patch is named by more than 12 panels, a bound that some block reaches; every patch is named somewhere.
All inputs are finite; a program needn't handle non-finite values.
Results may differ from a plain program's by a relative error of at most 0.0062.
Values may be sent and summed in bfloat16 or wider, within the bound.
No kernel may reach another device: no remote copies, remote signals or barrier semaphores. Data moves between devices by JAX's collectives and lax.ppermute only.
A program may use at most 128 MiB of HBM per device.

v0:
```python
import math

import jax
import jax.numpy as jnp
from jax import lax
from jax.sharding import PartitionSpec as P

F = 128
TSTEPS = 4096
BIN_STEP = 15
PHASE_LEVELS = 4096
TILE_DEV = 8


def scale_spectra(pressure, spectrum_amp, phase_code):
    phase_angle = phase_code.astype(jnp.float32) * (2.0 * math.pi / PHASE_LEVELS)
    amplitude = spectrum_amp.T[:, :, None]
    cosine = jnp.cos(phase_angle).T[:, :, None]
    sine_part = jnp.sin(phase_angle).T[:, :, None]
    real_part = pressure[0].astype(jnp.float32)
    imag_part = pressure[1].astype(jnp.float32)
    scaled_re = amplitude * (real_part * cosine - imag_part * sine_part)
    scaled_im = amplitude * (real_part * sine_part + imag_part * cosine)
    return jnp.stack([scaled_re, scaled_im]).astype(jnp.bfloat16)


def basis_table(step_count):
    freq_bin = 1 + BIN_STEP * jnp.arange(F, dtype=jnp.int32)
    step_ids = jnp.arange(step_count, dtype=jnp.int32)
    turn_count = freq_bin[:, None] * step_ids[None, :] % TSTEPS
    turn_angle = turn_count.astype(jnp.float32) * (2.0 * math.pi / TSTEPS)
    return jnp.concatenate([jnp.cos(turn_angle), -jnp.sin(turn_angle)], axis=0).astype(jnp.bfloat16)


def slot_members(tile_ids, tile_count, capacity):
    row_count = tile_ids.shape[0]
    onehot = (tile_ids[:, None] == jnp.arange(tile_count, dtype=jnp.int32)[None, :]).astype(
        jnp.int32
    )
    slot_rank = jnp.sum((jnp.cumsum(onehot, axis=0) - onehot) * onehot, axis=1)
    slot_index = tile_ids * capacity + slot_rank
    empty = jnp.full((tile_count * capacity,), row_count, jnp.int32)
    return empty.at[slot_index].set(jnp.arange(row_count, dtype=jnp.int32))


def shards(pressure, spectrum_amp, phase_code, panel_tile, patch_weight):
    regrouped = lax.all_to_all(pressure, "freq", split_axis=3, concat_axis=1, tiled=True)
    scaled = scale_spectra(regrouped, spectrum_amp, phase_code)
    freq_count = scaled.shape[1]
    headings = scaled.shape[2]
    panels = scaled.shape[3]
    owners = lax.axis_size("freq")
    windows = lax.axis_size("node")
    window_len = TSTEPS // windows
    tile_count = owners * TILE_DEV
    capacity = max(2, 3 * windows * panels // (2 * TILE_DEV * owners))
    tile_ids = panel_tile.reshape(-1)
    weights = patch_weight.reshape(-1, 128)
    members = slot_members(tile_ids, tile_count, capacity)
    sent_weight = jnp.take(weights, members, axis=0, mode="fill", fill_value=0)
    sent_weight = sent_weight.reshape(1, owners, TILE_DEV, capacity, 128)
    wave_basis = basis_table(TSTEPS)
    series = jnp.einsum(
        "khp,kt->hpt",
        scaled.reshape(2 * freq_count, headings, panels),
        wave_basis,
        preferred_element_type=jnp.float32,
    ).astype(jnp.bfloat16)
    window = lax.all_to_all(series, "node", split_axis=2, concat_axis=1, tiled=True)
    sent_rows = jnp.take(window, members, axis=1, mode="fill", fill_value=0)
    sent_rows = sent_rows.reshape(headings, owners, TILE_DEV, capacity, window_len)
    got_rows = lax.all_to_all(sent_rows, "freq", split_axis=1, concat_axis=1, tiled=True)
    got_weight = lax.all_to_all(sent_weight, "freq", split_axis=1, concat_axis=1, tiled=True)
    partial_value = jnp.einsum(
        "hskcw,skcn->hwkn", got_rows, got_weight[0], preferred_element_type=jnp.float32
    )
    node_loads = partial_value.reshape(partial_value.shape[0], partial_value.shape[1], -1)
    return node_loads.astype(jnp.bfloat16)


def solution(mesh):
    placed = (
        P(None, "freq", None, "node"),
        P(),
        P(),
        P("freq", None, None, None),
        P("freq", None, None, None),
    )
    return jax.shard_map(
        shards, mesh=mesh, in_specs=placed, out_specs=P(None, "node", "freq"), check_vma=False
    )
```

profile of v0, /device:TPU:2, one launch (start us, length us, event | category | flops | bytes accessed | tf_op | source)
XLA Modules:
  0.0 610.8 jit_solution(6448219081164938519)
XLA Ops:
  0.0 0.0 copy-start
  0.0 18.4 %copy.63 = bf16[2,4,4,8192]{2,1,0,3:T(4,128)(2,1)} copy(bf16[2,4,4,8192]{3,2,1,0:T(4,128)(2,1)} %param.5) | data formatting | bytes 1048576 | tf_op args[0]
  18.4 0.0 copy-start.3
  18.4 0.0 copy-start.4
  18.4 31.9 %reshape.201 = bf16[32,2,4096]{2,1,0:T(2,128)(2,1)} reshape(bf16[8192,2,4,4]{3,2,1,0:T(4,128)(2,1)} %bitcast.53) | data formatting | bytes 1048576
  50.2 7.6 %all-to-all-start.1 = ((bf16[32,2,4096]{2,1,0:T(2,128)(2,1)}), bf16[32,2,4096]{2,1,0:T(2,128)(2,1)S(1)}, u32[]{:S(2)}, u32[]{:S(2)}) async-start(bf16[32,2,4096]{2,1,0:T(2,128)(2,1)} %reshape.201), calls=%async_computation.1 | async-start | bytes 1048576 | tf_op jit(solution)/shard_map/all_to_all | solution.py:47
  57.9 0.0 copy-done.3
  57.9 0.1 copy.65
  58.1 0.1 copy.66
  58.2 0.0 copy-done.4
  58.2 0.1 copy.62
  58.3 9.0 %cosine_convert_fusion = (bf16[128,4096]{1,0:T(8,128)(2,1)S(1)}, bf16[128,4096]{1,0:T(8,128)(2,1)S(1)}) fusion(s32[128]{0:T(128)S(1)} %multiply_add_fusion), kind=kLoop, calls=%fused_computation.22 | loop fusion | flops 8912896 | bytes 2097664 | tf_op jit(solution)/shard_map/convert.2
  67.3 0.4 all-to-all-done.1
  67.7 37.1 %reshape.202 = bf16[8192,2,4,4]{3,2,1,0:T(4,128)(2,1)} reshape(bf16[32,2,4096]{2,1,0:T(2,128)(2,1)S(1)} %all-to-all-done.1) | data formatting | bytes 1048576
  104.8 22.6 %copy.64 = bf16[2,4,4,32,256]{4,2,1,3,0:T(4,128)(2,1)S(1)} copy(bf16[2,4,4,32,256]{2,1,0,4,3:T(4,128)(2,1)} %bitcast.52) | data formatting | bytes 1048576 | tf_op jit(solution)/shard_map/all_to_all | solution.py:47
  127.4 0.2 fusion.30
  127.6 0.5 fusion.21
  128.1 0.4 pad_maximum_fusion
  128.5 5.6 convolution_convert_fusion
  134.1 13.6 %copy.68 = bf16[4,256,4096]{1,0,2:T(4,128)(2,1)} copy(bf16[4,256,4096]{2,1,0:T(8,128)(2,1)} %convolution_convert_fusion) | data formatting | bytes 16777216 | tf_op jit(solution)/shard_map/convert_element_type | solution.py:68
  147.7 0.0 copy-start.2
  147.7 8.6 %all-to-all-start.2 = ((bf16[4,256,4096]{1,0,2:T(4,128)(2,1)}), bf16[4,256,4096]{1,0,2:T(4,128)(2,1)}, u32[]{:S(2)}, u32[]{:S(2)}) async-start(bf16[4,256,4096]{1,0,2:T(4,128)(2,1)} %copy.68), calls=%async_computation.2 | async-start | bytes 16777216 | tf_op jit(solution)/shard_map/all_to_all | solution.py:69
  156.3 0.0 copy-done.2
  156.3 0.1 copy.58
  156.4 0.3 fusion.14
  156.8 0.2 broadcast_add_fusion
  157.0 1.2 copy.59
  158.3 0.9 fusion.11
  159.3 8.1 %scatter_custom_fusion = s32[3072]{0:T(1024)S(1)} fusion(s32[2048]{0:T(1024)S(1)} %bitcast.67, s32[2048]{0:T(1024)S(1)} %iota.22, s32[]{:T(128)} %constant.33.clone.1), kind=kCustom, calls=%fused_computation.51 | custom fusion | bytes 12292 | tf_op jit(solution)/shard_map/scatter | solution.py:43
  167.3 0.2 broadcast_in_dim.35
  167.5 0.0 copy-done
  167.5 9.2 %gather_fusion = bf16[3072,128]{1,0:T(8,128)(2,1)S(1)} fusion(bf16[2048,128]{1,0:T(8,128)(2,1)S(1)} %bitcast.51, s32[3072]{0:T(1024)S(1)} %fusion.26), kind=kCustom, calls=%fused_computation | custom fusion | bytes 1585152 | tf_op jit(solution)/shard_map/jit(_take)/gather | solution.py:60
  176.7 0.2 gather.13
  176.9 0.7 broadcast_select_fusion.1
  177.6 1.1 copy.60
  178.7 165.2 %all-to-all-done.2 = bf16[4,256,4096]{1,0,2:T(4,128)(2,1)} async-done(((bf16[4,256,4096]{1,0,2:T(4,128)(2,1)}), bf16[4,256,4096]{1,0,2:T(4,128)(2,1)}, u32[]{:S(2)}, u32[]{:S(2)}) %all-to-all-start.2) | async-done | bytes 8388640 | tf_op jit(solution)/shard_map/all_to_all | solution.py:69
  343.9 6.3 %all-to-all-start = ((bf16[1,32,8,12,128]{4,2,3,0,1:T(8,128)(2,1)}), bf16[1,32,8,12,128]{4,2,3,0,1:T(8,128)(2,1)S(1)}, u32[]{:S(2)}, u32[]{:S(2)}) async-start(bf16[1,32,8,12,128]{4,2,3,0,1:T(8,128)(2,1)} %copy.60), calls=%async_computation | async-start | bytes 1572864 | tf_op jit(solution)/shard_map/all_to_all | solution.py:73
  350.2 7.7 %copy.69 = bf16[4,256,4096]{1,2,0:T(8,128)(2,1)} copy(bf16[4,256,4096]{1,0,2:T(4,128)(2,1)} %all-to-all-done.2) | data formatting | bytes 16777216 | tf_op jit(solution)/shard_map/all_to_all | solution.py:69
  357.9 11.4 %copy.70 = bf16[4,8,256,512]{3,2,1,0:T(8,128)(2,1)} copy(bf16[4,8,256,512]{2,3,1,0:T(8,128)(2,1)} %bitcast.55) | data formatting | bytes 16777216 | tf_op jit(solution)/shard_map/all_to_all | solution.py:69
  369.3 12.1 %copy.71 = bf16[4,2048,512]{2,0,1:T(4,128)(2,1)} copy(bf16[4,2048,512]{2,1,0:T(8,128)(2,1)} %bitcast.56) | data formatting | bytes 16777216 | tf_op jit(solution)/shard_map/all_to_all | solution.py:69
  381.4 34.7 %gather_fusion.1 = bf16[3072,4,512]{2,1,0:T(4,128)(2,1)} fusion(bf16[4,2048,512]{2,0,1:T(4,128)(2,1)} %copy.71, s32[3072]{0:T(1024)S(1)} %fusion.26), kind=kCustom, calls=%fused_computation.1 | custom fusion | bytes 25178112 | tf_op jit(solution)/shard_map/jit(_take)/gather | solution.py:70
  416.2 9.1 %broadcast_select_fusion = bf16[4,32,8,12,512]{4,0,3,2,1:T(4,128)(2,1)S(1)} fusion(bf16[4,32,8,12,512]{4,0,3,2,1:T(4,128)(2,1)} %bitcast.54, pred[32,8,12]{2,1,0:T(8,128)(4,1)S(1)} %broadcast_in_dim.35), kind=kLoop, calls=%fused_computation.5 | loop fusion | flops 6291456 | bytes 25168896 | tf_op jit(solution)/shard_map/jit(_take)/select_n | solution.py:70
  425.3 11.4 %copy.72 = bf16[4,32,8,12,512]{4,2,3,0,1:T(8,128)(2,1)} copy(bf16[4,32,8,12,512]{4,0,3,2,1:T(4,128)(2,1)S(1)} %broadcast_select_fusion) | data formatting | bytes 25165824 | tf_op jit(solution)/shard_map/jit(_take)/select_n | solution.py:70
  436.7 0.0 all-to-all-done
  436.7 145.4 %all_to_all.43 = bf16[4,32,8,12,512]{4,2,3,0,1:T(8,128)(2,1)S(1)} all-to-all(bf16[4,32,8,12,512]{4,2,3,0,1:T(8,128)(2,1)} %copy.72), channel_id=1, replica_groups=mesh['freq'=32,'node'=8] {'freq'}, dimensions={1} | all-to-all | bytes 25165824 | tf_op jit(solution)/shard_map/all_to_all | solution.py:72
  582.1 17.9 %fusion.2 = bf16[4,512,8,128]{1,3,0,2:T(8,128)(2,1)} fusion(bf16[4,32,8,12,512]{4,2,3,0,1:T(8,128)(2,1)S(1)} %all_to_all.43, bf16[32,8,12,128,1]{3,1,2,0,4:T(8,128)(2,1)S(1)} %bitcast.62), kind=kOutput, calls=%fused_computation.8 | convolution fusion | flops 1612709888 | bytes 17563648 | tf_op jit(solution)/shard_map/hskcw,skcn->hwkn/dot_general | solution.py:74
  600.0 4.6 copy.74
  604.5 0.0 copy-start.1
  604.5 6.2 %copy.75 = bf16[4,512,1024]{2,1,0:T(8,128)(2,1)} copy(bf16[4,512,1024]{1,2,0:T(8,128)(2,1)} %bitcast.57) | data formatting | bytes 8388608 | tf_op jit(solution)/shard_map/convert_element_type | solution.py:78
  610.8 0.0 copy-done.1
  (10 shorter events, 0.1 us)
Async XLA Ops:
  0.0 167.5 %copy-start = (bf16[1,8,256,128]{3,2,1,0:T(8,128)(2,1)S(1)}, bf16[1,8,256,128]{3,2,1,0:T(8,128)(2,1)}, u32[]{:S(2)}) copy-start(bf16[1,8,256,128]{3,2,1,0:T(8,128)(2,1)} %param.9) | copy-start | bytes 1572868
  18.4 39.5 %copy-start.3 = (s32[4,128]{1,0:T(4,128)S(1)}, s32[4,128]{1,0:T(4,128)}, u32[]{:S(2)}) copy-start(s32[4,128]{1,0:T(4,128)} %param.7) | copy-start | bytes 6148
  18.4 39.8 %copy-start.4 = (f32[4,128]{1,0:T(4,128)S(1)}, f32[4,128]{1,0:T(4,128)}, u32[]{:S(2)}) copy-start(f32[4,128]{1,0:T(4,128)} %param.6) | copy-start | bytes 6148
  50.2 17.4 %all-to-all-start.1 = ((bf16[32,2,4096]{2,1,0:T(2,128)(2,1)}), bf16[32,2,4096]{2,1,0:T(2,128)(2,1)S(1)}, u32[]{:S(2)}, u32[]{:S(2)}) async-start(bf16[32,2,4096]{2,1,0:T(2,128)(2,1)} %reshape.201), calls=%async_computation.1 | async-start | bytes 1048576 | tf_op jit(solution)/shard_map/all_to_all | solution.py:47
  147.7 8.6 %copy-start.2 = (s32[1,8,256,1]{2,3,1,0:T(1,128)S(1)}, s32[1,8,256,1]{2,3,1,0:T(1,128)}, u32[]{:S(2)}) copy-start(s32[1,8,256,1]{2,3,1,0:T(1,128)} %param.8) | copy-start | bytes 24580
  147.7 196.2 %all-to-all-start.2 = ((bf16[4,256,4096]{1,0,2:T(4,128)(2,1)}), bf16[4,256,4096]{1,0,2:T(4,128)(2,1)}, u32[]{:S(2)}, u32[]{:S(2)}) async-start(bf16[4,256,4096]{1,0,2:T(4,128)(2,1)} %copy.68), calls=%async_computation.2 | async-start | bytes 16777216 | tf_op jit(solution)/shard_map/all_to_all | solution.py:69
  343.9 92.8 %all-to-all-start = ((bf16[1,32,8,12,128]{4,2,3,0,1:T(8,128)(2,1)}), bf16[1,32,8,12,128]{4,2,3,0,1:T(8,128)(2,1)S(1)}, u32[]{:S(2)}, u32[]{:S(2)}) async-start(bf16[1,32,8,12,128]{4,2,3,0,1:T(8,128)(2,1)} %copy.60), calls=%async_computation | async-start | bytes 1572864 | tf_op jit(solution)/shard_map/all_to_all | solution.py:73
  604.5 6.3 %copy-start.1 = (bf16[1,8,256,128]{3,2,1,0:T(8,128)(2,1)S(1)}, bf16[1,8,256,128]{3,2,1,0:T(8,128)(2,1)}, u32[]{:S(2)}) copy-start(bf16[1,8,256,128]{3,2,1,0:T(8,128)(2,1)} %param.9) | copy-start | bytes 1572868
where the time goes:
time: 618 us; the launch traced here: 611 us
  local copies, waits for them, and re-layouts  232 us (38%)
  waiting for transfers between devices  166 us (27%)
  blocking collectives  145 us (23%)
  matrix products  23.5 us (4%)
  starting transfers between devices  22.6 us (4%)
  other arithmetic  21.3 us (3%)
    all_to_all x1, waiting for transfers between devices, shards(): lax.all_to_all(series, 'node', split_axis=2, concat_axis=1, tiled=True)  165 us
    all_to_all x1, blocking collectives, shards(): lax.all_to_all(sent_rows, 'freq', split_axis=1, concat_axis=1, tiled=True)  145 us
    unnamed x13, local copies, waits for them, and re-layouts  87.4 us
    gather x1, local copies, waits for them, and re-layouts, shards(): sent_rows = jnp.take(window, members, axis=1, mode='fill', fill_value=0)  34.7 us
    all_to_all x3, local copies, waits for them, and re-layouts, shards(): lax.all_to_all(series, 'node', split_axis=2, concat_axis=1, tiled=True)  31.2 us
    all_to_all x1, local copies, waits for them, and re-layouts, shards(): lax.all_to_all(pressure, 'freq', split_axis=3, concat_axis=1, tiled=True)  22.6 us
    dot_general x1, matrix products, shards(): jnp.einsum('hskcw,skcn->hwkn', got_rows, got_weight[0], preferred_element...  17.9 us
    convert_element_type x1, local copies, waits for them, and re-layouts, shards(): series = jnp.einsum('khp,kt->hpt', scaled.reshape(2 * freq_count, heading...  13.6 us
  transfers between devices with their start and end apart: 3, of which 2 were waited for; matrix products, arithmetic and copies ran while one was open for 19% of the time, Pallas kernels for 0%

commit v1 on v0

v1 whole, which is shorter than its diff:
```python
import math

import jax
import jax.numpy as jnp
from jax import lax
from jax.experimental import pallas as pl
from jax.experimental.pallas import tpu as pltpu
from jax.sharding import PartitionSpec as P

F = 128
TSTEPS = 4096
BIN_STEP = 15
PHASE_LEVELS = 4096
TILE_DEV = 8
BF = jnp.bfloat16
F32 = jnp.float32


def scale_kernel(group_ref, pressure_ref, amp_ref, code_ref, out_ref):
    owners, width = out_ref.shape[0], out_ref.shape[3]
    fl_count = pressure_ref.shape[1]
    lane = lax.broadcasted_iota(jnp.int32, amp_ref.shape, 1)
    angle = code_ref[...].astype(F32) * (2.0 * math.pi / PHASE_LEVELS)
    cosine, sine = jnp.cos(angle), jnp.sin(angle)
    amp = amp_ref[...]
    for fl in range(fl_count):
        chosen = lane == group_ref[0] * fl_count + fl

        def pick(table):
            return jnp.sum(jnp.where(chosen, table, 0.0), axis=1, keepdims=True)

        a, c, s = pick(amp), pick(cosine), pick(sine)

        for g in range(owners):
            cols = pl.ds(g * width, width)
            re = pressure_ref[0, fl, :, cols].astype(F32)
            im = pressure_ref[1, fl, :, cols].astype(F32)
            out_ref[g, fl] = (a * (re * c - im * s)).astype(BF)
            out_ref[g, fl_count + fl] = (a * (re * s + im * c)).astype(BF)


def scale_spectra(pressure, spectrum_amp, phase_code, group, owners):
    parts, fl_count, headings, panels = pressure.shape
    width = panels // owners
    return pl.pallas_call(
        scale_kernel,
        out_shape=jax.ShapeDtypeStruct((owners, parts * fl_count, headings, width), BF),
        in_specs=[
            pl.BlockSpec(memory_space=pltpu.SMEM),
            pl.BlockSpec(memory_space=pltpu.VMEM),
            pl.BlockSpec(memory_space=pltpu.VMEM),
            pl.BlockSpec(memory_space=pltpu.VMEM),
        ],
        out_specs=pl.BlockSpec(memory_space=pltpu.VMEM),
        cost_estimate=pl.CostEstimate(flops=2_000_000, bytes_accessed=1 << 20, transcendentals=0),
        name="scale",
    )(group.reshape(1), pressure, spectrum_amp, phase_code)


def fill_tilehot(tile_ref, hot_ref, tile_count):
    blocks, width = tile_ref.shape
    tile_iota = lax.broadcasted_iota(jnp.int32, (tile_count, width), 0)
    for k in range(blocks):
        hot = tile_iota == tile_ref[k : k + 1, :]
        hot_ref[:, k * width : (k + 1) * width] = jnp.where(hot, 1.0, 0.0).astype(BF)


def gather_slots(hot_ref, rank_ref, source_ref, out_ref, transposed):
    blocks, width = rank_ref.shape
    owners, capacity, tiles, lanes = out_ref.shape

    def one(s, carry):
        total = jnp.zeros((owners * tiles, lanes), F32)
        for k in range(blocks):
            cols = slice(k * width, (k + 1) * width)
            live = jnp.where(rank_ref[k : k + 1, :] == s.astype(F32), 1.0, 0.0).astype(BF)
            picked = hot_ref[:, cols] * live
            if transposed:
                total += lax.dot_general(
                    picked, source_ref[:, cols], (((1,), (1,)), ((), ())),
                    preferred_element_type=F32,
                )
            else:
                total += jnp.dot(picked, source_ref[cols, :], preferred_element_type=F32)
        out_ref[:, pl.ds(s, 1)] = total.astype(BF).reshape(owners, 1, tiles, lanes)
        return carry

    lax.fori_loop(0, capacity, one, 0)


def weight_kernel(tile_ref, weight_ref, out_ref, rank_ref, hot_ref):
    owners, _, tiles, _ = out_ref.shape
    blocks, width = tile_ref.shape
    fill_tilehot(tile_ref, hot_ref, owners * tiles)
    before = (
        lax.broadcasted_iota(jnp.int32, (width, width), 0)
        < lax.broadcasted_iota(jnp.int32, (width, width), 1)
    )
    before = jnp.where(before, 1.0, 0.0).astype(BF)
    seen = jnp.zeros((owners * tiles, 1), F32)
    for k in range(blocks):
        hot = hot_ref[:, k * width : (k + 1) * width]
        hot32 = hot.astype(F32)
        earlier = jnp.dot(hot, before, preferred_element_type=F32) + seen
        rank_ref[k : k + 1, :] = jnp.sum(hot32 * earlier, axis=0, keepdims=True)
        seen = seen + jnp.sum(hot32, axis=1, keepdims=True)
    gather_slots(hot_ref, rank_ref, weight_ref, out_ref, False)


def gather_weights(tile_ids, weights, owners, capacity):
    blocks, width = tile_ids.shape
    lanes = weights.shape[1]
    return pl.pallas_call(
        weight_kernel,
        out_shape=(
            jax.ShapeDtypeStruct((owners, capacity, TILE_DEV, lanes), BF),
            jax.ShapeDtypeStruct((blocks, width), F32),
        ),
        in_specs=[pl.BlockSpec(memory_space=pltpu.VMEM)] * 2,
        out_specs=(pl.BlockSpec(memory_space=pltpu.VMEM),) * 2,
        scratch_shapes=[pltpu.VMEM((owners * TILE_DEV, blocks * width), BF)],
        cost_estimate=pl.CostEstimate(
            flops=2 * owners * capacity * TILE_DEV * blocks * width * lanes,
            bytes_accessed=2 << 20, transcendentals=0,
        ),
        name="weight_slots",
    )(tile_ids, weights)


def row_kernel(tile_ref, rank_ref, spectra_ref, out_ref, hot_ref, rows_ref, packed_ref):
    groups, blocks, headings, width = spectra_ref.shape
    owners, _, tiles, _ = out_ref.shape
    fill_tilehot(tile_ref, hot_ref, owners * tiles)
    for k in range(blocks):
        for part in range(width // 128):
            cols = slice(part * 128, (part + 1) * 128)
            slot = k * (width // 128) + part
            for g in range(groups):
                rows_ref[slot, pl.ds(g, headings, stride=groups), :] = (
                    spectra_ref[g, k, :, cols].astype(F32)
                )
            packed_ref[:, slot * 128 : (slot + 1) * 128] = rows_ref[slot].astype(BF)
    gather_slots(hot_ref, rank_ref, packed_ref, out_ref, True)


def gather_rows(tile_ids, rank, spectra, owners, capacity):
    blocks, width = tile_ids.shape
    groups, _, headings, _ = spectra.shape
    lanes = groups * headings
    return pl.pallas_call(
        row_kernel,
        out_shape=jax.ShapeDtypeStruct((owners, capacity, TILE_DEV, lanes), BF),
        in_specs=[pl.BlockSpec(memory_space=pltpu.VMEM)] * 3,
        out_specs=pl.BlockSpec(memory_space=pltpu.VMEM),
        scratch_shapes=[
            pltpu.VMEM((owners * TILE_DEV, blocks * width), BF),
            pltpu.VMEM((blocks * width // 128, lanes, 128), F32),
            pltpu.VMEM((lanes, blocks * width), BF),
        ],
        cost_estimate=pl.CostEstimate(
            flops=2 * owners * capacity * TILE_DEV * blocks * width * lanes,
            bytes_accessed=2 << 20, transcendentals=0,
        ),
        name="row_slots",
    )(tile_ids, rank, spectra)


def node_kernel(rows_ref, weight_ref, out_ref, rows32_ref, weight32_ref):
    count, lanes = rows_ref.shape
    rows32_ref[...] = rows_ref[...].astype(F32)
    weight32_ref[...] = weight_ref[...].astype(F32)
    for tile in range(TILE_DEV):
        own = pl.ds(tile, count // TILE_DEV, stride=TILE_DEV)
        part = lax.dot_general(
            rows32_ref[own, :].astype(BF), weight32_ref[own, :].astype(BF),
            (((0,), (0,)), ((), ())), preferred_element_type=F32,
        )
        out_ref[:, tile * 128 : (tile + 1) * 128] = part.astype(BF)


def node_spectra(rows, weights):
    count, lanes = rows.shape
    return pl.pallas_call(
        node_kernel,
        out_shape=jax.ShapeDtypeStruct((lanes, TILE_DEV * 128), BF),
        in_specs=[pl.BlockSpec(memory_space=pltpu.VMEM)] * 2,
        out_specs=pl.BlockSpec(memory_space=pltpu.VMEM),
        scratch_shapes=[pltpu.VMEM((count, lanes), F32), pltpu.VMEM((count, 128), F32)],
        cost_estimate=pl.CostEstimate(
            flops=2 * count * lanes * 128, bytes_accessed=2 << 20, transcendentals=0
        ),
        name="node_spectra",
    )(rows, weights)


def history_kernel(basis_ref, *refs):
    out_ref = refs[-1]
    spectra = jnp.concatenate([r[...] for r in refs[:-1]], axis=0)
    out_ref[0] = jnp.dot(basis_ref[...], spectra, preferred_element_type=F32).astype(BF)


def histories(basis, chunks, headings):
    steps = basis.shape[0]
    lanes, nodes = chunks[0].shape
    group = lanes // headings
    return pl.pallas_call(
        history_kernel,
        grid=(headings,),
        out_shape=jax.ShapeDtypeStruct((headings, steps, nodes), BF),
        in_specs=[pl.BlockSpec(basis.shape, lambda h: (0, 0))]
        + [pl.BlockSpec((group, nodes), lambda h: (h, 0))] * len(chunks),
        out_specs=pl.BlockSpec((1, steps, nodes), lambda h: (h, 0, 0)),
        cost_estimate=pl.CostEstimate(
            flops=2 * steps * len(chunks) * lanes * nodes,
            bytes_accessed=6 << 20, transcendentals=0,
        ),
        name="histories",
    )(basis, *chunks)


def window_basis(sources, window, window_len, groups, fl_count):
    source = jnp.repeat(sources, groups)
    group = jnp.tile(jnp.arange(groups, dtype=jnp.int32), sources.shape[0])
    freq_bin = 1 + BIN_STEP * (fl_count * group + source % fl_count)
    step_ids = window * window_len + jnp.arange(window_len, dtype=jnp.int32)
    turn_count = freq_bin[None, :] * step_ids[:, None] % TSTEPS
    turn_angle = turn_count.astype(F32) * (2.0 * math.pi / TSTEPS)
    is_re = (source < fl_count)[None, :]
    return jnp.where(is_re, jnp.cos(turn_angle), -jnp.sin(turn_angle)).astype(BF)


def shards(pressure, spectrum_amp, phase_code, panel_tile, patch_weight):
    owners = lax.axis_size("freq")
    windows = lax.axis_size("node")
    group = lax.axis_index("freq")
    window = lax.axis_index("node")
    _, fl_count, headings, panels = pressure.shape
    width = panels // owners
    capacity = 12
    scaled = scale_spectra(pressure, spectrum_amp, phase_code, group, owners)
    spectra = lax.all_to_all(
        scaled.reshape(owners * windows, headings, width), ("freq", "node"), 0, 0, tiled=True
    ).reshape(owners, windows, headings, width)

    tile_ids = panel_tile.reshape(windows, width)
    weights = patch_weight.reshape(windows * width, 128)
    sent_weight, rank = gather_weights(tile_ids, weights, owners, capacity)
    got_weight = lax.all_to_all(sent_weight, "freq", 0, 0, tiled=True)

    sent_rows = gather_rows(tile_ids, rank, spectra, owners, capacity)
    got_rows = lax.all_to_all(sent_rows, "freq", 0, 0, tiled=True)
    own = node_spectra(got_rows.reshape(-1, owners * headings), got_weight.reshape(-1, 128))

    ahead = [(k, (k + 1) % windows) for k in range(windows)]
    back = [(k, (k - 1) % windows) for k in range(windows)]
    chunks, offsets = [own], [0]
    right = left = own
    for step in range(1, windows // 2 + 1):
        right_next = lax.ppermute(right, "node", ahead)
        chunks.append(right_next)
        offsets.append(-step)
        if step < windows - windows // 2:
            left = lax.ppermute(left, "node", back)
            chunks.append(left)
            offsets.append(step)
        right = right_next
    sources = (window + jnp.asarray(offsets, jnp.int32)) % windows
    basis = window_basis(sources, window, TSTEPS // windows, owners, fl_count)
    return histories(basis, chunks, headings)


def solution(mesh):
    placed = (
        P(None, "freq", None, "node"),
        P(),
        P(),
        P("freq", None, None, None),
        P("freq", None, None, None),
    )
    return jax.shard_map(
        shards, mesh=mesh, in_specs=placed, out_specs=P(None, "node", "freq"), check_vma=False
    )
```

time: 618 us -> 119 us (0.19); the launches traced: 611 us -> 118 us
  local copies, waits for them, and re-layouts: 232 us -> 2.26 us
  waiting for transfers between devices: 166 us -> 37.7 us
  blocking collectives: 145 us -> 18.5 us
  Pallas kernels: 0 us -> 26.7 us
  matrix products: 23.5 us -> 0 us
  other arithmetic: 21.3 us -> 3.19 us
  starting transfers between devices: 22.6 us -> 29.6 us
    all_to_all x3 -> x2, waiting for transfers between devices: 166 us -> 15.1 us  [the longest x1 11.4 us: shards(): lax.all_to_all(scaled.reshape(owners * windows, headings, width), ('freq'...]
    all_to_all x1, blocking collectives: 145 us -> 18.5 us  [shards(): got_rows = lax.all_to_all(sent_rows, 'freq', 0, 0, tiled=True)]
    unnamed x13 -> x21, local copies, waits for them, and re-layouts: 87.4 us -> 2.03 us
    all_to_all x4 -> x0, local copies, waits for them, and re-layouts: 53.8 us -> none  [the longest x3 31.2 us: shards(): lax.all_to_all(series, 'node', split_axis=2, concat_axis=1, tiled=True)]
    gather x3 -> x0, local copies, waits for them, and re-layouts: 44.1 us -> none  [the longest x1 34.7 us: shards(): sent_rows = jnp.take(window, members, axis=1, mode='fill', fill_value=0)]
    pallas_call x0 -> x5, Pallas kernels: none -> 26.7 us  [the longest x1 8.44 us: gather_rows(): pl.pallas_call(row_kernel, out_shape=jax.ShapeDtypeStruct((owners, capaci...]
    convert_element_type x3 -> x0, local copies, waits for them, and re-layouts: 24.4 us -> none  [the longest x1 13.6 us: shards(): series = jnp.einsum('khp,kt->hpt', scaled.reshape(2 * freq_count, heading...]
    dot_general x2 -> x0, matrix products: 23.5 us -> none  [the longest x1 17.9 us: shards(): jnp.einsum('hskcw,skcn->hwkn', got_rows, got_weight[0], preferred_element...]
  transfers between devices with their start and end apart: 3 -> 9, of which waited for: 2 -> 6; matrix products, arithmetic and copies ran while one was open for 19% -> 4% of each run, Pallas kernels for 0% -> 14%
where the time goes in v1:
time: 119 us; the launch traced here: 118 us
  waiting for transfers between devices  37.7 us (32%)
  starting transfers between devices  29.6 us (25%)
  Pallas kernels  26.7 us (22%)
  blocking collectives  18.5 us (16%)
  other arithmetic  3.19 us (3%)
  local copies, waits for them, and re-layouts  2.26 us (2%)
    ppermute x4, waiting for transfers between devices, shards(): right_next = lax.ppermute(right, 'node', ahead)  22.6 us
    all_to_all x1, blocking collectives, shards(): got_rows = lax.all_to_all(sent_rows, 'freq', 0, 0, tiled=True)  18.5 us
    all_to_all x1, starting transfers between devices, shards(): lax.all_to_all(scaled.reshape(owners * windows, headings, width), ('freq'...  14.7 us
    all_to_all x1, waiting for transfers between devices, shards(): lax.all_to_all(scaled.reshape(owners * windows, headings, width), ('freq'...  11.4 us
    ppermute x3, starting transfers between devices, shards(): left = lax.ppermute(left, 'node', back)  8.85 us
    pallas_call x1, Pallas kernels, gather_rows(): pl.pallas_call(row_kernel, out_shape=jax.ShapeDtypeStruct((owners, capaci...  8.44 us
    pallas_call x1, Pallas kernels, gather_weights(): pl.pallas_call(weight_kernel, out_shape=(jax.ShapeDtypeStruct((owners, ca...  7.71 us
    pallas_call x1, Pallas kernels, histories(): pl.pallas_call(history_kernel, grid=(headings,), out_shape=jax.ShapeDtype...  5.34 us
  transfers between devices with their start and end apart: 9, of which 6 were waited for; matrix products, arithmetic and copies ran while one was open for 4% of the time, Pallas kernels for 14%

profile of v1, /device:TPU:2, one launch (start us, length us, event | category | flops | bytes accessed | tf_op | source)
XLA Modules:
  0.0 118.0 jit_solution(12588441658785161840)
XLA Ops:
  0.0 2.3 %scale.1 = bf16[32,8,4,256]{3,2,1,0:T(4,128)(2,1)} custom-call(s32[1]{0:T(128)} %bitcast.1.group_ref, bf16[2,4,4,8192]{3,2,1,0:T(4,128)(2,1)} %pressure_ref.1, f32[4,128]{1,0:T(4,128)} %amp_ref.1, s32[4,128]{1,0:T(4,128)} %code_ref.1), custom_call_target="tpu_custom_call" | custom-call | flops 2000000 | bytes 1048576 | tf_op jit(solution)/shard_map/scale/pallas_call | solution.py:45
  2.3 14.7 %all-to-all-start = ((bf16[256,4,256]{2,1,0:T(4,128)(2,1)}), bf16[256,4,256]{2,1,0:T(4,128)(2,1)S(1)}, u32[]{:S(2)}, u32[]{:S(2)}) async-start(bf16[256,4,256]{2,1,0:T(4,128)(2,1)} %bitcast.11), calls=%async_computation | async-start | bytes 1048576 | tf_op jit(solution)/shard_map/all_to_all | solution.py:241
  17.0 1.3 %copy.9 = s32[1,8,256,1]{2,1,3,0:T(8,128)} copy(s32[1,8,256,1]{2,3,1,0:T(1,128)} %param.9) | data formatting | bytes 16384
  18.3 7.7 %weight_slots.1 = (bf16[32,12,8,128]{3,2,1,0:T(8,128)(2,1)}, f32[8,256]{1,0:T(8,128)}) custom-call(s32[8,256]{1,0:T(8,128)} %bitcast.13, bf16[2048,128]{1,0:T(8,128)(2,1)} %bitcast.15), custom_call_target="tpu_custom_call" | custom-call | flops 1610612736 | bytes 2097152 | tf_op jit(solution)/shard_map/weight_slots/pallas_call | solution.py:113
  26.0 11.4 %all-to-all-done = bf16[256,4,256]{2,1,0:T(4,128)(2,1)S(1)} async-done(((bf16[256,4,256]{2,1,0:T(4,128)(2,1)}), bf16[256,4,256]{2,1,0:T(4,128)(2,1)S(1)}, u32[]{:S(2)}, u32[]{:S(2)}) %all-to-all-start) | async-done | bytes 524320 | tf_op jit(solution)/shard_map/all_to_all | solution.py:241
  37.4 0.0 copy-start.1
  37.4 5.1 %all-to-all-start.2 = ((bf16[32,12,8,128]{3,2,1,0:T(8,128)(2,1)}), bf16[32,12,8,128]{3,2,1,0:T(8,128)(2,1)S(1)}, u32[]{:S(2)}, u32[]{:S(2)}) async-start(bf16[32,12,8,128]{3,2,1,0:T(8,128)(2,1)} %get-tuple-element.8), calls=%async_computation.2 | async-start | bytes 1572864 | tf_op jit(solution)/shard_map/all_to_all | solution.py:248
  42.5 0.0 copy-done.1
  42.5 0.0 copy-start.9
  42.5 8.4 %row_slots.1 = bf16[32,12,8,128]{3,2,1,0:T(8,128)(2,1)} custom-call(s32[8,256]{1,0:T(8,128)} %bitcast.14, f32[8,256]{1,0:T(8,128)} %get-tuple-element.7.rank_ref, bf16[32,8,4,256]{3,2,1,0:T(4,128)(2,1)} %bitcast.12), custom_call_target="tpu_custom_call" | custom-call | flops 1610612736 | bytes 2097152 | tf_op jit(solution)/shard_map/row_slots/pallas_call | solution.py:150
  50.9 3.6 %all-to-all-done.2 = bf16[32,12,8,128]{3,2,1,0:T(8,128)(2,1)S(1)} async-done(((bf16[32,12,8,128]{3,2,1,0:T(8,128)(2,1)}), bf16[32,12,8,128]{3,2,1,0:T(8,128)(2,1)S(1)}, u32[]{:S(2)}, u32[]{:S(2)}) %all-to-all-start.2) | async-done | bytes 786464 | tf_op jit(solution)/shard_map/all_to_all | solution.py:248
  54.6 0.0 copy-start
  54.6 18.5 %all_to_all.15 = bf16[32,12,8,128]{3,2,1,0:T(8,128)(2,1)} all-to-all(bf16[32,12,8,128]{3,2,1,0:T(8,128)(2,1)} %row_slots.1), channel_id=1, replica_groups=mesh['freq'=32,'node'=8] {'freq'}, dimensions={0} | all-to-all | bytes 1572864 | tf_op jit(solution)/shard_map/all_to_all | solution.py:251
  73.1 0.0 copy-done
  73.1 2.9 %node_spectra.1.refs_0_ = bf16[128,1024]{1,0:T(8,128)(2,1)} custom-call(bf16[3072,128]{1,0:T(8,128)(2,1)} %bitcast.10, bf16[3072,128]{1,0:T(8,128)(2,1)} %bitcast.9), custom_call_target="tpu_custom_call" | custom-call | flops 100663296 | bytes 2097152 | tf_op jit(solution)/shard_map/node_spectra/pallas_call | solution.py:183
  76.0 1.0 collective-permute-start
  77.0 2.2 %collective-permute-start.1 = (bf16[128,1024]{1,0:T(8,128)(2,1)}, bf16[128,1024]{1,0:T(8,128)(2,1)S(1)}, u32[]{:S(2)}, u32[]{:S(2)}) collective-permute-start(bf16[128,1024]{1,0:T(8,128)(2,1)} %node_spectra.1.refs_0_), channel_id=1, source_target_pairs={{0,7},{1,0},{2,1},{3,2},{4,3},{5,4},{6,5},{7,6},{8,15},{9,8},{10,9... | collective-permute-start | bytes 786440 | tf_op jit(solution)/shard_map/ppermute | solution.py:263
  79.2 7.2 %collective-permute-done.refs_1_ = bf16[128,1024]{1,0:T(8,128)(2,1)S(1)} collective-permute-done((bf16[128,1024]{1,0:T(8,128)(2,1)}, bf16[128,1024]{1,0:T(8,128)(2,1)S(1)}, u32[]{:S(2)}, u32[]{:S(2)}) %collective-permute-start) | collective-permute-done | bytes 262176 | tf_op jit(solution)/shard_map/ppermute | solution.py:259
  86.4 0.0 copy-start.2
  86.4 0.0 collective-permute-start.2
  86.4 0.0 copy-done.9
  86.5 0.1 broadcast_in_dim.14
  86.5 0.1 reshape.64
  86.6 0.0 collective-permute-done.1.refs_2_
  86.6 0.0 copy-start.3
  86.6 3.3 %collective-permute-start.3 = (bf16[128,1024]{1,0:T(8,128)(2,1)S(1)}, bf16[128,1024]{1,0:T(8,128)(2,1)S(1)}, u32[]{:S(2)}, u32[]{:S(2)}) collective-permute-start(bf16[128,1024]{1,0:T(8,128)(2,1)S(1)} %collective-permute-done.1.refs_2_), channel_id=1, source_target_pairs={{0,7},{1,0},{2,1},{3,2},{4,3},{5,4},{6,5},{7,6},{8,15},{9,8},{10,9... | collective-permute-start | bytes 786440 | tf_op jit(solution)/shard_map/ppermute | solution.py:263
  89.9 5.9 %collective-permute-done.2.refs_3_ = bf16[128,1024]{1,0:T(8,128)(2,1)S(1)} collective-permute-done((bf16[128,1024]{1,0:T(8,128)(2,1)S(1)}, bf16[128,1024]{1,0:T(8,128)(2,1)S(1)}, u32[]{:S(2)}, u32[]{:S(2)}) %collective-permute-start.2) | collective-permute-done | bytes 262176 | tf_op jit(solution)/shard_map/ppermute | solution.py:259
  95.8 0.0 copy-start.4
  95.8 0.0 collective-permute-start.4
  95.8 0.1 mul.43
  95.9 0.0 collective-permute-done.3.refs_4_
  95.9 0.0 copy-start.5
  95.9 3.3 %collective-permute-start.5 = (bf16[128,1024]{1,0:T(8,128)(2,1)S(1)}, bf16[128,1024]{1,0:T(8,128)(2,1)S(1)}, u32[]{:S(2)}, u32[]{:S(2)}) collective-permute-start(bf16[128,1024]{1,0:T(8,128)(2,1)S(1)} %collective-permute-done.3.refs_4_), channel_id=1, source_target_pairs={{0,7},{1,0},{2,1},{3,2},{4,3},{5,4},{6,5},{7,6},{8,15},{9,8},{10,9... | collective-permute-start | bytes 786440 | tf_op jit(solution)/shard_map/ppermute | solution.py:263
  99.2 5.1 %collective-permute-done.4.refs_5_ = bf16[128,1024]{1,0:T(8,128)(2,1)S(1)} collective-permute-done((bf16[128,1024]{1,0:T(8,128)(2,1)S(1)}, bf16[128,1024]{1,0:T(8,128)(2,1)S(1)}, u32[]{:S(2)}, u32[]{:S(2)}) %collective-permute-start.4) | collective-permute-done | bytes 262176 | tf_op jit(solution)/shard_map/ppermute | solution.py:259
  104.3 0.0 copy-start.6
  104.3 0.0 collective-permute-start.6
  104.3 3.1 %select_convert_fusion.basis_ref = bf16[512,256]{1,0:T(8,128)(2,1)} fusion(s32[512]{0:T(512)S(1)} %iota_add_fusion, s32[256]{0:T(256)S(1)} %multiply_add_fusion, pred[256]{0:T(512)(128)(4,1)S(1)} %broadcast_compare_fusion), kind=kLoop, calls=%fused_computation.8 | loop fusion | flops 2228224 | bytes 265472 | tf_op jit(solution)/shard_map/convert_element_type | solution.py:229
  107.5 0.0 collective-permute-done.5.refs_6_
  107.5 0.0 copy-start.7
  107.5 4.5 %collective-permute-done.6.refs_7_ = bf16[128,1024]{1,0:T(8,128)(2,1)S(1)} collective-permute-done((bf16[128,1024]{1,0:T(8,128)(2,1)S(1)}, bf16[128,1024]{1,0:T(8,128)(2,1)S(1)}, u32[]{:S(2)}, u32[]{:S(2)}) %collective-permute-start.6) | collective-permute-done | bytes 262176 | tf_op jit(solution)/shard_map/ppermute | solution.py:259
  112.0 0.0 copy-done.2
  112.0 0.0 copy-done.3
  112.0 0.0 copy-done.4
  112.0 0.0 copy-done.5
  112.0 0.0 copy-done.6
  112.0 0.0 copy-done.7
  112.0 0.0 copy-start.8
  112.0 0.7 copy-done.8
  112.7 5.3 %histories.1 = bf16[4,512,1024]{2,1,0:T(8,128)(2,1)} custom-call(bf16[512,256]{1,0:T(8,128)(2,1)} %select_convert_fusion.basis_ref, bf16[128,1024]{1,0:T(8,128)(2,1)} %node_spectra.1.refs_0_, bf16[128,1024]{1,0:T(8,128)(2,1)} %copy-done.2, bf16[128,1024]{1,0:T(8,128)(2,1)} %copy-done.3, bf16[128,1024]{1,0:T(8,128)(2,1)} %copy-done.4, ...), custom_call_target="tpu_custom_call" | custom-call | flops 1073741824 | bytes 6291456 | tf_op jit(solution)/shard_map/histories/pallas_call | solution.py:206
  (5 shorter events, 0.0 us)
Async XLA Ops:
  2.3 35.1 %all-to-all-start = ((bf16[256,4,256]{2,1,0:T(4,128)(2,1)}), bf16[256,4,256]{2,1,0:T(4,128)(2,1)S(1)}, u32[]{:S(2)}, u32[]{:S(2)}) async-start(bf16[256,4,256]{2,1,0:T(4,128)(2,1)} %bitcast.11), calls=%async_computation | async-start | bytes 1048576 | tf_op jit(solution)/shard_map/all_to_all | solution.py:241
  37.4 5.1 %copy-start.1 = (bf16[256,4,256]{2,1,0:T(4,128)(2,1)}, bf16[256,4,256]{2,1,0:T(4,128)(2,1)S(1)}, u32[]{:S(2)}) copy-start(bf16[256,4,256]{2,1,0:T(4,128)(2,1)S(1)} %all-to-all-done) | copy-start | bytes 1572868
  37.4 17.2 %all-to-all-start.2 = ((bf16[32,12,8,128]{3,2,1,0:T(8,128)(2,1)}), bf16[32,12,8,128]{3,2,1,0:T(8,128)(2,1)S(1)}, u32[]{:S(2)}, u32[]{:S(2)}) async-start(bf16[32,12,8,128]{3,2,1,0:T(8,128)(2,1)} %get-tuple-element.8), calls=%async_computation.2 | async-start | bytes 1572864 | tf_op jit(solution)/shard_map/all_to_all | solution.py:248
  42.5 43.9 %copy-start.9 = (s32[8]{0:T(128)S(1)}, s32[8]{0:T(128)}, u32[]{:S(2)}) copy-start(s32[8]{0:T(128)} %constant.63.clone) | copy-start | bytes 100
  54.6 18.5 %copy-start = (bf16[32,12,8,128]{3,2,1,0:T(8,128)(2,1)}, bf16[32,12,8,128]{3,2,1,0:T(8,128)(2,1)S(1)}, u32[]{:S(2)}) copy-start(bf16[32,12,8,128]{3,2,1,0:T(8,128)(2,1)S(1)} %all-to-all-done.2) | copy-start | bytes 2359300
  76.0 10.4 %collective-permute-start = (bf16[128,1024]{1,0:T(8,128)(2,1)}, bf16[128,1024]{1,0:T(8,128)(2,1)S(1)}, u32[]{:S(2)}, u32[]{:S(2)}) collective-permute-start(bf16[128,1024]{1,0:T(8,128)(2,1)} %node_spectra.1.refs_0_), channel_id=1, source_target_pairs={{0,1},{1,2},{2,3},{3,4},{4,5},{5,6},{6,7},{7,0},{8,9},{9,10},{10,1... | collective-permute-start | bytes 786440 | tf_op jit(solution)/shard_map/ppermute | solution.py:259
  77.0 9.6 %collective-permute-start.1 = (bf16[128,1024]{1,0:T(8,128)(2,1)}, bf16[128,1024]{1,0:T(8,128)(2,1)S(1)}, u32[]{:S(2)}, u32[]{:S(2)}) collective-permute-start(bf16[128,1024]{1,0:T(8,128)(2,1)} %node_spectra.1.refs_0_), channel_id=1, source_target_pairs={{0,7},{1,0},{2,1},{3,2},{4,3},{5,4},{6,5},{7,6},{8,15},{9,8},{10,9... | collective-permute-start | bytes 786440 | tf_op jit(solution)/shard_map/ppermute | solution.py:263
  86.4 25.5 %copy-start.2 = (bf16[128,1024]{1,0:T(8,128)(2,1)}, bf16[128,1024]{1,0:T(8,128)(2,1)S(1)}, u32[]{:S(2)}) copy-start(bf16[128,1024]{1,0:T(8,128)(2,1)S(1)} %collective-permute-done.refs_1_) | copy-start | bytes 786436
  86.4 9.4 %collective-permute-start.2 = (bf16[128,1024]{1,0:T(8,128)(2,1)S(1)}, bf16[128,1024]{1,0:T(8,128)(2,1)S(1)}, u32[]{:S(2)}, u32[]{:S(2)}) collective-permute-start(bf16[128,1024]{1,0:T(8,128)(2,1)S(1)} %collective-permute-done.refs_1_), channel_id=1, source_target_pairs={{0,1},{1,2},{2,3},{3,4},{4,5},{5,6},{6,7},{7,0},{8,9},{9,10},{10,1... | collective-permute-start | bytes 786440 | tf_op jit(solution)/shard_map/ppermute | solution.py:259
  86.6 25.3 %copy-start.3 = (bf16[128,1024]{1,0:T(8,128)(2,1)}, bf16[128,1024]{1,0:T(8,128)(2,1)S(1)}, u32[]{:S(2)}) copy-start(bf16[128,1024]{1,0:T(8,128)(2,1)S(1)} %collective-permute-done.1.refs_2_) | copy-start | bytes 786436
  86.6 9.3 %collective-permute-start.3 = (bf16[128,1024]{1,0:T(8,128)(2,1)S(1)}, bf16[128,1024]{1,0:T(8,128)(2,1)S(1)}, u32[]{:S(2)}, u32[]{:S(2)}) collective-permute-start(bf16[128,1024]{1,0:T(8,128)(2,1)S(1)} %collective-permute-done.1.refs_2_), channel_id=1, source_target_pairs={{0,7},{1,0},{2,1},{3,2},{4,3},{5,4},{6,5},{7,6},{8,15},{9,8},{10,9... | collective-permute-start | bytes 786440 | tf_op jit(solution)/shard_map/ppermute | solution.py:263
  95.8 16.2 %copy-start.4 = (bf16[128,1024]{1,0:T(8,128)(2,1)}, bf16[128,1024]{1,0:T(8,128)(2,1)S(1)}, u32[]{:S(2)}) copy-start(bf16[128,1024]{1,0:T(8,128)(2,1)S(1)} %collective-permute-done.2.refs_3_) | copy-start | bytes 786436
  95.8 8.5 %collective-permute-start.4 = (bf16[128,1024]{1,0:T(8,128)(2,1)S(1)}, bf16[128,1024]{1,0:T(8,128)(2,1)S(1)}, u32[]{:S(2)}, u32[]{:S(2)}) collective-permute-start(bf16[128,1024]{1,0:T(8,128)(2,1)S(1)} %collective-permute-done.2.refs_3_), channel_id=1, source_target_pairs={{0,1},{1,2},{2,3},{3,4},{4,5},{5,6},{6,7},{7,0},{8,9},{9,10},{10,1... | collective-permute-start | bytes 786440 | tf_op jit(solution)/shard_map/ppermute | solution.py:259
  95.9 16.1 %copy-start.5 = (bf16[128,1024]{1,0:T(8,128)(2,1)}, bf16[128,1024]{1,0:T(8,128)(2,1)S(1)}, u32[]{:S(2)}) copy-start(bf16[128,1024]{1,0:T(8,128)(2,1)S(1)} %collective-permute-done.3.refs_4_) | copy-start | bytes 786436
  95.9 11.6 %collective-permute-start.5 = (bf16[128,1024]{1,0:T(8,128)(2,1)S(1)}, bf16[128,1024]{1,0:T(8,128)(2,1)S(1)}, u32[]{:S(2)}, u32[]{:S(2)}) collective-permute-start(bf16[128,1024]{1,0:T(8,128)(2,1)S(1)} %collective-permute-done.3.refs_4_), channel_id=1, source_target_pairs={{0,7},{1,0},{2,1},{3,2},{4,3},{5,4},{6,5},{7,6},{8,15},{9,8},{10,9... | collective-permute-start | bytes 786440 | tf_op jit(solution)/shard_map/ppermute | solution.py:263
  104.3 7.7 %copy-start.6 = (bf16[128,1024]{1,0:T(8,128)(2,1)}, bf16[128,1024]{1,0:T(8,128)(2,1)S(1)}, u32[]{:S(2)}) copy-start(bf16[128,1024]{1,0:T(8,128)(2,1)S(1)} %collective-permute-done.4.refs_5_) | copy-start | bytes 786436
  104.3 7.6 %collective-permute-start.6 = (bf16[128,1024]{1,0:T(8,128)(2,1)S(1)}, bf16[128,1024]{1,0:T(8,128)(2,1)S(1)}, u32[]{:S(2)}, u32[]{:S(2)}) collective-permute-start(bf16[128,1024]{1,0:T(8,128)(2,1)S(1)} %collective-permute-done.4.refs_5_), channel_id=1, source_target_pairs={{0,1},{1,2},{2,3},{3,4},{4,5},{5,6},{6,7},{7,0},{8,9},{9,10},{10,1... | collective-permute-start | bytes 786440 | tf_op jit(solution)/shard_map/ppermute | solution.py:259
  107.5 4.5 %copy-start.7 = (bf16[128,1024]{1,0:T(8,128)(2,1)}, bf16[128,1024]{1,0:T(8,128)(2,1)S(1)}, u32[]{:S(2)}) copy-start(bf16[128,1024]{1,0:T(8,128)(2,1)S(1)} %collective-permute-done.5.refs_6_) | copy-start | bytes 786436
  112.0 0.7 copy-start.8

commit v2 on v1

--- a/solution.py
+++ b/solution.py
@@ -14,6 +14,7 @@
 TILE_DEV = 8
 BF = jnp.bfloat16
 F32 = jnp.float32
+VMEM_LIMIT = 20 << 20
 
 
 def scale_kernel(group_ref, pressure_ref, amp_ref, code_ref, out_ref):
@@ -65,7 +66,7 @@
         hot_ref[:, k * width : (k + 1) * width] = jnp.where(hot, 1.0, 0.0).astype(BF)
 
 
-def gather_slots(hot_ref, rank_ref, source_ref, out_ref, transposed):
+def gather_slots(hot_ref, rank_ref, source_ref, out_ref):
     blocks, width = rank_ref.shape
     owners, capacity, tiles, lanes = out_ref.shape
 
@@ -74,14 +75,9 @@
         for k in range(blocks):
             cols = slice(k * width, (k + 1) * width)
             live = jnp.where(rank_ref[k : k + 1, :] == s.astype(F32), 1.0, 0.0).astype(BF)
-            picked = hot_ref[:, cols] * live
-            if transposed:
-                total += lax.dot_general(
-                    picked, source_ref[:, cols], (((1,), (1,)), ((), ())),
-                    preferred_element_type=F32,
-                )
-            else:
-                total += jnp.dot(picked, source_ref[cols, :], preferred_element_type=F32)
+            total += jnp.dot(
+                hot_ref[:, cols] * live, source_ref[cols, :], preferred_element_type=F32
+            )
         out_ref[:, pl.ds(s, 1)] = total.astype(BF).reshape(owners, 1, tiles, lanes)
         return carry
 
@@ -104,7 +100,7 @@
         earlier = jnp.dot(hot, before, preferred_element_type=F32) + seen
         rank_ref[k : k + 1, :] = jnp.sum(hot32 * earlier, axis=0, keepdims=True)
         seen = seen + jnp.sum(hot32, axis=1, keepdims=True)
-    gather_slots(hot_ref, rank_ref, weight_ref, out_ref, False)
+    gather_slots(hot_ref, rank_ref, weight_ref, out_ref)
 
 
 def gather_weights(tile_ids, weights, owners, capacity):
@@ -119,6 +115,7 @@
         in_specs=[pl.BlockSpec(memory_space=pltpu.VMEM)] * 2,
         out_specs=(pl.BlockSpec(memory_space=pltpu.VMEM),) * 2,
         scratch_shapes=[pltpu.VMEM((owners * TILE_DEV, blocks * width), BF)],
+        compiler_params=pltpu.CompilerParams(vmem_limit_bytes=VMEM_LIMIT),
         cost_estimate=pl.CostEstimate(
             flops=2 * owners * capacity * TILE_DEV * blocks * width * lanes,
             bytes_accessed=2 << 20, transcendentals=0,
@@ -127,91 +124,128 @@
     )(tile_ids, weights)
 
 
-def row_kernel(tile_ref, rank_ref, spectra_ref, out_ref, hot_ref, rows_ref, packed_ref):
+def row_kernel(tile_ref, rank_ref, weight_ref, spectra_ref, out_ref, hot_ref, rows_ref, packed_ref):
     groups, blocks, headings, width = spectra_ref.shape
-    owners, _, tiles, _ = out_ref.shape
+    owners, capacity, tiles, _ = out_ref.shape
+    lanes = groups * headings
+    parts = width // 128
+    out_ref[:, :, :, lanes:] = weight_ref[...]
     fill_tilehot(tile_ref, hot_ref, owners * tiles)
     for k in range(blocks):
-        for part in range(width // 128):
-            cols = slice(part * 128, (part + 1) * 128)
-            slot = k * (width // 128) + part
+        for part in range(parts):
+            slot = k * parts + part
             for g in range(groups):
                 rows_ref[slot, pl.ds(g, headings, stride=groups), :] = (
-                    spectra_ref[g, k, :, cols].astype(F32)
+                    spectra_ref[g, k, :, part * 128 : (part + 1) * 128].astype(F32)
                 )
             packed_ref[:, slot * 128 : (slot + 1) * 128] = rows_ref[slot].astype(BF)
-    gather_slots(hot_ref, rank_ref, packed_ref, out_ref, True)
-
-
-def gather_rows(tile_ids, rank, spectra, owners, capacity):
+
+    def pair(step, carry):
+        total = jnp.zeros((owners * tiles, 2 * lanes), F32)
+        for k in range(blocks):
+            cols = slice(k * width, (k + 1) * width)
+            rank, rows = rank_ref[k : k + 1, :], packed_ref[:, cols]
+            live = [
+                jnp.where(rank == (2 * step + i).astype(F32), 1.0, 0.0).astype(BF)
+                for i in range(2)
+            ]
+            total += lax.dot_general(
+                hot_ref[:, cols], jnp.concatenate([rows * live[0], rows * live[1]], axis=0),
+                (((1,), (1,)), ((), ())), preferred_element_type=F32,
+            )
+        for i in range(2):
+            out_ref[:, pl.ds(2 * step + i, 1), :, :lanes] = (
+                total[:, i * lanes : (i + 1) * lanes].astype(BF).reshape(owners, 1, tiles, lanes)
+            )
+        return carry
+
+    lax.fori_loop(0, capacity // 2, pair, 0)
+
+
+def gather_rows(tile_ids, rank, weights, spectra):
     blocks, width = tile_ids.shape
     groups, _, headings, _ = spectra.shape
+    owners, capacity, tiles, nodes = weights.shape
     lanes = groups * headings
     return pl.pallas_call(
         row_kernel,
-        out_shape=jax.ShapeDtypeStruct((owners, capacity, TILE_DEV, lanes), BF),
-        in_specs=[pl.BlockSpec(memory_space=pltpu.VMEM)] * 3,
+        out_shape=jax.ShapeDtypeStruct((owners, capacity, tiles, lanes + nodes), BF),
+        in_specs=[pl.BlockSpec(memory_space=pltpu.VMEM)] * 4,
         out_specs=pl.BlockSpec(memory_space=pltpu.VMEM),
         scratch_shapes=[
-            pltpu.VMEM((owners * TILE_DEV, blocks * width), BF),
+            pltpu.VMEM((owners * tiles, blocks * width), BF),
             pltpu.VMEM((blocks * width // 128, lanes, 128), F32),
             pltpu.VMEM((lanes, blocks * width), BF),
         ],
+        compiler_params=pltpu.CompilerParams(vmem_limit_bytes=VMEM_LIMIT),
         cost_estimate=pl.CostEstimate(
-            flops=2 * owners * capacity * TILE_DEV * blocks * width * lanes,
-            bytes_accessed=2 << 20, transcendentals=0,
+            flops=2 * owners * capacity * tiles * blocks * width * lanes,
+            bytes_accessed=3 << 20, transcendentals=0,
         ),
         name="row_slots",
-    )(tile_ids, rank, spectra)
-
-
-def node_kernel(rows_ref, weight_ref, out_ref, rows32_ref, weight32_ref):
-    count, lanes = rows_ref.shape
-    rows32_ref[...] = rows_ref[...].astype(F32)
-    weight32_ref[...] = weight_ref[...].astype(F32)
+    )(tile_ids, rank, weights, spectra)
+
+
+def node_kernel(slots_ref, out_ref, wide_ref):
+    count, width = slots_ref.shape
+    lanes = out_ref.shape[0]
+    nodes = width - lanes
+    for half in range(2):
+        wide_ref[half] = slots_ref[:, half * lanes : (half + 1) * lanes].astype(F32)
     for tile in range(TILE_DEV):
         own = pl.ds(tile, count // TILE_DEV, stride=TILE_DEV)
         part = lax.dot_general(
-            rows32_ref[own, :].astype(BF), weight32_ref[own, :].astype(BF),
+            wide_ref[0, own, :].astype(BF), wide_ref[1, own, :].astype(BF),
             (((0,), (0,)), ((), ())), preferred_element_type=F32,
         )
-        out_ref[:, tile * 128 : (tile + 1) * 128] = part.astype(BF)
-
-
-def node_spectra(rows, weights):
-    count, lanes = rows.shape
+        out_ref[:, tile * nodes : (tile + 1) * nodes] = part.astype(BF)
+
+
+def node_spectra(slots):
+    count, width = slots.shape
+    lanes = width // 2
     return pl.pallas_call(
         node_kernel,
-        out_shape=jax.ShapeDtypeStruct((lanes, TILE_DEV * 128), BF),
-        in_specs=[pl.BlockSpec(memory_space=pltpu.VMEM)] * 2,
+        out_shape=jax.ShapeDtypeStruct((lanes, TILE_DEV * lanes), BF),
+        in_specs=[pl.BlockSpec(memory_space=pltpu.VMEM)],
         out_specs=pl.BlockSpec(memory_space=pltpu.VMEM),
-        scratch_shapes=[pltpu.VMEM((count, lanes), F32), pltpu.VMEM((count, 128), F32)],
+        scratch_shapes=[pltpu.VMEM((2, count, lanes), F32)],
+        compiler_params=pltpu.CompilerParams(vmem_limit_bytes=VMEM_LIMIT),
         cost_estimate=pl.CostEstimate(
-            flops=2 * count * lanes * 128, bytes_accessed=2 << 20, transcendentals=0
+            flops=2 * count * lanes * lanes, bytes_accessed=2 << 20, transcendentals=0
         ),
         name="node_spectra",
-    )(rows, weights)
+    )(slots)
 
 
 def history_kernel(basis_ref, *refs):
     out_ref = refs[-1]
-    spectra = jnp.concatenate([r[...] for r in refs[:-1]], axis=0)
+    heading = pl.program_id(0)
+    group = basis_ref.shape[1] // (len(refs) - 2)
+    own = pl.ds(pl.multiple_of(heading * group, group), group)
+    chunks = [r[own, :] for r in refs[:-3]]
+    low, high = refs[-3], refs[-2]
+    half = low.shape[0] // group
+    inner = pl.ds(pl.multiple_of(lax.rem(heading, half) * group, group), group)
+    chunks.append(jnp.where(heading < half, low[inner, :], high[inner, :]))
+    spectra = jnp.concatenate(chunks, axis=0)
     out_ref[0] = jnp.dot(basis_ref[...], spectra, preferred_element_type=F32).astype(BF)
 
 
 def histories(basis, chunks, headings):
     steps = basis.shape[0]
     lanes, nodes = chunks[0].shape
-    group = lanes // headings
+    cut = 2
     return pl.pallas_call(
         history_kernel,
-        grid=(headings,),
+        grid=(headings, cut),
         out_shape=jax.ShapeDtypeStruct((headings, steps, nodes), BF),
-        in_specs=[pl.BlockSpec(basis.shape, lambda h: (0, 0))]
-        + [pl.BlockSpec((group, nodes), lambda h: (h, 0))] * len(chunks),
-        out_specs=pl.BlockSpec((1, steps, nodes), lambda h: (h, 0, 0)),
+        in_specs=[pl.BlockSpec((steps // cut, basis.shape[1]), lambda h, i: (i, 0))]
+        + [pl.BlockSpec(memory_space=pltpu.VMEM)] * len(chunks),
+        out_specs=pl.BlockSpec((1, steps // cut, nodes), lambda h, i: (h, i, 0)),
+        compiler_params=pltpu.CompilerParams(vmem_limit_bytes=VMEM_LIMIT),
         cost_estimate=pl.CostEstimate(
-            flops=2 * steps * len(chunks) * lanes * nodes,
+            flops=2 * steps * basis.shape[1] * headings * nodes,
             bytes_accessed=6 << 20, transcendentals=0,
         ),
         name="histories",
@@ -244,27 +278,23 @@
 
     tile_ids = panel_tile.reshape(windows, width)
     weights = patch_weight.reshape(windows * width, 128)
-    sent_weight, rank = gather_weights(tile_ids, weights, owners, capacity)
-    got_weight = lax.all_to_all(sent_weight, "freq", 0, 0, tiled=True)
-
-    sent_rows = gather_rows(tile_ids, rank, spectra, owners, capacity)
-    got_rows = lax.all_to_all(sent_rows, "freq", 0, 0, tiled=True)
-    own = node_spectra(got_rows.reshape(-1, owners * headings), got_weight.reshape(-1, 128))
-
-    ahead = [(k, (k + 1) % windows) for k in range(windows)]
-    back = [(k, (k - 1) % windows) for k in range(windows)]
-    chunks, offsets = [own], [0]
-    right = left = own
-    for step in range(1, windows // 2 + 1):
-        right_next = lax.ppermute(right, "node", ahead)
-        chunks.append(right_next)
-        offsets.append(-step)
-        if step < windows - windows // 2:
-            left = lax.ppermute(left, "node", back)
-            chunks.append(left)
-            offsets.append(step)
-        right = right_next
-    sources = (window + jnp.asarray(offsets, jnp.int32)) % windows
+    slot_weight, rank = gather_weights(tile_ids, weights, owners, capacity)
+    sent = gather_rows(tile_ids, rank, slot_weight, spectra)
+    got = lax.all_to_all(sent, "freq", 0, 0, tiled=True)
+    own = node_spectra(got.reshape(-1, got.shape[-1]))
+
+    def shift(chunk, distance):
+        pairs = [(k, (k + distance) % windows) for k in range(windows)]
+        return lax.ppermute(chunk, "node", pairs)
+
+    half = own.shape[0] // 2
+    plus2, minus2 = shift(own, 2), shift(own, -2)
+    plus1, minus1 = shift(own, 1), shift(own, -1)
+    plus3, minus3 = shift(plus2, 1), shift(minus2, -1)
+    low4, high4 = shift(plus3[:half], 1), shift(minus3[half:], -1)
+    chunks = [own, plus1, minus1, plus2, minus2, plus3, minus3, low4, high4]
+    offsets = jnp.asarray([0, -1, 1, -2, 2, -3, 3, 4], jnp.int32)
+    sources = (window + offsets) % windows
     basis = window_basis(sources, window, TSTEPS // windows, owners, fl_count)
     return histories(basis, chunks, headings)
 

time: 119 us -> 109 us (0.916); the launches traced: 118 us -> 107 us
  blocking collectives: 18.5 us -> 0 us
  waiting for transfers between devices: 37.7 us -> 55 us
  Pallas kernels: 26.7 us -> 19 us
  local copies, waits for them, and re-layouts: 2.26 us -> 0.26 us
    all_to_all x1 -> x0, blocking collectives: 18.5 us -> none  [shards(): got_rows = lax.all_to_all(sent_rows, 'freq', 0, 0, tiled=True)]
    all_to_all x1, waiting for transfers between devices: 3.64 us -> 20.2 us  [shards(): got = lax.all_to_all(sent, 'freq', 0, 0, tiled=True)]
    all_to_all x1, waiting for transfers between devices: 11.4 us -> 14.6 us  [shards(): lax.all_to_all(scaled.reshape(owners * windows, headings, width), ('freq'...]
    pallas_call x1, Pallas kernels: 8.44 us -> 5.38 us  [gather_rows(): pl.pallas_call(row_kernel, out_shape=jax.ShapeDtypeStruct((owners, capaci...]
    ppermute x7 -> x8, waiting for transfers between devices: 22.6 us -> 20.2 us  [shift(): return lax.ppermute(chunk, 'node', pairs)]
    pallas_call x1, Pallas kernels: 2.91 us -> 0.85 us  [node_spectra(): pl.pallas_call(node_kernel, out_shape=jax.ShapeDtypeStruct((lanes, TILE_D...]
    unnamed x21 -> x7, local copies, waits for them, and re-layouts: 2.03 us -> 0.01 us
    pallas_call x1, Pallas kernels: 7.71 us -> 5.78 us  [gather_weights(): pl.pallas_call(weight_kernel, out_shape=(jax.ShapeDtypeStruct((owners, ca...]
  transfers between devices with their start and end apart: 9 -> 10, of which waited for: 6 -> 8; matrix products, arithmetic and copies ran while one was open for 4% -> 3% of each run, Pallas kernels for 14% -> 5%
where the time goes in v2:
time: 109 us; the launch traced here: 107 us
  waiting for transfers between devices  55 us (50%)
  starting transfers between devices  29.6 us (27%)
  Pallas kernels  19 us (17%)
  other arithmetic  2.55 us (2%)
    ppermute x8, waiting for transfers between devices, shift(): return lax.ppermute(chunk, 'node', pairs)  20.2 us
    all_to_all x1, waiting for transfers between devices, shards(): got = lax.all_to_all(sent, 'freq', 0, 0, tiled=True)  20.2 us
    all_to_all x1, starting transfers between devices, shards(): lax.all_to_all(scaled.reshape(owners * windows, headings, width), ('freq'...  14.7 us
    all_to_all x1, waiting for transfers between devices, shards(): lax.all_to_all(scaled.reshape(owners * windows, headings, width), ('freq'...  14.6 us
    ppermute x8, starting transfers between devices, shift(): return lax.ppermute(chunk, 'node', pairs)  9.69 us
    pallas_call x1, Pallas kernels, gather_weights(): pl.pallas_call(weight_kernel, out_shape=(jax.ShapeDtypeStruct((owners, ca...  5.78 us
    pallas_call x1, Pallas kernels, gather_rows(): pl.pallas_call(row_kernel, out_shape=jax.ShapeDtypeStruct((owners, capaci...  5.38 us
    all_to_all x1, starting transfers between devices, shards(): got = lax.all_to_all(sent, 'freq', 0, 0, tiled=True)  5.24 us
  transfers between devices with their start and end apart: 10, of which 8 were waited for; matrix products, arithmetic and copies ran while one was open for 3% of the time, Pallas kernels for 5%

profile of v2, /device:TPU:2, one launch (start us, length us, event | category | flops | bytes accessed | tf_op | source)
XLA Modules:
  0.0 106.6 jit_solution(6412338807594628290)
XLA Ops:
  0.0 0.0 copy-start.1
  0.0 0.0 copy-start
  0.0 2.3 %scale.1 = bf16[32,8,4,256]{3,2,1,0:T(4,128)(2,1)} custom-call(s32[1]{0:T(128)} %bitcast.1.group_ref, bf16[2,4,4,8192]{3,2,1,0:T(4,128)(2,1)} %pressure_ref.1, f32[4,128]{1,0:T(4,128)} %amp_ref.1, s32[4,128]{1,0:T(4,128)} %code_ref.1), custom_call_target="tpu_custom_call" | custom-call | flops 2000000 | bytes 1048576 | tf_op jit(solution)/shard_map/scale/pallas_call | solution.py:46
  2.3 14.7 %all-to-all-start = ((bf16[256,4,256]{2,1,0:T(4,128)(2,1)}), bf16[256,4,256]{2,1,0:T(4,128)(2,1)S(1)}, u32[]{:S(2)}, u32[]{:S(2)}) async-start(bf16[256,4,256]{2,1,0:T(4,128)(2,1)} %bitcast.13), calls=%async_computation | async-start | bytes 1048576 | tf_op jit(solution)/shard_map/all_to_all | solution.py:275
  17.0 0.0 copy-done.1
  17.0 0.0 copy-done
  17.0 5.8 %weight_slots.1 = (bf16[32,12,8,128]{3,2,1,0:T(8,128)(2,1)S(1)}, f32[8,256]{1,0:T(8,128)S(1)}) custom-call(s32[8,256]{1,0:T(8,128)S(1)} %bitcast.10, bf16[2048,128]{1,0:T(8,128)(2,1)S(1)} %bitcast.12), custom_call_target="tpu_custom_call" | custom-call | flops 1610612736 | bytes 2097152 | tf_op jit(solution)/shard_map/weight_slots/pallas_call | solution.py:109
  22.8 14.6 %all-to-all-done = bf16[256,4,256]{2,1,0:T(4,128)(2,1)S(1)} async-done(((bf16[256,4,256]{2,1,0:T(4,128)(2,1)}), bf16[256,4,256]{2,1,0:T(4,128)(2,1)S(1)}, u32[]{:S(2)}, u32[]{:S(2)}) %all-to-all-start) | async-done | bytes 524320 | tf_op jit(solution)/shard_map/all_to_all | solution.py:275
  37.5 5.4 %row_slots.1 = bf16[32,12,8,256]{3,2,1,0:T(8,128)(2,1)} custom-call(s32[8,256]{1,0:T(8,128)S(1)} %bitcast.11, f32[8,256]{1,0:T(8,128)S(1)} %get-tuple-element.7.rank_ref, bf16[32,12,8,128]{3,2,1,0:T(8,128)(2,1)S(1)} %get-tuple-element.8.weight_ref, bf16[32,8,4,256]{3,2,1,0:T(4,128)(2,1)S(1)} %bitcast.9), custom_call_target="tpu_custom_call" | custom-call | flops 1610612736 | bytes 3145728 | tf_op jit(solution)/shard_map/row_slots/pallas_call | solution.py:170
  42.8 0.0 copy-start.2
  42.8 5.2 %all-to-all-start.1 = ((bf16[32,12,8,256]{3,2,1,0:T(8,128)(2,1)}), bf16[32,12,8,256]{3,2,1,0:T(8,128)(2,1)S(1)}, u32[]{:S(2)}, u32[]{:S(2)}) async-start(bf16[32,12,8,256]{3,2,1,0:T(8,128)(2,1)} %row_slots.1), calls=%async_computation.1 | async-start | bytes 3145728 | tf_op jit(solution)/shard_map/all_to_all | solution.py:283
  48.1 0.0 copy-done.2
  48.1 20.2 %all-to-all-done.1 = bf16[32,12,8,256]{3,2,1,0:T(8,128)(2,1)S(1)} async-done(((bf16[32,12,8,256]{3,2,1,0:T(8,128)(2,1)}), bf16[32,12,8,256]{3,2,1,0:T(8,128)(2,1)S(1)}, u32[]{:S(2)}, u32[]{:S(2)}) %all-to-all-start.1) | async-done | bytes 1572896 | tf_op jit(solution)/shard_map/all_to_all | solution.py:283
  68.3 0.8 node_spectra.1.refs_0_
  69.1 0.5 collective-permute-start.3
  69.7 2.5 %collective-permute-start.2 = (bf16[128,1024]{1,0:T(8,128)(2,1)S(1)}, bf16[128,1024]{1,0:T(8,128)(2,1)S(1)}, u32[]{:S(2)}, u32[]{:S(2)}) collective-permute-start(bf16[128,1024]{1,0:T(8,128)(2,1)S(1)} %node_spectra.1.refs_0_), channel_id=1, source_target_pairs={{0,2},{1,3},{2,4},{3,5},{4,6},{5,7},{6,0},{7,1},{8,10},{9,11},{10,... | collective-permute-start | bytes 786440 | tf_op jit(solution)/shard_map/ppermute | solution.py:288
  72.1 0.1 broadcast_in_dim.14
  72.2 0.1 reshape.61
  72.3 0.1 mul.43
  72.4 12.0 %collective-permute-done.3.refs_4_ = bf16[128,1024]{1,0:T(8,128)(2,1)S(1)} collective-permute-done((bf16[128,1024]{1,0:T(8,128)(2,1)S(1)}, bf16[128,1024]{1,0:T(8,128)(2,1)S(1)}, u32[]{:S(2)}, u32[]{:S(2)}) %collective-permute-start.3) | collective-permute-done | bytes 262176 | tf_op jit(solution)/shard_map/ppermute | solution.py:288
  84.4 0.0 collective-permute-start.5
  84.4 0.0 collective-permute-done.2.refs_3_
  84.4 2.3 %collective-permute-start.4 = (bf16[128,1024]{1,0:T(8,128)(2,1)S(1)}, bf16[128,1024]{1,0:T(8,128)(2,1)S(1)}, u32[]{:S(2)}, u32[]{:S(2)}) collective-permute-start(bf16[128,1024]{1,0:T(8,128)(2,1)S(1)} %collective-permute-done.2.refs_3_), channel_id=1, source_target_pairs={{0,1},{1,2},{2,3},{3,4},{4,5},{5,6},{6,7},{7,0},{8,9},{9,10},{10,1... | collective-permute-start | bytes 786440 | tf_op jit(solution)/shard_map/ppermute | solution.py:288
  86.7 0.9 collective-permute-start.1
  87.6 1.1 %collective-permute-start = (bf16[128,1024]{1,0:T(8,128)(2,1)S(1)}, bf16[128,1024]{1,0:T(8,128)(2,1)S(1)}, u32[]{:S(2)}, u32[]{:S(2)}) collective-permute-start(bf16[128,1024]{1,0:T(8,128)(2,1)S(1)} %node_spectra.1.refs_0_), channel_id=1, source_target_pairs={{0,1},{1,2},{2,3},{3,4},{4,5},{5,6},{6,7},{7,0},{8,9},{9,10},{10,1... | collective-permute-start | bytes 786440 | tf_op jit(solution)/shard_map/ppermute | solution.py:288
  88.7 4.8 %collective-permute-done.5.refs_6_ = bf16[128,1024]{1,0:T(8,128)(2,1)S(1)} collective-permute-done((bf16[128,1024]{1,0:T(8,128)(2,1)S(1)}, bf16[128,1024]{1,0:T(8,128)(2,1)S(1)}, u32[]{:S(2)}, u32[]{:S(2)}) %collective-permute-start.5) | collective-permute-done | bytes 262176 | tf_op jit(solution)/shard_map/ppermute | solution.py:288
  93.6 1.3 %collective-permute-start.7 = (bf16[64,1024]{1,0:T(8,128)(2,1)S(1)}, bf16[64,1024]{1,0:T(8,128)(2,1)S(1)}, u32[]{:S(2)}, u32[]{:S(2)}) collective-permute-start(bf16[64,1024]{1,0:T(8,128)(2,1)S(1)} %slice.9), channel_id=1, source_target_pairs={{0,7},{1,0},{2,1},{3,2},{4,3},{5,4},{6,5},{7,6},{8,15},{9,8},{10,9... | collective-permute-start | bytes 393224 | tf_op jit(solution)/shard_map/ppermute | solution.py:288
  94.9 0.0 collective-permute-done.4.refs_5_
  94.9 1.1 %collective-permute-start.6 = (bf16[64,1024]{1,0:T(8,128)(2,1)S(1)}, bf16[64,1024]{1,0:T(8,128)(2,1)S(1)}, u32[]{:S(2)}, u32[]{:S(2)}) collective-permute-start(bf16[64,1024]{1,0:T(8,128)(2,1)S(1)} %slice.8), channel_id=1, source_target_pairs={{0,1},{1,2},{2,3},{3,4},{4,5},{5,6},{6,7},{7,0},{8,9},{9,10},{10,1... | collective-permute-start | bytes 393224 | tf_op jit(solution)/shard_map/ppermute | solution.py:288
  96.0 2.5 %select_convert_fusion.basis_ref = bf16[512,256]{1,0:T(8,128)(2,1)S(1)} fusion(s32[512]{0:T(512)S(1)} %iota_add_fusion, s32[256]{0:T(256)S(1)} %multiply_add_fusion, pred[256]{0:T(512)(128)(4,1)S(1)} %broadcast_compare_fusion), kind=kLoop, calls=%fused_computation.8 | loop fusion | flops 2228224 | bytes 265472 | tf_op jit(solution)/shard_map/convert_element_type | solution.py:263
  98.5 0.7 collective-permute-done.1.refs_2_
  99.2 1.2 %collective-permute-done.refs_1_ = bf16[128,1024]{1,0:T(8,128)(2,1)S(1)} collective-permute-done((bf16[128,1024]{1,0:T(8,128)(2,1)S(1)}, bf16[128,1024]{1,0:T(8,128)(2,1)S(1)}, u32[]{:S(2)}, u32[]{:S(2)}) %collective-permute-start) | collective-permute-done | bytes 262176 | tf_op jit(solution)/shard_map/ppermute | solution.py:288
  100.4 0.2 collective-permute-done.7.refs_8_
  100.6 1.2 %collective-permute-done.6.refs_7_ = bf16[64,1024]{1,0:T(8,128)(2,1)S(1)} collective-permute-done((bf16[64,1024]{1,0:T(8,128)(2,1)S(1)}, bf16[64,1024]{1,0:T(8,128)(2,1)S(1)}, u32[]{:S(2)}, u32[]{:S(2)}) %collective-permute-start.6) | collective-permute-done | bytes 131104 | tf_op jit(solution)/shard_map/ppermute | solution.py:288
  101.9 4.7 %histories.1 = bf16[4,512,1024]{2,1,0:T(8,128)(2,1)} custom-call(bf16[512,256]{1,0:T(8,128)(2,1)S(1)} %select_convert_fusion.basis_ref, bf16[128,1024]{1,0:T(8,128)(2,1)S(1)} %node_spectra.1.refs_0_, bf16[128,1024]{1,0:T(8,128)(2,1)S(1)} %collective-permute-done.refs_1_, bf16[128,1024]{1,0:T(8,128)(2,1)S(1)} %collective-permute-done.1.refs_2_, ...), custom_call_target="tpu_custom_call" | custom-call | flops 1073741824 | bytes 6291456 | tf_op jit(solution)/shard_map/histories/pallas_call | solution.py:239
  (8 shorter events, 0.1 us)
Async XLA Ops:
  0.0 17.0 %copy-start.1 = (s32[1,8,256,1]{2,3,1,0:T(1,128)S(1)}, s32[1,8,256,1]{2,3,1,0:T(1,128)}, u32[]{:S(2)}) copy-start(s32[1,8,256,1]{2,3,1,0:T(1,128)} %param.9) | copy-start | bytes 24580
  0.0 17.0 %copy-start = (bf16[1,8,256,128]{3,2,1,0:T(8,128)(2,1)S(1)}, bf16[1,8,256,128]{3,2,1,0:T(8,128)(2,1)}, u32[]{:S(2)}) copy-start(bf16[1,8,256,128]{3,2,1,0:T(8,128)(2,1)} %param.10) | copy-start | bytes 1572868
  2.3 35.1 %all-to-all-start = ((bf16[256,4,256]{2,1,0:T(4,128)(2,1)}), bf16[256,4,256]{2,1,0:T(4,128)(2,1)S(1)}, u32[]{:S(2)}, u32[]{:S(2)}) async-start(bf16[256,4,256]{2,1,0:T(4,128)(2,1)} %bitcast.13), calls=%async_computation | async-start | bytes 1048576 | tf_op jit(solution)/shard_map/all_to_all | solution.py:275
  42.8 5.3 %copy-start.2 = (s32[8]{0:T(128)S(1)}, s32[8]{0:T(128)}, u32[]{:S(2)}) copy-start(s32[8]{0:T(128)} %constant.63.clone) | copy-start | bytes 100
  42.8 25.4 %all-to-all-start.1 = ((bf16[32,12,8,256]{3,2,1,0:T(8,128)(2,1)}), bf16[32,12,8,256]{3,2,1,0:T(8,128)(2,1)S(1)}, u32[]{:S(2)}, u32[]{:S(2)}) async-start(bf16[32,12,8,256]{3,2,1,0:T(8,128)(2,1)} %row_slots.1), calls=%async_computation.1 | async-start | bytes 3145728 | tf_op jit(solution)/shard_map/all_to_all | solution.py:283
  69.1 15.3 %collective-permute-start.3 = (bf16[128,1024]{1,0:T(8,128)(2,1)S(1)}, bf16[128,1024]{1,0:T(8,128)(2,1)S(1)}, u32[]{:S(2)}, u32[]{:S(2)}) collective-permute-start(bf16[128,1024]{1,0:T(8,128)(2,1)S(1)} %node_spectra.1.refs_0_), channel_id=1, source_target_pairs={{0,6},{1,7},{2,0},{3,1},{4,2},{5,3},{6,4},{7,5},{8,14},{9,15},{10,... | collective-permute-start | bytes 786440 | tf_op jit(solution)/shard_map/ppermute | solution.py:288
  69.7 14.7 %collective-permute-start.2 = (bf16[128,1024]{1,0:T(8,128)(2,1)S(1)}, bf16[128,1024]{1,0:T(8,128)(2,1)S(1)}, u32[]{:S(2)}, u32[]{:S(2)}) collective-permute-start(bf16[128,1024]{1,0:T(8,128)(2,1)S(1)} %node_spectra.1.refs_0_), channel_id=1, source_target_pairs={{0,2},{1,3},{2,4},{3,5},{4,6},{5,7},{6,0},{7,1},{8,10},{9,11},{10,... | collective-permute-start | bytes 786440 | tf_op jit(solution)/shard_map/ppermute | solution.py:288
  84.4 9.2 %collective-permute-start.5 = (bf16[128,1024]{1,0:T(8,128)(2,1)S(1)}, bf16[128,1024]{1,0:T(8,128)(2,1)S(1)}, u32[]{:S(2)}, u32[]{:S(2)}) collective-permute-start(bf16[128,1024]{1,0:T(8,128)(2,1)S(1)} %collective-permute-done.3.refs_4_), channel_id=1, source_target_pairs={{0,7},{1,0},{2,1},{3,2},{4,3},{5,4},{6,5},{7,6},{8,15},{9,8},{10,9... | collective-permute-start | bytes 786440 | tf_op jit(solution)/shard_map/ppermute | solution.py:288
  84.4 10.5 %collective-permute-start.4 = (bf16[128,1024]{1,0:T(8,128)(2,1)S(1)}, bf16[128,1024]{1,0:T(8,128)(2,1)S(1)}, u32[]{:S(2)}, u32[]{:S(2)}) collective-permute-start(bf16[128,1024]{1,0:T(8,128)(2,1)S(1)} %collective-permute-done.2.refs_3_), channel_id=1, source_target_pairs={{0,1},{1,2},{2,3},{3,4},{4,5},{5,6},{6,7},{7,0},{8,9},{9,10},{10,1... | collective-permute-start | bytes 786440 | tf_op jit(solution)/shard_map/ppermute | solution.py:288
  86.7 12.5 %collective-permute-start.1 = (bf16[128,1024]{1,0:T(8,128)(2,1)S(1)}, bf16[128,1024]{1,0:T(8,128)(2,1)S(1)}, u32[]{:S(2)}, u32[]{:S(2)}) collective-permute-start(bf16[128,1024]{1,0:T(8,128)(2,1)S(1)} %node_spectra.1.refs_0_), channel_id=1, source_target_pairs={{0,7},{1,0},{2,1},{3,2},{4,3},{5,4},{6,5},{7,6},{8,15},{9,8},{10,9... | collective-permute-start | bytes 786440 | tf_op jit(solution)/shard_map/ppermute | solution.py:288
  87.6 12.8 %collective-permute-start = (bf16[128,1024]{1,0:T(8,128)(2,1)S(1)}, bf16[128,1024]{1,0:T(8,128)(2,1)S(1)}, u32[]{:S(2)}, u32[]{:S(2)}) collective-permute-start(bf16[128,1024]{1,0:T(8,128)(2,1)S(1)} %node_spectra.1.refs_0_), channel_id=1, source_target_pairs={{0,1},{1,2},{2,3},{3,4},{4,5},{5,6},{6,7},{7,0},{8,9},{9,10},{10,1... | collective-permute-start | bytes 786440 | tf_op jit(solution)/shard_map/ppermute | solution.py:288
  93.6 7.1 %collective-permute-start.7 = (bf16[64,1024]{1,0:T(8,128)(2,1)S(1)}, bf16[64,1024]{1,0:T(8,128)(2,1)S(1)}, u32[]{:S(2)}, u32[]{:S(2)}) collective-permute-start(bf16[64,1024]{1,0:T(8,128)(2,1)S(1)} %slice.9), channel_id=1, source_target_pairs={{0,7},{1,0},{2,1},{3,2},{4,3},{5,4},{6,5},{7,6},{8,15},{9,8},{10,9... | collective-permute-start | bytes 393224 | tf_op jit(solution)/shard_map/ppermute | solution.py:288
  94.9 7.0 %collective-permute-start.6 = (bf16[64,1024]{1,0:T(8,128)(2,1)S(1)}, bf16[64,1024]{1,0:T(8,128)(2,1)S(1)}, u32[]{:S(2)}, u32[]{:S(2)}) collective-permute-start(bf16[64,1024]{1,0:T(8,128)(2,1)S(1)} %slice.8), channel_id=1, source_target_pairs={{0,1},{1,2},{2,3},{3,4},{4,5},{5,6},{6,7},{7,0},{8,9},{9,10},{10,1... | collective-permute-start | bytes 393224 | tf_op jit(solution)/shard_map/ppermute | solution.py:288

commit v3 on v2

--- a/solution.py
+++ b/solution.py
@@ -111,10 +111,10 @@
         out_shape=(
             jax.ShapeDtypeStruct((owners, capacity, TILE_DEV, lanes), BF),
             jax.ShapeDtypeStruct((blocks, width), F32),
+            jax.ShapeDtypeStruct((owners * TILE_DEV, blocks * width), BF),
         ),
         in_specs=[pl.BlockSpec(memory_space=pltpu.VMEM)] * 2,
-        out_specs=(pl.BlockSpec(memory_space=pltpu.VMEM),) * 2,
-        scratch_shapes=[pltpu.VMEM((owners * TILE_DEV, blocks * width), BF)],
+        out_specs=(pl.BlockSpec(memory_space=pltpu.VMEM),) * 3,
         compiler_params=pltpu.CompilerParams(vmem_limit_bytes=VMEM_LIMIT),
         cost_estimate=pl.CostEstimate(
             flops=2 * owners * capacity * TILE_DEV * blocks * width * lanes,
@@ -124,13 +124,12 @@
     )(tile_ids, weights)
 
 
-def row_kernel(tile_ref, rank_ref, weight_ref, spectra_ref, out_ref, hot_ref, rows_ref, packed_ref):
+def row_kernel(hot_ref, rank_ref, weight_ref, spectra_ref, out_ref, rows_ref, packed_ref, masked_ref):
     groups, blocks, headings, width = spectra_ref.shape
     owners, capacity, tiles, _ = out_ref.shape
     lanes = groups * headings
     parts = width // 128
     out_ref[:, :, :, lanes:] = weight_ref[...]
-    fill_tilehot(tile_ref, hot_ref, owners * tiles)
     for k in range(blocks):
         for part in range(parts):
             slot = k * parts + part
@@ -141,18 +140,15 @@
             packed_ref[:, slot * 128 : (slot + 1) * 128] = rows_ref[slot].astype(BF)
 
     def pair(step, carry):
-        total = jnp.zeros((owners * tiles, 2 * lanes), F32)
         for k in range(blocks):
             cols = slice(k * width, (k + 1) * width)
             rank, rows = rank_ref[k : k + 1, :], packed_ref[:, cols]
-            live = [
-                jnp.where(rank == (2 * step + i).astype(F32), 1.0, 0.0).astype(BF)
-                for i in range(2)
-            ]
-            total += lax.dot_general(
-                hot_ref[:, cols], jnp.concatenate([rows * live[0], rows * live[1]], axis=0),
-                (((1,), (1,)), ((), ())), preferred_element_type=F32,
-            )
+            for i in range(2):
+                live = jnp.where(rank == (2 * step + i).astype(F32), 1.0, 0.0).astype(BF)
+                masked_ref[i * lanes : (i + 1) * lanes, cols] = rows * live
+        total = lax.dot_general(
+            hot_ref[...], masked_ref[...], (((1,), (1,)), ((), ())), preferred_element_type=F32
+        )
         for i in range(2):
             out_ref[:, pl.ds(2 * step + i, 1), :, :lanes] = (
                 total[:, i * lanes : (i + 1) * lanes].astype(BF).reshape(owners, 1, tiles, lanes)
@@ -162,8 +158,8 @@
     lax.fori_loop(0, capacity // 2, pair, 0)
 
 
-def gather_rows(tile_ids, rank, weights, spectra):
-    blocks, width = tile_ids.shape
+def gather_rows(hot, rank, weights, spectra):
+    blocks, width = rank.shape
     groups, _, headings, _ = spectra.shape
     owners, capacity, tiles, nodes = weights.shape
     lanes = groups * headings
@@ -173,9 +169,9 @@
         in_specs=[pl.BlockSpec(memory_space=pltpu.VMEM)] * 4,
         out_specs=pl.BlockSpec(memory_space=pltpu.VMEM),
         scratch_shapes=[
-            pltpu.VMEM((owners * tiles, blocks * width), BF),
             pltpu.VMEM((blocks * width // 128, lanes, 128), F32),
             pltpu.VMEM((lanes, blocks * width), BF),
+            pltpu.VMEM((2 * lanes, blocks * width), BF),
         ],
         compiler_params=pltpu.CompilerParams(vmem_limit_bytes=VMEM_LIMIT),
         cost_estimate=pl.CostEstimate(
@@ -183,7 +179,7 @@
             bytes_accessed=3 << 20, transcendentals=0,
         ),
         name="row_slots",
-    )(tile_ids, rank, weights, spectra)
+    )(hot, rank, weights, spectra)
 
 
 def node_kernel(slots_ref, out_ref, wide_ref):
@@ -223,11 +219,13 @@
     heading = pl.program_id(0)
     group = basis_ref.shape[1] // (len(refs) - 2)
     own = pl.ds(pl.multiple_of(heading * group, group), group)
-    chunks = [r[own, :] for r in refs[:-3]]
+    nodes = out_ref.shape[2]
+    cols = pl.ds(pl.multiple_of(pl.program_id(1) * nodes, nodes), nodes)
+    chunks = [r[own, cols] for r in refs[:-3]]
     low, high = refs[-3], refs[-2]
     half = low.shape[0] // group
     inner = pl.ds(pl.multiple_of(lax.rem(heading, half) * group, group), group)
-    chunks.append(jnp.where(heading < half, low[inner, :], high[inner, :]))
+    chunks.append(jnp.where(heading < half, low[inner, cols], high[inner, cols]))
     spectra = jnp.concatenate(chunks, axis=0)
     out_ref[0] = jnp.dot(basis_ref[...], spectra, preferred_element_type=F32).astype(BF)
 
@@ -240,9 +238,8 @@
         history_kernel,
         grid=(headings, cut),
         out_shape=jax.ShapeDtypeStruct((headings, steps, nodes), BF),
-        in_specs=[pl.BlockSpec((steps // cut, basis.shape[1]), lambda h, i: (i, 0))]
-        + [pl.BlockSpec(memory_space=pltpu.VMEM)] * len(chunks),
-        out_specs=pl.BlockSpec((1, steps // cut, nodes), lambda h, i: (h, i, 0)),
+        in_specs=[pl.BlockSpec(memory_space=pltpu.VMEM)] * (1 + len(chunks)),
+        out_specs=pl.BlockSpec((1, steps, nodes // cut), lambda h, i: (h, 0, i)),
         compiler_params=pltpu.CompilerParams(vmem_limit_bytes=VMEM_LIMIT),
         cost_estimate=pl.CostEstimate(
             flops=2 * steps * basis.shape[1] * headings * nodes,
@@ -278,8 +275,8 @@
 
     tile_ids = panel_tile.reshape(windows, width)
     weights = patch_weight.reshape(windows * width, 128)
-    slot_weight, rank = gather_weights(tile_ids, weights, owners, capacity)
-    sent = gather_rows(tile_ids, rank, slot_weight, spectra)
+    slot_weight, rank, hot = gather_weights(tile_ids, weights, owners, capacity)
+    sent = gather_rows(hot, rank, slot_weight, spectra)
     got = lax.all_to_all(sent, "freq", 0, 0, tiled=True)
     own = node_spectra(got.reshape(-1, got.shape[-1]))
 
@@ -288,10 +285,10 @@
         return lax.ppermute(chunk, "node", pairs)
 
     half = own.shape[0] // 2
+    plus1, minus1 = shift(own, 1), shift(own, -1)
     plus2, minus2 = shift(own, 2), shift(own, -2)
-    plus1, minus1 = shift(own, 1), shift(own, -1)
-    plus3, minus3 = shift(plus2, 1), shift(minus2, -1)
-    low4, high4 = shift(plus3[:half], 1), shift(minus3[half:], -1)
+    plus3, minus3 = shift(plus1, 2), shift(minus1, -2)
+    low4, high4 = shift(plus2[:half], 2), shift(minus2[half:], -2)
     chunks = [own, plus1, minus1, plus2, minus2, plus3, minus3, low4, high4]
     offsets = jnp.asarray([0, -1, 1, -2, 2, -3, 3, 4], jnp.int32)
     sources = (window + offsets) % windows

time: 109 us -> 114 us (1.046)
  waiting for transfers between devices: 55 us -> 61.5 us
    ppermute x8, waiting for transfers between devices: 20.2 us -> 26.9 us  [shift(): return lax.ppermute(chunk, 'node', pairs)]
  transfers between devices with their start and end apart: 10 -> 10, of which waited for: 8 -> 7; matrix products, arithmetic and copies ran while one was open for 3% -> 3% of each run, Pallas kernels for 5% -> 5%
where the time goes in v3:
time: 114 us; the launch traced here: 112 us
  waiting for transfers between devices  61.5 us (54%)
  starting transfers between devices  28.7 us (25%)
  Pallas kernels  18.6 us (16%)
  other arithmetic  2.54 us (2%)
    ppermute x8, waiting for transfers between devices, shift(): return lax.ppermute(chunk, 'node', pairs)  26.9 us
    all_to_all x1, waiting for transfers between devices, shards(): got = lax.all_to_all(sent, 'freq', 0, 0, tiled=True)  19.9 us
    all_to_all x1, starting transfers between devices, shards(): lax.all_to_all(scaled.reshape(owners * windows, headings, width), ('freq'...  14.7 us
    all_to_all x1, waiting for transfers between devices, shards(): lax.all_to_all(scaled.reshape(owners * windows, headings, width), ('freq'...  14.7 us
    ppermute x8, starting transfers between devices, shift(): return lax.ppermute(chunk, 'node', pairs)  8.81 us
    pallas_call x1, Pallas kernels, gather_weights(): pl.pallas_call(weight_kernel, out_shape=(jax.ShapeDtypeStruct((owners, ca...  5.76 us
    all_to_all x1, starting transfers between devices, shards(): got = lax.all_to_all(sent, 'freq', 0, 0, tiled=True)  5.25 us
    pallas_call x1, Pallas kernels, gather_rows(): pl.pallas_call(row_kernel, out_shape=jax.ShapeDtypeStruct((owners, capaci...  4.93 us
  transfers between devices with their start and end apart: 10, of which 7 were waited for; matrix products, arithmetic and copies ran while one was open for 3% of the time, Pallas kernels for 5%

profile of v3, /device:TPU:2, one launch (start us, length us, event | category | flops | bytes accessed | tf_op | source)
XLA Modules:
  0.0 111.7 jit_solution(13460088709455949927)
XLA Ops:
  0.0 0.0 copy-start.1
  0.0 0.0 copy-start
  0.0 2.3 %scale.1 = bf16[32,8,4,256]{3,2,1,0:T(4,128)(2,1)} custom-call(s32[1]{0:T(128)} %bitcast.1.group_ref, bf16[2,4,4,8192]{3,2,1,0:T(4,128)(2,1)} %pressure_ref.1, f32[4,128]{1,0:T(4,128)} %amp_ref.1, s32[4,128]{1,0:T(4,128)} %code_ref.1), custom_call_target="tpu_custom_call" | custom-call | flops 2000000 | bytes 1048576 | tf_op jit(solution)/shard_map/scale/pallas_call | solution.py:46
  2.3 14.7 %all-to-all-start = ((bf16[256,4,256]{2,1,0:T(4,128)(2,1)}), bf16[256,4,256]{2,1,0:T(4,128)(2,1)S(1)}, u32[]{:S(2)}, u32[]{:S(2)}) async-start(bf16[256,4,256]{2,1,0:T(4,128)(2,1)} %bitcast.12), calls=%async_computation | async-start | bytes 1048576 | tf_op jit(solution)/shard_map/all_to_all | solution.py:272
  17.0 0.0 copy-done.1
  17.0 0.0 copy-done
  17.0 5.8 %weight_slots.1 = (bf16[32,12,8,128]{3,2,1,0:T(8,128)(2,1)S(1)}, f32[8,256]{1,0:T(8,128)S(1)}, bf16[256,2048]{1,0:T(8,128)(2,1)S(1)}) custom-call(s32[8,256]{1,0:T(8,128)S(1)} %bitcast.10, bf16[2048,128]{1,0:T(8,128)(2,1)S(1)} %bitcast.11), custom_call_target="tpu_custom_call" | custom-call | flops 1610612736 | bytes 2097152 | tf_op jit(solution)/shard_map/weight_slots/pallas_call | solution.py:109
  22.8 14.7 %all-to-all-done = bf16[256,4,256]{2,1,0:T(4,128)(2,1)S(1)} async-done(((bf16[256,4,256]{2,1,0:T(4,128)(2,1)}), bf16[256,4,256]{2,1,0:T(4,128)(2,1)S(1)}, u32[]{:S(2)}, u32[]{:S(2)}) %all-to-all-start) | async-done | bytes 524320 | tf_op jit(solution)/shard_map/all_to_all | solution.py:272
  37.5 4.9 %row_slots.1 = bf16[32,12,8,256]{3,2,1,0:T(8,128)(2,1)} custom-call(bf16[256,2048]{1,0:T(8,128)(2,1)S(1)} %get-tuple-element.8.hot_ref, f32[8,256]{1,0:T(8,128)S(1)} %get-tuple-element.9.rank_ref, bf16[32,12,8,128]{3,2,1,0:T(8,128)(2,1)S(1)} %get-tuple-element.10.weight_ref, bf16[32,8,4,256]{3,2,1,0:T(4,128)(2,1)S(1)} %bitcast.9), custom_call_target="tpu_custom_call" | custom-call | flops 1610612736 | bytes 3145728 | tf_op jit(solution)/shard_map/row_slots/pallas_call | solution.py:166
  42.4 0.0 copy-start.2
  42.4 5.2 %all-to-all-start.1 = ((bf16[32,12,8,256]{3,2,1,0:T(8,128)(2,1)}), bf16[32,12,8,256]{3,2,1,0:T(8,128)(2,1)S(1)}, u32[]{:S(2)}, u32[]{:S(2)}) async-start(bf16[32,12,8,256]{3,2,1,0:T(8,128)(2,1)} %row_slots.1), calls=%async_computation.1 | async-start | bytes 3145728 | tf_op jit(solution)/shard_map/all_to_all | solution.py:280
  47.7 0.0 copy-done.2
  47.7 0.1 broadcast_in_dim.14
  47.8 0.1 reshape.61
  47.8 0.1 mul.43
  47.9 19.9 %all-to-all-done.1 = bf16[32,12,8,256]{3,2,1,0:T(8,128)(2,1)S(1)} async-done(((bf16[32,12,8,256]{3,2,1,0:T(8,128)(2,1)}), bf16[32,12,8,256]{3,2,1,0:T(8,128)(2,1)S(1)}, u32[]{:S(2)}, u32[]{:S(2)}) %all-to-all-start.1) | async-done | bytes 1572896 | tf_op jit(solution)/shard_map/all_to_all | solution.py:280
  67.8 0.8 node_spectra.1.refs_0_
  68.7 0.1 collective-permute-start.1
  68.8 2.0 %collective-permute-start = (bf16[128,1024]{1,0:T(8,128)(2,1)S(1)}, bf16[128,1024]{1,0:T(8,128)(2,1)S(1)}, u32[]{:S(2)}, u32[]{:S(2)}) collective-permute-start(bf16[128,1024]{1,0:T(8,128)(2,1)S(1)} %node_spectra.1.refs_0_), channel_id=1, source_target_pairs={{0,1},{1,2},{2,3},{3,4},{4,5},{5,6},{6,7},{7,0},{8,9},{9,10},{10,1... | collective-permute-start | bytes 786440 | tf_op jit(solution)/shard_map/ppermute | solution.py:285
  70.8 0.5 collective-permute-start.3
  71.3 2.5 %collective-permute-start.2 = (bf16[128,1024]{1,0:T(8,128)(2,1)S(1)}, bf16[128,1024]{1,0:T(8,128)(2,1)S(1)}, u32[]{:S(2)}, u32[]{:S(2)}) collective-permute-start(bf16[128,1024]{1,0:T(8,128)(2,1)S(1)} %node_spectra.1.refs_0_), channel_id=1, source_target_pairs={{0,2},{1,3},{2,4},{3,5},{4,6},{5,7},{6,0},{7,1},{8,10},{9,11},{10,... | collective-permute-start | bytes 786440 | tf_op jit(solution)/shard_map/ppermute | solution.py:285
  73.8 4.2 %collective-permute-done.1.refs_2_ = bf16[128,1024]{1,0:T(8,128)(2,1)S(1)} collective-permute-done((bf16[128,1024]{1,0:T(8,128)(2,1)S(1)}, bf16[128,1024]{1,0:T(8,128)(2,1)S(1)}, u32[]{:S(2)}, u32[]{:S(2)}) %collective-permute-start.1) | collective-permute-done | bytes 262176 | tf_op jit(solution)/shard_map/ppermute | solution.py:285
  78.1 0.4 collective-permute-start.5
  78.4 3.2 %collective-permute-done.refs_1_ = bf16[128,1024]{1,0:T(8,128)(2,1)S(1)} collective-permute-done((bf16[128,1024]{1,0:T(8,128)(2,1)S(1)}, bf16[128,1024]{1,0:T(8,128)(2,1)S(1)}, u32[]{:S(2)}, u32[]{:S(2)}) %collective-permute-start) | collective-permute-done | bytes 262176 | tf_op jit(solution)/shard_map/ppermute | solution.py:285
  81.6 0.3 collective-permute-start.4
  81.9 16.1 %collective-permute-done.3.refs_4_ = bf16[128,1024]{1,0:T(8,128)(2,1)S(1)} collective-permute-done((bf16[128,1024]{1,0:T(8,128)(2,1)S(1)}, bf16[128,1024]{1,0:T(8,128)(2,1)S(1)}, u32[]{:S(2)}, u32[]{:S(2)}) %collective-permute-start.3) | collective-permute-done | bytes 262176 | tf_op jit(solution)/shard_map/ppermute | solution.py:285
  98.1 1.8 %collective-permute-start.7 = (bf16[64,1024]{1,0:T(8,128)(2,1)S(1)}, bf16[64,1024]{1,0:T(8,128)(2,1)S(1)}, u32[]{:S(2)}, u32[]{:S(2)}) collective-permute-start(bf16[64,1024]{1,0:T(8,128)(2,1)S(1)} %slice.9), channel_id=1, source_target_pairs={{0,6},{1,7},{2,0},{3,1},{4,2},{5,3},{6,4},{7,5},{8,14},{9,15},{10,... | collective-permute-start | bytes 393224 | tf_op jit(solution)/shard_map/ppermute | solution.py:285
  99.8 0.0 collective-permute-done.2.refs_3_
  99.8 1.3 %collective-permute-start.6 = (bf16[64,1024]{1,0:T(8,128)(2,1)S(1)}, bf16[64,1024]{1,0:T(8,128)(2,1)S(1)}, u32[]{:S(2)}, u32[]{:S(2)}) collective-permute-start(bf16[64,1024]{1,0:T(8,128)(2,1)S(1)} %slice.8), channel_id=1, source_target_pairs={{0,2},{1,3},{2,4},{3,5},{4,6},{5,7},{6,0},{7,1},{8,10},{9,11},{10,... | collective-permute-start | bytes 393224 | tf_op jit(solution)/shard_map/ppermute | solution.py:285
  101.2 2.5 %select_convert_fusion.basis_ref = bf16[512,256]{1,0:T(8,128)(2,1)S(1)} fusion(s32[512]{0:T(512)S(1)} %iota_add_fusion, s32[256]{0:T(256)S(1)} %multiply_add_fusion, pred[256]{0:T(512)(128)(4,1)S(1)} %broadcast_compare_fusion), kind=kLoop, calls=%fused_computation.8 | loop fusion | flops 2228224 | bytes 265472 | tf_op jit(solution)/shard_map/convert_element_type | solution.py:260
  103.7 2.3 %collective-permute-done.7.refs_8_ = bf16[64,1024]{1,0:T(8,128)(2,1)S(1)} collective-permute-done((bf16[64,1024]{1,0:T(8,128)(2,1)S(1)}, bf16[64,1024]{1,0:T(8,128)(2,1)S(1)}, u32[]{:S(2)}, u32[]{:S(2)}) %collective-permute-start.7) | collective-permute-done | bytes 131104 | tf_op jit(solution)/shard_map/ppermute | solution.py:285
  106.0 1.0 collective-permute-done.6.refs_7_
  107.0 0.0 collective-permute-done.5.refs_6_
  107.0 0.0 collective-permute-done.4.refs_5_
  107.0 4.7 %histories.1 = bf16[4,512,1024]{2,1,0:T(8,128)(2,1)} custom-call(bf16[512,256]{1,0:T(8,128)(2,1)S(1)} %select_convert_fusion.basis_ref, bf16[128,1024]{1,0:T(8,128)(2,1)S(1)} %node_spectra.1.refs_0_, bf16[128,1024]{1,0:T(8,128)(2,1)S(1)} %collective-permute-done.refs_1_, bf16[128,1024]{1,0:T(8,128)(2,1)S(1)} %collective-permute-done.1.refs_2_, ...), custom_call_target="tpu_custom_call" | custom-call | flops 1073741824 | bytes 6291456 | tf_op jit(solution)/shard_map/histories/pallas_call | solution.py:237
  (8 shorter events, 0.1 us)
Async XLA Ops:
  0.0 17.0 %copy-start.1 = (s32[1,8,256,1]{2,3,1,0:T(1,128)S(1)}, s32[1,8,256,1]{2,3,1,0:T(1,128)}, u32[]{:S(2)}) copy-start(s32[1,8,256,1]{2,3,1,0:T(1,128)} %param.9) | copy-start | bytes 24580
  0.0 17.0 %copy-start = (bf16[1,8,256,128]{3,2,1,0:T(8,128)(2,1)S(1)}, bf16[1,8,256,128]{3,2,1,0:T(8,128)(2,1)}, u32[]{:S(2)}) copy-start(bf16[1,8,256,128]{3,2,1,0:T(8,128)(2,1)} %param.10) | copy-start | bytes 1572868
  2.3 35.1 %all-to-all-start = ((bf16[256,4,256]{2,1,0:T(4,128)(2,1)}), bf16[256,4,256]{2,1,0:T(4,128)(2,1)S(1)}, u32[]{:S(2)}, u32[]{:S(2)}) async-start(bf16[256,4,256]{2,1,0:T(4,128)(2,1)} %bitcast.12), calls=%async_computation | async-start | bytes 1048576 | tf_op jit(solution)/shard_map/all_to_all | solution.py:272
  42.4 5.3 %copy-start.2 = (s32[8]{0:T(128)S(1)}, s32[8]{0:T(128)}, u32[]{:S(2)}) copy-start(s32[8]{0:T(128)} %constant.63.clone) | copy-start | bytes 100
  42.4 25.4 %all-to-all-start.1 = ((bf16[32,12,8,256]{3,2,1,0:T(8,128)(2,1)}), bf16[32,12,8,256]{3,2,1,0:T(8,128)(2,1)S(1)}, u32[]{:S(2)}, u32[]{:S(2)}) async-start(bf16[32,12,8,256]{3,2,1,0:T(8,128)(2,1)} %row_slots.1), calls=%async_computation.1 | async-start | bytes 3145728 | tf_op jit(solution)/shard_map/all_to_all | solution.py:280
  68.7 9.4 %collective-permute-start.1 = (bf16[128,1024]{1,0:T(8,128)(2,1)S(1)}, bf16[128,1024]{1,0:T(8,128)(2,1)S(1)}, u32[]{:S(2)}, u32[]{:S(2)}) collective-permute-start(bf16[128,1024]{1,0:T(8,128)(2,1)S(1)} %node_spectra.1.refs_0_), channel_id=1, source_target_pairs={{0,7},{1,0},{2,1},{3,2},{4,3},{5,4},{6,5},{7,6},{8,15},{9,8},{10,9... | collective-permute-start | bytes 786440 | tf_op jit(solution)/shard_map/ppermute | solution.py:285
  68.8 12.8 %collective-permute-start = (bf16[128,1024]{1,0:T(8,128)(2,1)S(1)}, bf16[128,1024]{1,0:T(8,128)(2,1)S(1)}, u32[]{:S(2)}, u32[]{:S(2)}) collective-permute-start(bf16[128,1024]{1,0:T(8,128)(2,1)S(1)} %node_spectra.1.refs_0_), channel_id=1, source_target_pairs={{0,1},{1,2},{2,3},{3,4},{4,5},{5,6},{6,7},{7,0},{8,9},{9,10},{10,1... | collective-permute-start | bytes 786440 | tf_op jit(solution)/shard_map/ppermute | solution.py:285
  70.8 27.2 %collective-permute-start.3 = (bf16[128,1024]{1,0:T(8,128)(2,1)S(1)}, bf16[128,1024]{1,0:T(8,128)(2,1)S(1)}, u32[]{:S(2)}, u32[]{:S(2)}) collective-permute-start(bf16[128,1024]{1,0:T(8,128)(2,1)S(1)} %node_spectra.1.refs_0_), channel_id=1, source_target_pairs={{0,6},{1,7},{2,0},{3,1},{4,2},{5,3},{6,4},{7,5},{8,14},{9,15},{10,... | collective-permute-start | bytes 786440 | tf_op jit(solution)/shard_map/ppermute | solution.py:285
  71.3 28.5 %collective-permute-start.2 = (bf16[128,1024]{1,0:T(8,128)(2,1)S(1)}, bf16[128,1024]{1,0:T(8,128)(2,1)S(1)}, u32[]{:S(2)}, u32[]{:S(2)}) collective-permute-start(bf16[128,1024]{1,0:T(8,128)(2,1)S(1)} %node_spectra.1.refs_0_), channel_id=1, source_target_pairs={{0,2},{1,3},{2,4},{3,5},{4,6},{5,7},{6,0},{7,1},{8,10},{9,11},{10,... | collective-permute-start | bytes 786440 | tf_op jit(solution)/shard_map/ppermute | solution.py:285
  78.1 28.9 %collective-permute-start.5 = (bf16[128,1024]{1,0:T(8,128)(2,1)S(1)}, bf16[128,1024]{1,0:T(8,128)(2,1)S(1)}, u32[]{:S(2)}, u32[]{:S(2)}) collective-permute-start(bf16[128,1024]{1,0:T(8,128)(2,1)S(1)} %collective-permute-done.1.refs_2_), channel_id=1, source_target_pairs={{0,6},{1,7},{2,0},{3,1},{4,2},{5,3},{6,4},{7,5},{8,14},{9,15},{10,... | collective-permute-start | bytes 786440 | tf_op jit(solution)/shard_map/ppermute | solution.py:285
  81.6 25.4 %collective-permute-start.4 = (bf16[128,1024]{1,0:T(8,128)(2,1)S(1)}, bf16[128,1024]{1,0:T(8,128)(2,1)S(1)}, u32[]{:S(2)}, u32[]{:S(2)}) collective-permute-start(bf16[128,1024]{1,0:T(8,128)(2,1)S(1)} %collective-permute-done.refs_1_), channel_id=1, source_target_pairs={{0,2},{1,3},{2,4},{3,5},{4,6},{5,7},{6,0},{7,1},{8,10},{9,11},{10,... | collective-permute-start | bytes 786440 | tf_op jit(solution)/shard_map/ppermute | solution.py:285
  98.1 7.9 %collective-permute-start.7 = (bf16[64,1024]{1,0:T(8,128)(2,1)S(1)}, bf16[64,1024]{1,0:T(8,128)(2,1)S(1)}, u32[]{:S(2)}, u32[]{:S(2)}) collective-permute-start(bf16[64,1024]{1,0:T(8,128)(2,1)S(1)} %slice.9), channel_id=1, source_target_pairs={{0,6},{1,7},{2,0},{3,1},{4,2},{5,3},{6,4},{7,5},{8,14},{9,15},{10,... | collective-permute-start | bytes 393224 | tf_op jit(solution)/shard_map/ppermute | solution.py:285
  99.8 7.2 %collective-permute-start.6 = (bf16[64,1024]{1,0:T(8,128)(2,1)S(1)}, bf16[64,1024]{1,0:T(8,128)(2,1)S(1)}, u32[]{:S(2)}, u32[]{:S(2)}) collective-permute-start(bf16[64,1024]{1,0:T(8,128)(2,1)S(1)} %slice.8), channel_id=1, source_target_pairs={{0,2},{1,3},{2,4},{3,5},{4,6},{5,7},{6,0},{7,1},{8,10},{9,11},{10,... | collective-permute-start | bytes 393224 | tf_op jit(solution)/shard_map/ppermute | solution.py:285

commit v4 on v3

--- a/solution.py
+++ b/solution.py
@@ -182,9 +182,10 @@
     )(hot, rank, weights, spectra)
 
 
-def node_kernel(slots_ref, out_ref, wide_ref):
+def node_kernel(slots_ref, low_ref, high_ref, wide_ref):
     count, width = slots_ref.shape
-    lanes = out_ref.shape[0]
+    half_lanes = low_ref.shape[0]
+    lanes = 2 * half_lanes
     nodes = width - lanes
     for half in range(2):
         wide_ref[half] = slots_ref[:, half * lanes : (half + 1) * lanes].astype(F32)
@@ -194,7 +195,8 @@
             wide_ref[0, own, :].astype(BF), wide_ref[1, own, :].astype(BF),
             (((0,), (0,)), ((), ())), preferred_element_type=F32,
         )
-        out_ref[:, tile * nodes : (tile + 1) * nodes] = part.astype(BF)
+        low_ref[:, tile * nodes : (tile + 1) * nodes] = part[:half_lanes].astype(BF)
+        high_ref[:, tile * nodes : (tile + 1) * nodes] = part[half_lanes:].astype(BF)
 
 
 def node_spectra(slots):
@@ -202,9 +204,9 @@
     lanes = width // 2
     return pl.pallas_call(
         node_kernel,
-        out_shape=jax.ShapeDtypeStruct((lanes, TILE_DEV * lanes), BF),
+        out_shape=(jax.ShapeDtypeStruct((lanes // 2, TILE_DEV * lanes), BF),) * 2,
         in_specs=[pl.BlockSpec(memory_space=pltpu.VMEM)],
-        out_specs=pl.BlockSpec(memory_space=pltpu.VMEM),
+        out_specs=(pl.BlockSpec(memory_space=pltpu.VMEM),) * 2,
         scratch_shapes=[pltpu.VMEM((2, count, lanes), F32)],
         compiler_params=pltpu.CompilerParams(vmem_limit_bytes=VMEM_LIMIT),
         cost_estimate=pl.CostEstimate(
@@ -215,24 +217,26 @@
 
 
 def history_kernel(basis_ref, *refs):
-    out_ref = refs[-1]
+    spectra_refs, out_ref = refs[:-1], refs[-1]
+    count = len(spectra_refs) // 2
+    group = basis_ref.shape[1] // count
+    half = spectra_refs[0].shape[0] // group
     heading = pl.program_id(0)
-    group = basis_ref.shape[1] // (len(refs) - 2)
-    own = pl.ds(pl.multiple_of(heading * group, group), group)
+    own = pl.ds(pl.multiple_of(lax.rem(heading, half) * group, group), group)
     nodes = out_ref.shape[2]
     cols = pl.ds(pl.multiple_of(pl.program_id(1) * nodes, nodes), nodes)
-    chunks = [r[own, cols] for r in refs[:-3]]
-    low, high = refs[-3], refs[-2]
-    half = low.shape[0] // group
-    inner = pl.ds(pl.multiple_of(lax.rem(heading, half) * group, group), group)
-    chunks.append(jnp.where(heading < half, low[inner, cols], high[inner, cols]))
-    spectra = jnp.concatenate(chunks, axis=0)
-    out_ref[0] = jnp.dot(basis_ref[...], spectra, preferred_element_type=F32).astype(BF)
+    for part in range(2):
+
+        @pl.when(heading // half == part)
+        def _():
+            chunks = [r[own, cols] for r in spectra_refs[part * count : (part + 1) * count]]
+            spectra = jnp.concatenate(chunks, axis=0)
+            out_ref[0] = jnp.dot(basis_ref[...], spectra, preferred_element_type=F32).astype(BF)
 
 
 def histories(basis, chunks, headings):
     steps = basis.shape[0]
-    lanes, nodes = chunks[0].shape
+    nodes = chunks[0].shape[1]
     cut = 2
     return pl.pallas_call(
         history_kernel,
@@ -278,19 +282,25 @@
     slot_weight, rank, hot = gather_weights(tile_ids, weights, owners, capacity)
     sent = gather_rows(hot, rank, slot_weight, spectra)
     got = lax.all_to_all(sent, "freq", 0, 0, tiled=True)
-    own = node_spectra(got.reshape(-1, got.shape[-1]))
+    low, high = node_spectra(got.reshape(-1, got.shape[-1]))
 
     def shift(chunk, distance):
         pairs = [(k, (k + distance) % windows) for k in range(windows)]
         return lax.ppermute(chunk, "node", pairs)
 
-    half = own.shape[0] // 2
-    plus1, minus1 = shift(own, 1), shift(own, -1)
-    plus2, minus2 = shift(own, 2), shift(own, -2)
-    plus3, minus3 = shift(plus1, 2), shift(minus1, -2)
-    low4, high4 = shift(plus2[:half], 2), shift(minus2[half:], -2)
-    chunks = [own, plus1, minus1, plus2, minus2, plus3, minus3, low4, high4]
-    offsets = jnp.asarray([0, -1, 1, -2, 2, -3, 3, 4], jnp.int32)
+    lows, highs, offsets = [low], [high], [0]
+    low_up = low_down = low
+    high_up = high_down = high
+    for step in range(1, windows // 2):
+        low_up = shift(low_up, 1)
+        high_down = shift(high_down, -1)
+        high_up = shift(high_up, 1)
+        low_down = shift(low_down, -1)
+        lows += [low_up, low_down]
+        highs += [high_up, high_down]
+        offsets += [-step, step]
+    chunks = lows + [shift(low_up, 1)] + highs + [shift(high_down, -1)]
+    offsets = jnp.asarray(offsets + [windows // 2], jnp.int32)
     sources = (window + offsets) % windows
     basis = window_basis(sources, window, TSTEPS // windows, owners, fl_count)
     return histories(basis, chunks, headings)

time: 114 us -> 103 us (0.904)
  waiting for transfers between devices: 61.5 us -> 39.2 us
  starting transfers between devices: 28.7 us -> 41 us
    ppermute x8 -> x14, waiting for transfers between devices: 26.9 us -> 4.33 us  [shift(): return lax.ppermute(chunk, 'node', pairs)]
    ppermute x8 -> x14, starting transfers between devices: 8.81 us -> 21.2 us  [shift(): return lax.ppermute(chunk, 'node', pairs)]
  transfers between devices with their start and end apart: 10 -> 16, of which waited for: 7 -> 9; matrix products, arithmetic and copies ran while one was open for 3% -> 3% of each run, Pallas kernels for 5% -> 6%
where the time goes in v4:
time: 103 us; the launch traced here: 102 us
  starting transfers between devices  41 us (40%)
  waiting for transfers between devices  39.2 us (38%)
  Pallas kernels  18.6 us (18%)
  other arithmetic  2.54 us (2%)
    ppermute x14, starting transfers between devices, shift(): return lax.ppermute(chunk, 'node', pairs)  21.2 us
    all_to_all x1, waiting for transfers between devices, shards(): got = lax.all_to_all(sent, 'freq', 0, 0, tiled=True)  20.2 us
    all_to_all x1, starting transfers between devices, shards(): lax.all_to_all(scaled.reshape(owners * windows, headings, width), ('freq'...  14.7 us
    all_to_all x1, waiting for transfers between devices, shards(): lax.all_to_all(scaled.reshape(owners * windows, headings, width), ('freq'...  14.7 us
    pallas_call x1, Pallas kernels, gather_weights(): pl.pallas_call(weight_kernel, out_shape=(jax.ShapeDtypeStruct((owners, ca...  5.75 us
    all_to_all x1, starting transfers between devices, shards(): got = lax.all_to_all(sent, 'freq', 0, 0, tiled=True)  5.12 us
    pallas_call x1, Pallas kernels, gather_rows(): pl.pallas_call(row_kernel, out_shape=jax.ShapeDtypeStruct((owners, capaci...  4.93 us
    pallas_call x1, Pallas kernels, histories(): pl.pallas_call(history_kernel, grid=(headings, cut), out_shape=jax.ShapeD...  4.72 us
  transfers between devices with their start and end apart: 16, of which 9 were waited for; matrix products, arithmetic and copies ran while one was open for 3% of the time, Pallas kernels for 6%

profile of v4, /device:TPU:2, one launch (start us, length us, event | category | flops | bytes accessed | tf_op | source)
XLA Modules:
  0.0 101.7 jit_solution(16408474287044165532)
XLA Ops:
  0.0 0.0 copy-start.1
  0.0 0.0 copy-start
  0.0 2.3 %scale.1 = bf16[32,8,4,256]{3,2,1,0:T(4,128)(2,1)} custom-call(s32[1]{0:T(128)} %bitcast.1.group_ref, bf16[2,4,4,8192]{3,2,1,0:T(4,128)(2,1)} %pressure_ref.1, f32[4,128]{1,0:T(4,128)} %amp_ref.1, s32[4,128]{1,0:T(4,128)} %code_ref.1), custom_call_target="tpu_custom_call" | custom-call | flops 2000000 | bytes 1048576 | tf_op jit(solution)/shard_map/scale/pallas_call | solution.py:46
  2.3 14.7 %all-to-all-start = ((bf16[256,4,256]{2,1,0:T(4,128)(2,1)}), bf16[256,4,256]{2,1,0:T(4,128)(2,1)S(1)}, u32[]{:S(2)}, u32[]{:S(2)}) async-start(bf16[256,4,256]{2,1,0:T(4,128)(2,1)} %bitcast.12), calls=%async_computation | async-start | bytes 1048576 | tf_op jit(solution)/shard_map/all_to_all | solution.py:276
  17.0 0.0 copy-done.1
  17.0 0.0 copy-done
  17.0 5.8 %weight_slots.1 = (bf16[32,12,8,128]{3,2,1,0:T(8,128)(2,1)S(1)}, f32[8,256]{1,0:T(8,128)S(1)}, bf16[256,2048]{1,0:T(8,128)(2,1)S(1)}) custom-call(s32[8,256]{1,0:T(8,128)S(1)} %bitcast.10, bf16[2048,128]{1,0:T(8,128)(2,1)S(1)} %bitcast.11), custom_call_target="tpu_custom_call" | custom-call | flops 1610612736 | bytes 2097152 | tf_op jit(solution)/shard_map/weight_slots/pallas_call | solution.py:109
  22.8 14.7 %all-to-all-done = bf16[256,4,256]{2,1,0:T(4,128)(2,1)S(1)} async-done(((bf16[256,4,256]{2,1,0:T(4,128)(2,1)}), bf16[256,4,256]{2,1,0:T(4,128)(2,1)S(1)}, u32[]{:S(2)}, u32[]{:S(2)}) %all-to-all-start) | async-done | bytes 524320 | tf_op jit(solution)/shard_map/all_to_all | solution.py:276
  37.5 4.9 %row_slots.1 = bf16[32,12,8,256]{3,2,1,0:T(8,128)(2,1)} custom-call(bf16[256,2048]{1,0:T(8,128)(2,1)S(1)} %get-tuple-element.10.hot_ref, f32[8,256]{1,0:T(8,128)S(1)} %get-tuple-element.11.rank_ref, bf16[32,12,8,128]{3,2,1,0:T(8,128)(2,1)S(1)} %get-tuple-element.12.weight_ref, bf16[32,8,4,256]{3,2,1,0:T(4,128)(2,1)S(1)} %bitcast.9), custom_call_target="tpu_custom_call" | custom-call | flops 1610612736 | bytes 3145728 | tf_op jit(solution)/shard_map/row_slots/pallas_call | solution.py:166
  42.4 5.1 %all-to-all-start.1 = ((bf16[32,12,8,256]{3,2,1,0:T(8,128)(2,1)}), bf16[32,12,8,256]{3,2,1,0:T(8,128)(2,1)S(1)}, u32[]{:S(2)}, u32[]{:S(2)}) async-start(bf16[32,12,8,256]{3,2,1,0:T(8,128)(2,1)} %row_slots.1), calls=%async_computation.1 | async-start | bytes 3145728 | tf_op jit(solution)/shard_map/all_to_all | solution.py:284
  47.5 0.0 copy-start.2
  47.5 20.2 %all-to-all-done.1 = bf16[32,12,8,256]{3,2,1,0:T(8,128)(2,1)S(1)} async-done(((bf16[32,12,8,256]{3,2,1,0:T(8,128)(2,1)}), bf16[32,12,8,256]{3,2,1,0:T(8,128)(2,1)S(1)}, u32[]{:S(2)}, u32[]{:S(2)}) %all-to-all-start.1) | async-done | bytes 1572896 | tf_op jit(solution)/shard_map/all_to_all | solution.py:284
  67.7 0.8 node_spectra.1
  68.6 1.1 %collective-permute-start = (bf16[64,1024]{1,0:T(8,128)(2,1)S(1)}, bf16[64,1024]{1,0:T(8,128)(2,1)S(1)}, u32[]{:S(2)}, u32[]{:S(2)}) collective-permute-start(bf16[64,1024]{1,0:T(8,128)(2,1)S(1)} %get-tuple-element.13.refs_0_), channel_id=1, source_target_pairs={{0,1},{1,2},{2,3},{3,4},{4,5},{5,6},{6,7},{7,0},{8,9},{9,10},{10,1... | collective-permute-start | bytes 393224 | tf_op jit(solution)/shard_map/ppermute | solution.py:289
  69.6 2.2 %collective-permute-start.8 = (bf16[64,1024]{1,0:T(8,128)(2,1)S(1)}, bf16[64,1024]{1,0:T(8,128)(2,1)S(1)}, u32[]{:S(2)}, u32[]{:S(2)}) collective-permute-start(bf16[64,1024]{1,0:T(8,128)(2,1)S(1)} %get-tuple-element.14.refs_8_), channel_id=1, source_target_pairs={{0,7},{1,0},{2,1},{3,2},{4,3},{5,4},{6,5},{7,6},{8,15},{9,8},{10,9... | collective-permute-start | bytes 393224 | tf_op jit(solution)/shard_map/ppermute | solution.py:289
  71.9 0.0 copy-done.2
  71.9 0.1 broadcast_in_dim.14
  72.0 0.1 reshape.61
  72.0 0.1 mul.43
  72.1 0.0 collective-permute-start.1
  72.1 2.0 %collective-permute-start.7 = (bf16[64,1024]{1,0:T(8,128)(2,1)S(1)}, bf16[64,1024]{1,0:T(8,128)(2,1)S(1)}, u32[]{:S(2)}, u32[]{:S(2)}) collective-permute-start(bf16[64,1024]{1,0:T(8,128)(2,1)S(1)} %get-tuple-element.14.refs_8_), channel_id=1, source_target_pairs={{0,1},{1,2},{2,3},{3,4},{4,5},{5,6},{6,7},{7,0},{8,9},{9,10},{10,1... | collective-permute-start | bytes 393224 | tf_op jit(solution)/shard_map/ppermute | solution.py:289
  74.2 1.5 %collective-permute-done.refs_1_ = bf16[64,1024]{1,0:T(8,128)(2,1)S(1)} collective-permute-done((bf16[64,1024]{1,0:T(8,128)(2,1)S(1)}, bf16[64,1024]{1,0:T(8,128)(2,1)S(1)}, u32[]{:S(2)}, u32[]{:S(2)}) %collective-permute-start) | collective-permute-done | bytes 131104 | tf_op jit(solution)/shard_map/ppermute | solution.py:289
  75.7 0.0 collective-permute-start.2
  75.7 0.1 collective-permute-done.8.refs_10_
  75.8 3.7 %collective-permute-start.10 = (bf16[64,1024]{1,0:T(8,128)(2,1)S(1)}, bf16[64,1024]{1,0:T(8,128)(2,1)S(1)}, u32[]{:S(2)}, u32[]{:S(2)}) collective-permute-start(bf16[64,1024]{1,0:T(8,128)(2,1)S(1)} %collective-permute-done.8.refs_10_), channel_id=1, source_target_pairs={{0,7},{1,0},{2,1},{3,2},{4,3},{5,4},{6,5},{7,6},{8,15},{9,8},{10,9... | collective-permute-start | bytes 393224 | tf_op jit(solution)/shard_map/ppermute | solution.py:289
  79.5 0.0 collective-permute-done.1.refs_2_
  79.5 2.0 %collective-permute-start.3 = (bf16[64,1024]{1,0:T(8,128)(2,1)S(1)}, bf16[64,1024]{1,0:T(8,128)(2,1)S(1)}, u32[]{:S(2)}, u32[]{:S(2)}) collective-permute-start(bf16[64,1024]{1,0:T(8,128)(2,1)S(1)} %collective-permute-done.1.refs_2_), channel_id=1, source_target_pairs={{0,7},{1,0},{2,1},{3,2},{4,3},{5,4},{6,5},{7,6},{8,15},{9,8},{10,9... | collective-permute-start | bytes 393224 | tf_op jit(solution)/shard_map/ppermute | solution.py:289
  81.5 0.0 collective-permute-done.7.refs_9_
  81.5 0.1 collective-permute-start.9
  81.6 0.3 collective-permute-done.2.refs_3_
  81.9 0.1 collective-permute-start.4
  82.0 1.0 collective-permute-done.10.refs_12_
  83.0 3.7 %collective-permute-start.12 = (bf16[64,1024]{1,0:T(8,128)(2,1)S(1)}, bf16[64,1024]{1,0:T(8,128)(2,1)S(1)}, u32[]{:S(2)}, u32[]{:S(2)}) collective-permute-start(bf16[64,1024]{1,0:T(8,128)(2,1)S(1)} %collective-permute-done.10.refs_12_), channel_id=1, source_target_pairs={{0,7},{1,0},{2,1},{3,2},{4,3},{5,4},{6,5},{7,6},{8,15},{9,8},{10,9... | collective-permute-start | bytes 393224 | tf_op jit(solution)/shard_map/ppermute | solution.py:289
  86.7 0.0 collective-permute-done.3.refs_4_
  86.7 2.7 %collective-permute-start.5 = (bf16[64,1024]{1,0:T(8,128)(2,1)S(1)}, bf16[64,1024]{1,0:T(8,128)(2,1)S(1)}, u32[]{:S(2)}, u32[]{:S(2)}) collective-permute-start(bf16[64,1024]{1,0:T(8,128)(2,1)S(1)} %collective-permute-done.3.refs_4_), channel_id=1, source_target_pairs={{0,7},{1,0},{2,1},{3,2},{4,3},{5,4},{6,5},{7,6},{8,15},{9,8},{10,9... | collective-permute-start | bytes 393224 | tf_op jit(solution)/shard_map/ppermute | solution.py:289
  89.4 0.0 collective-permute-done.9.refs_11_
  89.4 0.0 collective-permute-start.11
  89.4 0.6 collective-permute-done.4.refs_5_
  89.9 0.0 collective-permute-start.6
  89.9 0.5 collective-permute-done.12.refs_14_
  90.4 3.7 %collective-permute-start.13 = (bf16[64,1024]{1,0:T(8,128)(2,1)S(1)}, bf16[64,1024]{1,0:T(8,128)(2,1)S(1)}, u32[]{:S(2)}, u32[]{:S(2)}) collective-permute-start(bf16[64,1024]{1,0:T(8,128)(2,1)S(1)} %collective-permute-done.12.refs_14_), channel_id=1, source_target_pairs={{0,7},{1,0},{2,1},{3,2},{4,3},{5,4},{6,5},{7,6},{8,15},{9,8},{10,9... | collective-permute-start | bytes 393224 | tf_op jit(solution)/shard_map/ppermute | solution.py:289
  94.1 2.5 %select_convert_fusion.basis_ref = bf16[512,256]{1,0:T(8,128)(2,1)S(1)} fusion(s32[512]{0:T(512)S(1)} %iota_add_fusion, s32[256]{0:T(256)S(1)} %multiply_add_fusion, pred[256]{0:T(512)(128)(4,1)S(1)} %broadcast_compare_fusion), kind=kLoop, calls=%fused_computation.8 | loop fusion | flops 2228224 | bytes 265472 | tf_op jit(solution)/shard_map/convert_element_type | solution.py:264
  96.6 0.0 collective-permute-done.5.refs_6_
  96.6 0.0 collective-permute-done.11.refs_13_
  96.6 0.3 collective-permute-done.6.refs_7_
  96.9 0.0 collective-permute-done.13.refs_15_
  96.9 4.7 %histories.1 = bf16[4,512,1024]{2,1,0:T(8,128)(2,1)} custom-call(bf16[512,256]{1,0:T(8,128)(2,1)S(1)} %select_convert_fusion.basis_ref, bf16[64,1024]{1,0:T(8,128)(2,1)S(1)} %get-tuple-element.13.refs_0_, bf16[64,1024]{1,0:T(8,128)(2,1)S(1)} %collective-permute-done.refs_1_, bf16[64,1024]{1,0:T(8,128)(2,1)S(1)} %collective-permute-done.1.refs_2_, ...), custom_call_target="tpu_custom_call" | custom-call | flops 1073741824 | bytes 6291456 | tf_op jit(solution)/shard_map/histories/pallas_call | solution.py:241
  (6 shorter events, 0.0 us)
Async XLA Ops:
  0.0 17.0 %copy-start.1 = (s32[1,8,256,1]{2,3,1,0:T(1,128)S(1)}, s32[1,8,256,1]{2,3,1,0:T(1,128)}, u32[]{:S(2)}) copy-start(s32[1,8,256,1]{2,3,1,0:T(1,128)} %param.9) | copy-start | bytes 24580
  0.0 17.0 %copy-start = (bf16[1,8,256,128]{3,2,1,0:T(8,128)(2,1)S(1)}, bf16[1,8,256,128]{3,2,1,0:T(8,128)(2,1)}, u32[]{:S(2)}) copy-start(bf16[1,8,256,128]{3,2,1,0:T(8,128)(2,1)} %param.10) | copy-start | bytes 1572868
  2.3 35.1 %all-to-all-start = ((bf16[256,4,256]{2,1,0:T(4,128)(2,1)}), bf16[256,4,256]{2,1,0:T(4,128)(2,1)S(1)}, u32[]{:S(2)}, u32[]{:S(2)}) async-start(bf16[256,4,256]{2,1,0:T(4,128)(2,1)} %bitcast.12), calls=%async_computation | async-start | bytes 1048576 | tf_op jit(solution)/shard_map/all_to_all | solution.py:276
  42.4 25.3 %all-to-all-start.1 = ((bf16[32,12,8,256]{3,2,1,0:T(8,128)(2,1)}), bf16[32,12,8,256]{3,2,1,0:T(8,128)(2,1)S(1)}, u32[]{:S(2)}, u32[]{:S(2)}) async-start(bf16[32,12,8,256]{3,2,1,0:T(8,128)(2,1)} %row_slots.1), calls=%async_computation.1 | async-start | bytes 3145728 | tf_op jit(solution)/shard_map/all_to_all | solution.py:284
  47.5 24.4 %copy-start.2 = (s32[8]{0:T(128)S(1)}, s32[8]{0:T(128)}, u32[]{:S(2)}) copy-start(s32[8]{0:T(128)} %constant.63.clone) | copy-start | bytes 100
  68.6 7.1 %collective-permute-start = (bf16[64,1024]{1,0:T(8,128)(2,1)S(1)}, bf16[64,1024]{1,0:T(8,128)(2,1)S(1)}, u32[]{:S(2)}, u32[]{:S(2)}) collective-permute-start(bf16[64,1024]{1,0:T(8,128)(2,1)S(1)} %get-tuple-element.13.refs_0_), channel_id=1, source_target_pairs={{0,1},{1,2},{2,3},{3,4},{4,5},{5,6},{6,7},{7,0},{8,9},{9,10},{10,1... | collective-permute-start | bytes 393224 | tf_op jit(solution)/shard_map/ppermute | solution.py:289
  69.6 6.2 %collective-permute-start.8 = (bf16[64,1024]{1,0:T(8,128)(2,1)S(1)}, bf16[64,1024]{1,0:T(8,128)(2,1)S(1)}, u32[]{:S(2)}, u32[]{:S(2)}) collective-permute-start(bf16[64,1024]{1,0:T(8,128)(2,1)S(1)} %get-tuple-element.14.refs_8_), channel_id=1, source_target_pairs={{0,7},{1,0},{2,1},{3,2},{4,3},{5,4},{6,5},{7,6},{8,15},{9,8},{10,9... | collective-permute-start | bytes 393224 | tf_op jit(solution)/shard_map/ppermute | solution.py:289
  72.1 7.3 %collective-permute-start.1 = (bf16[64,1024]{1,0:T(8,128)(2,1)S(1)}, bf16[64,1024]{1,0:T(8,128)(2,1)S(1)}, u32[]{:S(2)}, u32[]{:S(2)}) collective-permute-start(bf16[64,1024]{1,0:T(8,128)(2,1)S(1)} %get-tuple-element.13.refs_0_), channel_id=1, source_target_pairs={{0,7},{1,0},{2,1},{3,2},{4,3},{5,4},{6,5},{7,6},{8,15},{9,8},{10,9... | collective-permute-start | bytes 393224 | tf_op jit(solution)/shard_map/ppermute | solution.py:289
  72.1 9.3 %collective-permute-start.7 = (bf16[64,1024]{1,0:T(8,128)(2,1)S(1)}, bf16[64,1024]{1,0:T(8,128)(2,1)S(1)}, u32[]{:S(2)}, u32[]{:S(2)}) collective-permute-start(bf16[64,1024]{1,0:T(8,128)(2,1)S(1)} %get-tuple-element.14.refs_8_), channel_id=1, source_target_pairs={{0,1},{1,2},{2,3},{3,4},{4,5},{5,6},{6,7},{7,0},{8,9},{9,10},{10,1... | collective-permute-start | bytes 393224 | tf_op jit(solution)/shard_map/ppermute | solution.py:289
  75.7 6.2 %collective-permute-start.2 = (bf16[64,1024]{1,0:T(8,128)(2,1)S(1)}, bf16[64,1024]{1,0:T(8,128)(2,1)S(1)}, u32[]{:S(2)}, u32[]{:S(2)}) collective-permute-start(bf16[64,1024]{1,0:T(8,128)(2,1)S(1)} %collective-permute-done.refs_1_), channel_id=1, source_target_pairs={{0,1},{1,2},{2,3},{3,4},{4,5},{5,6},{6,7},{7,0},{8,9},{9,10},{10,1... | collective-permute-start | bytes 393224 | tf_op jit(solution)/shard_map/ppermute | solution.py:289
  75.8 7.2 %collective-permute-start.10 = (bf16[64,1024]{1,0:T(8,128)(2,1)S(1)}, bf16[64,1024]{1,0:T(8,128)(2,1)S(1)}, u32[]{:S(2)}, u32[]{:S(2)}) collective-permute-start(bf16[64,1024]{1,0:T(8,128)(2,1)S(1)} %collective-permute-done.8.refs_10_), channel_id=1, source_target_pairs={{0,7},{1,0},{2,1},{3,2},{4,3},{5,4},{6,5},{7,6},{8,15},{9,8},{10,9... | collective-permute-start | bytes 393224 | tf_op jit(solution)/shard_map/ppermute | solution.py:289
  79.5 7.2 %collective-permute-start.3 = (bf16[64,1024]{1,0:T(8,128)(2,1)S(1)}, bf16[64,1024]{1,0:T(8,128)(2,1)S(1)}, u32[]{:S(2)}, u32[]{:S(2)}) collective-permute-start(bf16[64,1024]{1,0:T(8,128)(2,1)S(1)} %collective-permute-done.1.refs_2_), channel_id=1, source_target_pairs={{0,7},{1,0},{2,1},{3,2},{4,3},{5,4},{6,5},{7,6},{8,15},{9,8},{10,9... | collective-permute-start | bytes 393224 | tf_op jit(solution)/shard_map/ppermute | solution.py:289
  81.5 7.9 %collective-permute-start.9 = (bf16[64,1024]{1,0:T(8,128)(2,1)S(1)}, bf16[64,1024]{1,0:T(8,128)(2,1)S(1)}, u32[]{:S(2)}, u32[]{:S(2)}) collective-permute-start(bf16[64,1024]{1,0:T(8,128)(2,1)S(1)} %collective-permute-done.7.refs_9_), channel_id=1, source_target_pairs={{0,1},{1,2},{2,3},{3,4},{4,5},{5,6},{6,7},{7,0},{8,9},{9,10},{10,1... | collective-permute-start | bytes 393224 | tf_op jit(solution)/shard_map/ppermute | solution.py:289
  81.9 8.0 %collective-permute-start.4 = (bf16[64,1024]{1,0:T(8,128)(2,1)S(1)}, bf16[64,1024]{1,0:T(8,128)(2,1)S(1)}, u32[]{:S(2)}, u32[]{:S(2)}) collective-permute-start(bf16[64,1024]{1,0:T(8,128)(2,1)S(1)} %collective-permute-done.2.refs_3_), channel_id=1, source_target_pairs={{0,1},{1,2},{2,3},{3,4},{4,5},{5,6},{6,7},{7,0},{8,9},{9,10},{10,1... | collective-permute-start | bytes 393224 | tf_op jit(solution)/shard_map/ppermute | solution.py:289
  83.0 7.4 %collective-permute-start.12 = (bf16[64,1024]{1,0:T(8,128)(2,1)S(1)}, bf16[64,1024]{1,0:T(8,128)(2,1)S(1)}, u32[]{:S(2)}, u32[]{:S(2)}) collective-permute-start(bf16[64,1024]{1,0:T(8,128)(2,1)S(1)} %collective-permute-done.10.refs_12_), channel_id=1, source_target_pairs={{0,7},{1,0},{2,1},{3,2},{4,3},{5,4},{6,5},{7,6},{8,15},{9,8},{10,9... | collective-permute-start | bytes 393224 | tf_op jit(solution)/shard_map/ppermute | solution.py:289
  86.7 9.9 %collective-permute-start.5 = (bf16[64,1024]{1,0:T(8,128)(2,1)S(1)}, bf16[64,1024]{1,0:T(8,128)(2,1)S(1)}, u32[]{:S(2)}, u32[]{:S(2)}) collective-permute-start(bf16[64,1024]{1,0:T(8,128)(2,1)S(1)} %collective-permute-done.3.refs_4_), channel_id=1, source_target_pairs={{0,7},{1,0},{2,1},{3,2},{4,3},{5,4},{6,5},{7,6},{8,15},{9,8},{10,9... | collective-permute-start | bytes 393224 | tf_op jit(solution)/shard_map/ppermute | solution.py:289
  89.4 7.3 %collective-permute-start.11 = (bf16[64,1024]{1,0:T(8,128)(2,1)S(1)}, bf16[64,1024]{1,0:T(8,128)(2,1)S(1)}, u32[]{:S(2)}, u32[]{:S(2)}) collective-permute-start(bf16[64,1024]{1,0:T(8,128)(2,1)S(1)} %collective-permute-done.9.refs_11_), channel_id=1, source_target_pairs={{0,1},{1,2},{2,3},{3,4},{4,5},{5,6},{6,7},{7,0},{8,9},{9,10},{10,1... | collective-permute-start | bytes 393224 | tf_op jit(solution)/shard_map/ppermute | solution.py:289
  89.9 7.0 %collective-permute-start.6 = (bf16[64,1024]{1,0:T(8,128)(2,1)S(1)}, bf16[64,1024]{1,0:T(8,128)(2,1)S(1)}, u32[]{:S(2)}, u32[]{:S(2)}) collective-permute-start(bf16[64,1024]{1,0:T(8,128)(2,1)S(1)} %collective-permute-done.4.refs_5_), channel_id=1, source_target_pairs={{0,1},{1,2},{2,3},{3,4},{4,5},{5,6},{6,7},{7,0},{8,9},{9,10},{10,1... | collective-permute-start | bytes 393224 | tf_op jit(solution)/shard_map/ppermute | solution.py:289
  90.4 6.5 %collective-permute-start.13 = (bf16[64,1024]{1,0:T(8,128)(2,1)S(1)}, bf16[64,1024]{1,0:T(8,128)(2,1)S(1)}, u32[]{:S(2)}, u32[]{:S(2)}) collective-permute-start(bf16[64,1024]{1,0:T(8,128)(2,1)S(1)} %collective-permute-done.12.refs_14_), channel_id=1, source_target_pairs={{0,7},{1,0},{2,1},{3,2},{4,3},{5,4},{6,5},{7,6},{8,15},{9,8},{10,9... | collective-permute-start | bytes 393224 | tf_op jit(solution)/shard_map/ppermute | solution.py:289

commit v5 on v4

--- a/solution.py
+++ b/solution.py
@@ -1,3 +1,4 @@
+import functools
 import math
 
 import jax
@@ -139,23 +140,20 @@
                 )
             packed_ref[:, slot * 128 : (slot + 1) * 128] = rows_ref[slot].astype(BF)
 
-    def pair(step, carry):
+    for step in range(capacity // 2):
         for k in range(blocks):
             cols = slice(k * width, (k + 1) * width)
             rank, rows = rank_ref[k : k + 1, :], packed_ref[:, cols]
             for i in range(2):
-                live = jnp.where(rank == (2 * step + i).astype(F32), 1.0, 0.0).astype(BF)
+                live = jnp.where(rank == float(2 * step + i), 1.0, 0.0).astype(BF)
                 masked_ref[i * lanes : (i + 1) * lanes, cols] = rows * live
         total = lax.dot_general(
             hot_ref[...], masked_ref[...], (((1,), (1,)), ((), ())), preferred_element_type=F32
         )
         for i in range(2):
-            out_ref[:, pl.ds(2 * step + i, 1), :, :lanes] = (
-                total[:, i * lanes : (i + 1) * lanes].astype(BF).reshape(owners, 1, tiles, lanes)
+            out_ref[:, 2 * step + i, :, :lanes] = (
+                total[:, i * lanes : (i + 1) * lanes].astype(BF).reshape(owners, tiles, lanes)
             )
-        return carry
-
-    lax.fori_loop(0, capacity // 2, pair, 0)
 
 
 def gather_rows(hot, rank, weights, spectra):
@@ -165,7 +163,7 @@
     lanes = groups * headings
     return pl.pallas_call(
         row_kernel,
-        out_shape=jax.ShapeDtypeStruct((owners, capacity, tiles, lanes + nodes), BF),
+        out_shape=pltpu.VMEM((owners, capacity, tiles, lanes + nodes), BF),
         in_specs=[pl.BlockSpec(memory_space=pltpu.VMEM)] * 4,
         out_specs=pl.BlockSpec(memory_space=pltpu.VMEM),
         scratch_shapes=[
@@ -216,34 +214,48 @@
     )(slots)
 
 
-def history_kernel(basis_ref, *refs):
-    spectra_refs, out_ref = refs[:-1], refs[-1]
+def history_kernel(headings, basis_ref, *refs):
+    spectra_refs, (out_ref, held_ref, sem) = refs[:-3], refs[-3:]
     count = len(spectra_refs) // 2
     group = basis_ref.shape[1] // count
-    half = spectra_refs[0].shape[0] // group
-    heading = pl.program_id(0)
-    own = pl.ds(pl.multiple_of(lax.rem(heading, half) * group, group), group)
-    nodes = out_ref.shape[2]
-    cols = pl.ds(pl.multiple_of(pl.program_id(1) * nodes, nodes), nodes)
-    for part in range(2):
-
-        @pl.when(heading // half == part)
-        def _():
-            chunks = [r[own, cols] for r in spectra_refs[part * count : (part + 1) * count]]
+    half = headings // 2
+    pieces = sem.shape[1]
+    width = held_ref.shape[2] // pieces
+    copies = []
+    for heading in range(headings):
+        part, inner = divmod(heading, half)
+        rows = slice(inner * group, (inner + 1) * group)
+        for piece in range(pieces):
+            cols = slice(piece * width, (piece + 1) * width)
+            chunks = [r[rows, cols] for r in spectra_refs[part * count : (part + 1) * count]]
             spectra = jnp.concatenate(chunks, axis=0)
-            out_ref[0] = jnp.dot(basis_ref[...], spectra, preferred_element_type=F32).astype(BF)
+            held_ref[heading, :, cols] = jnp.dot(
+                basis_ref[...], spectra, preferred_element_type=F32
+            ).astype(BF)
+            window = pl.ds(piece * width, width)
+            copy = pltpu.make_async_copy(
+                held_ref.at[heading, :, window],
+                out_ref.at[heading, :, window],
+                sem.at[heading, piece],
+            )
+            copy.start()
+            copies.append(copy)
+    for copy in copies:
+        copy.wait()
 
 
 def histories(basis, chunks, headings):
     steps = basis.shape[0]
     nodes = chunks[0].shape[1]
-    cut = 2
-    return pl.pallas_call(
-        history_kernel,
-        grid=(headings, cut),
+    return pl.pallas_call(
+        functools.partial(history_kernel, headings),
         out_shape=jax.ShapeDtypeStruct((headings, steps, nodes), BF),
         in_specs=[pl.BlockSpec(memory_space=pltpu.VMEM)] * (1 + len(chunks)),
-        out_specs=pl.BlockSpec((1, steps, nodes // cut), lambda h, i: (h, 0, i)),
+        out_specs=pl.BlockSpec(memory_space=pl.ANY),
+        scratch_shapes=[
+            pltpu.VMEM((headings, steps, nodes), BF),
+            pltpu.SemaphoreType.DMA((headings, 2)),
+        ],
         compiler_params=pltpu.CompilerParams(vmem_limit_bytes=VMEM_LIMIT),
         cost_estimate=pl.CostEstimate(
             flops=2 * steps * basis.shape[1] * headings * nodes,
@@ -280,6 +292,13 @@
     tile_ids = panel_tile.reshape(windows, width)
     weights = patch_weight.reshape(windows * width, 128)
     slot_weight, rank, hot = gather_weights(tile_ids, weights, owners, capacity)
+    offsets = [0]
+    for step in range(1, windows // 2):
+        offsets += [-step, step]
+    sources = (window + jnp.asarray(offsets + [windows // 2], jnp.int32)) % windows
+    basis = window_basis(sources, window, TSTEPS // windows, owners, fl_count)
+    rank, basis = lax.optimization_barrier((rank, basis))
+
     sent = gather_rows(hot, rank, slot_weight, spectra)
     got = lax.all_to_all(sent, "freq", 0, 0, tiled=True)
     low, high = node_spectra(got.reshape(-1, got.shape[-1]))
@@ -288,7 +307,7 @@
         pairs = [(k, (k + distance) % windows) for k in range(windows)]
         return lax.ppermute(chunk, "node", pairs)
 
-    lows, highs, offsets = [low], [high], [0]
+    lows, highs = [low], [high]
     low_up = low_down = low
     high_up = high_down = high
     for step in range(1, windows // 2):
@@ -298,11 +317,7 @@
         low_down = shift(low_down, -1)
         lows += [low_up, low_down]
         highs += [high_up, high_down]
-        offsets += [-step, step]
     chunks = lows + [shift(low_up, 1)] + highs + [shift(high_down, -1)]
-    offsets = jnp.asarray(offsets + [windows // 2], jnp.int32)
-    sources = (window + offsets) % windows
-    basis = window_basis(sources, window, TSTEPS // windows, owners, fl_count)
     return histories(basis, chunks, headings)
 
 

time: 103 us -> 97.8 us (0.950)
  blocking collectives: 0 us -> 25.3 us
  waiting for transfers between devices: 39.2 us -> 19.7 us
  starting transfers between devices: 41 us -> 35.2 us
  Pallas kernels: 18.6 us -> 14 us
    all_to_all x0 -> x1, blocking collectives: none -> 25.3 us  [shards(): got = lax.all_to_all(sent, 'freq', 0, 0, tiled=True)]
    all_to_all x1 -> x0, waiting for transfers between devices: 20.2 us -> none  [shards(): got = lax.all_to_all(sent, 'freq', 0, 0, tiled=True)]
    all_to_all x1 -> x0, starting transfers between devices: 5.12 us -> none  [shards(): got = lax.all_to_all(sent, 'freq', 0, 0, tiled=True)]
    pallas_call x2, Pallas kernels: 9.65 us -> 5.04 us  [the longest x1 2.67 us: gather_rows(): pl.pallas_call(row_kernel, out_shape=pltpu.VMEM((owners, capacity, tiles,...]
    ppermute x14, waiting for transfers between devices: 4.33 us -> 7.86 us  [shift(): return lax.ppermute(chunk, 'node', pairs)]
    all_to_all x1, waiting for transfers between devices: 14.7 us -> 11.8 us  [shards(): lax.all_to_all(scaled.reshape(owners * windows, headings, width), ('freq'...]
  transfers between devices with their start and end apart: 16 -> 15, of which waited for: 9 -> 7; matrix products, arithmetic and copies ran while one was open for 3% -> 3% of each run, Pallas kernels for 6% -> 6%
where the time goes in v5:
time: 97.8 us; the launch traced here: 97.2 us
  starting transfers between devices  35.2 us (36%)
  blocking collectives  25.3 us (26%)
  waiting for transfers between devices  19.7 us (20%)
  Pallas kernels  14 us (14%)
  other arithmetic  2.57 us (3%)
    all_to_all x1, blocking collectives, shards(): got = lax.all_to_all(sent, 'freq', 0, 0, tiled=True)  25.3 us
    ppermute x14, starting transfers between devices, shift(): return lax.ppermute(chunk, 'node', pairs)  20.5 us
    all_to_all x1, starting transfers between devices, shards(): lax.all_to_all(scaled.reshape(owners * windows, headings, width), ('freq'...  14.7 us
    all_to_all x1, waiting for transfers between devices, shards(): lax.all_to_all(scaled.reshape(owners * windows, headings, width), ('freq'...  11.8 us
    ppermute x14, waiting for transfers between devices, shift(): return lax.ppermute(chunk, 'node', pairs)  7.86 us
    pallas_call x1, Pallas kernels, gather_weights(): pl.pallas_call(weight_kernel, out_shape=(jax.ShapeDtypeStruct((owners, ca...  5.76 us
    pallas_call x1, Pallas kernels, gather_rows(): pl.pallas_call(row_kernel, out_shape=pltpu.VMEM((owners, capacity, tiles,...  2.67 us
    convert_element_type x1, other arithmetic, window_basis(): jnp.where(is_re, jnp.cos(turn_angle), -jnp.sin(turn_angle)).astype(BF)  2.53 us
  transfers between devices with their start and end apart: 15, of which 7 were waited for; matrix products, arithmetic and copies ran while one was open for 3% of the time, Pallas kernels for 6%

profile of v5, /device:TPU:2, one launch (start us, length us, event | category | flops | bytes accessed | tf_op | source)
XLA Modules:
  0.0 97.2 jit_solution(10793699858159067234)
XLA Ops:
  0.0 0.0 copy-start.2
  0.0 0.0 copy-start.1
  0.0 0.0 copy-start
  0.0 2.3 %scale.1 = bf16[32,8,4,256]{3,2,1,0:T(4,128)(2,1)} custom-call(s32[1]{0:T(128)} %bitcast.1.group_ref, bf16[2,4,4,8192]{3,2,1,0:T(4,128)(2,1)} %pressure_ref.1, f32[4,128]{1,0:T(4,128)} %amp_ref.1, s32[4,128]{1,0:T(4,128)} %code_ref.1), custom_call_target="tpu_custom_call" | custom-call | flops 2000000 | bytes 1048576 | tf_op jit(solution)/shard_map/scale/pallas_call | solution.py:47
  2.3 14.7 %all-to-all-start = ((bf16[256,4,256]{2,1,0:T(4,128)(2,1)}), bf16[256,4,256]{2,1,0:T(4,128)(2,1)S(1)}, u32[]{:S(2)}, u32[]{:S(2)}) async-start(bf16[256,4,256]{2,1,0:T(4,128)(2,1)} %bitcast.12), calls=%async_computation | async-start | bytes 1048576 | tf_op jit(solution)/shard_map/all_to_all | solution.py:288
  17.0 0.0 copy-done.2
  17.1 0.1 broadcast_in_dim.14
  17.1 0.1 reshape.63
  17.2 0.1 mul.43
  17.3 0.0 copy-done.1
  17.3 0.0 copy-done
  17.3 5.8 %weight_slots.1 = (bf16[32,12,8,128]{3,2,1,0:T(8,128)(2,1)S(1)}, f32[8,256]{1,0:T(8,128)S(1)}, bf16[256,2048]{1,0:T(8,128)(2,1)S(1)}) custom-call(s32[8,256]{1,0:T(8,128)S(1)} %bitcast.10, bf16[2048,128]{1,0:T(8,128)(2,1)S(1)} %bitcast.11), custom_call_target="tpu_custom_call" | custom-call | flops 1610612736 | bytes 2097152 | tf_op jit(solution)/shard_map/weight_slots/pallas_call | solution.py:110
  23.1 2.5 %select_convert_fusion.basis_ref = bf16[512,256]{1,0:T(8,128)(2,1)S(1)} fusion(s32[512]{0:T(512)S(1)} %iota_add_fusion, s32[256]{0:T(256)S(1)} %multiply_add_fusion, pred[256]{0:T(512)(128)(4,1)S(1)} %broadcast_compare_fusion), kind=kLoop, calls=%fused_computation.8 | loop fusion | flops 2228224 | bytes 265472 | tf_op jit(solution)/shard_map/convert_element_type | solution.py:276
  25.6 11.8 %all-to-all-done = bf16[256,4,256]{2,1,0:T(4,128)(2,1)S(1)} async-done(((bf16[256,4,256]{2,1,0:T(4,128)(2,1)}), bf16[256,4,256]{2,1,0:T(4,128)(2,1)S(1)}, u32[]{:S(2)}, u32[]{:S(2)}) %all-to-all-start) | async-done | bytes 524320 | tf_op jit(solution)/shard_map/all_to_all | solution.py:288
  37.5 2.7 %row_slots.1 = bf16[32,12,8,256]{3,2,1,0:T(8,128)(2,1)S(1)} custom-call(bf16[256,2048]{1,0:T(8,128)(2,1)S(1)} %get-tuple-element.14.hot_ref, f32[8,256]{1,0:T(8,128)S(1)} %get-tuple-element.15.rank_ref, bf16[32,12,8,128]{3,2,1,0:T(8,128)(2,1)S(1)} %get-tuple-element.16.weight_ref, bf16[32,8,4,256]{3,2,1,0:T(4,128)(2,1)S(1)} %bitcast.9), custom_call_target="tpu_custom_call" | custom-call | flops 1610612736 | bytes 3145728 | tf_op jit(solution)/shard_map/row_slots/pallas_call | solution.py:164
  40.1 25.3 %all_to_all.10 = bf16[32,12,8,256]{3,2,1,0:T(8,128)(2,1)S(1)} all-to-all(bf16[32,12,8,256]{3,2,1,0:T(8,128)(2,1)S(1)} %row_slots.1), channel_id=1, replica_groups=mesh['freq'=32,'node'=8] {'freq'}, dimensions={0} | all-to-all | bytes 3145728 | tf_op jit(solution)/shard_map/all_to_all | solution.py:303
  65.4 0.8 node_spectra.1
  66.3 1.1 %collective-permute-start = (bf16[64,1024]{1,0:T(8,128)(2,1)S(1)}, bf16[64,1024]{1,0:T(8,128)(2,1)S(1)}, u32[]{:S(2)}, u32[]{:S(2)}) collective-permute-start(bf16[64,1024]{1,0:T(8,128)(2,1)S(1)} %get-tuple-element.17.refs_0_), channel_id=1, source_target_pairs={{0,1},{1,2},{2,3},{3,4},{4,5},{5,6},{6,7},{7,0},{8,9},{9,10},{10,1... | collective-permute-start | bytes 393224 | tf_op jit(solution)/shard_map/ppermute | solution.py:308
  67.3 2.2 %collective-permute-start.8 = (bf16[64,1024]{1,0:T(8,128)(2,1)S(1)}, bf16[64,1024]{1,0:T(8,128)(2,1)S(1)}, u32[]{:S(2)}, u32[]{:S(2)}) collective-permute-start(bf16[64,1024]{1,0:T(8,128)(2,1)S(1)} %get-tuple-element.18.refs_8_), channel_id=1, source_target_pairs={{0,7},{1,0},{2,1},{3,2},{4,3},{5,4},{6,5},{7,6},{8,15},{9,8},{10,9... | collective-permute-start | bytes 393224 | tf_op jit(solution)/shard_map/ppermute | solution.py:308
  69.6 0.0 collective-permute-start.1
  69.6 2.0 %collective-permute-start.7 = (bf16[64,1024]{1,0:T(8,128)(2,1)S(1)}, bf16[64,1024]{1,0:T(8,128)(2,1)S(1)}, u32[]{:S(2)}, u32[]{:S(2)}) collective-permute-start(bf16[64,1024]{1,0:T(8,128)(2,1)S(1)} %get-tuple-element.18.refs_8_), channel_id=1, source_target_pairs={{0,1},{1,2},{2,3},{3,4},{4,5},{5,6},{6,7},{7,0},{8,9},{9,10},{10,1... | collective-permute-start | bytes 393224 | tf_op jit(solution)/shard_map/ppermute | solution.py:308
  71.6 2.2 %collective-permute-done.refs_1_ = bf16[64,1024]{1,0:T(8,128)(2,1)S(1)} collective-permute-done((bf16[64,1024]{1,0:T(8,128)(2,1)S(1)}, bf16[64,1024]{1,0:T(8,128)(2,1)S(1)}, u32[]{:S(2)}, u32[]{:S(2)}) %collective-permute-start) | collective-permute-done | bytes 131104 | tf_op jit(solution)/shard_map/ppermute | solution.py:308
  73.8 0.0 collective-permute-start.2
  73.8 0.0 collective-permute-done.8.refs_10_
  73.8 3.4 %collective-permute-start.10 = (bf16[64,1024]{1,0:T(8,128)(2,1)S(1)}, bf16[64,1024]{1,0:T(8,128)(2,1)S(1)}, u32[]{:S(2)}, u32[]{:S(2)}) collective-permute-start(bf16[64,1024]{1,0:T(8,128)(2,1)S(1)} %collective-permute-done.8.refs_10_), channel_id=1, source_target_pairs={{0,7},{1,0},{2,1},{3,2},{4,3},{5,4},{6,5},{7,6},{8,15},{9,8},{10,9... | collective-permute-start | bytes 393224 | tf_op jit(solution)/shard_map/ppermute | solution.py:308
  77.2 0.0 collective-permute-done.1.refs_2_
  77.2 2.3 %collective-permute-start.3 = (bf16[64,1024]{1,0:T(8,128)(2,1)S(1)}, bf16[64,1024]{1,0:T(8,128)(2,1)S(1)}, u32[]{:S(2)}, u32[]{:S(2)}) collective-permute-start(bf16[64,1024]{1,0:T(8,128)(2,1)S(1)} %collective-permute-done.1.refs_2_), channel_id=1, source_target_pairs={{0,7},{1,0},{2,1},{3,2},{4,3},{5,4},{6,5},{7,6},{8,15},{9,8},{10,9... | collective-permute-start | bytes 393224 | tf_op jit(solution)/shard_map/ppermute | solution.py:308
  79.4 0.0 collective-permute-done.7.refs_9_
  79.4 0.0 collective-permute-start.9
  79.4 0.7 collective-permute-done.2.refs_3_
  80.2 0.0 collective-permute-start.4
  80.2 0.0 collective-permute-done.10.refs_12_
  80.2 3.7 %collective-permute-start.12 = (bf16[64,1024]{1,0:T(8,128)(2,1)S(1)}, bf16[64,1024]{1,0:T(8,128)(2,1)S(1)}, u32[]{:S(2)}, u32[]{:S(2)}) collective-permute-start(bf16[64,1024]{1,0:T(8,128)(2,1)S(1)} %collective-permute-done.10.refs_12_), channel_id=1, source_target_pairs={{0,7},{1,0},{2,1},{3,2},{4,3},{5,4},{6,5},{7,6},{8,15},{9,8},{10,9... | collective-permute-start | bytes 393224 | tf_op jit(solution)/shard_map/ppermute | solution.py:308
  83.8 0.0 collective-permute-done.3.refs_4_
  83.8 2.6 %collective-permute-start.5 = (bf16[64,1024]{1,0:T(8,128)(2,1)S(1)}, bf16[64,1024]{1,0:T(8,128)(2,1)S(1)}, u32[]{:S(2)}, u32[]{:S(2)}) collective-permute-start(bf16[64,1024]{1,0:T(8,128)(2,1)S(1)} %collective-permute-done.3.refs_4_), channel_id=1, source_target_pairs={{0,7},{1,0},{2,1},{3,2},{4,3},{5,4},{6,5},{7,6},{8,15},{9,8},{10,9... | collective-permute-start | bytes 393224 | tf_op jit(solution)/shard_map/ppermute | solution.py:308
  86.5 0.3 collective-permute-done.9.refs_11_
  86.8 0.0 collective-permute-start.11
  86.8 1.4 %collective-permute-done.4.refs_5_ = bf16[64,1024]{1,0:T(8,128)(2,1)S(1)} collective-permute-done((bf16[64,1024]{1,0:T(8,128)(2,1)S(1)}, bf16[64,1024]{1,0:T(8,128)(2,1)S(1)}, u32[]{:S(2)}, u32[]{:S(2)}) %collective-permute-start.4) | collective-permute-done | bytes 131104 | tf_op jit(solution)/shard_map/ppermute | solution.py:308
  88.2 0.0 collective-permute-start.6
  88.2 0.0 collective-permute-done.12.refs_14_
  88.2 3.2 %collective-permute-start.13 = (bf16[64,1024]{1,0:T(8,128)(2,1)S(1)}, bf16[64,1024]{1,0:T(8,128)(2,1)S(1)}, u32[]{:S(2)}, u32[]{:S(2)}) collective-permute-start(bf16[64,1024]{1,0:T(8,128)(2,1)S(1)} %collective-permute-done.12.refs_14_), channel_id=1, source_target_pairs={{0,7},{1,0},{2,1},{3,2},{4,3},{5,4},{6,5},{7,6},{8,15},{9,8},{10,9... | collective-permute-start | bytes 393224 | tf_op jit(solution)/shard_map/ppermute | solution.py:308
  91.4 0.0 collective-permute-done.5.refs_6_
  91.4 1.8 %collective-permute-done.11.refs_13_ = bf16[64,1024]{1,0:T(8,128)(2,1)S(1)} collective-permute-done((bf16[64,1024]{1,0:T(8,128)(2,1)S(1)}, bf16[64,1024]{1,0:T(8,128)(2,1)S(1)}, u32[]{:S(2)}, u32[]{:S(2)}) %collective-permute-start.11) | collective-permute-done | bytes 131104 | tf_op jit(solution)/shard_map/ppermute | solution.py:308
  93.2 1.4 %collective-permute-done.6.refs_7_ = bf16[64,1024]{1,0:T(8,128)(2,1)S(1)} collective-permute-done((bf16[64,1024]{1,0:T(8,128)(2,1)S(1)}, bf16[64,1024]{1,0:T(8,128)(2,1)S(1)}, u32[]{:S(2)}, u32[]{:S(2)}) %collective-permute-start.6) | collective-permute-done | bytes 131104 | tf_op jit(solution)/shard_map/ppermute | solution.py:308
  94.6 0.0 collective-permute-done.13.refs_15_
  94.7 2.4 %histories.1 = bf16[4,512,1024]{2,1,0:T(8,128)(2,1)} custom-call(bf16[512,256]{1,0:T(8,128)(2,1)S(1)} %select_convert_fusion.basis_ref, bf16[64,1024]{1,0:T(8,128)(2,1)S(1)} %get-tuple-element.17.refs_0_, bf16[64,1024]{1,0:T(8,128)(2,1)S(1)} %collective-permute-done.refs_1_, bf16[64,1024]{1,0:T(8,128)(2,1)S(1)} %collective-permute-done.1.refs_2_, ...), custom_call_target="tpu_custom_call" | custom-call | flops 1073741824 | bytes 6291456 | tf_op jit(solution)/shard_map/histories/pallas_call | solution.py:250
  (6 shorter events, 0.0 us)
Async XLA Ops:
  0.0 17.0 %copy-start.2 = (s32[8]{0:T(128)S(1)}, s32[8]{0:T(128)}, u32[]{:S(2)}) copy-start(s32[8]{0:T(128)} %constant.63.clone) | copy-start | bytes 100
  0.0 17.3 %copy-start.1 = (s32[1,8,256,1]{2,3,1,0:T(1,128)S(1)}, s32[1,8,256,1]{2,3,1,0:T(1,128)}, u32[]{:S(2)}) copy-start(s32[1,8,256,1]{2,3,1,0:T(1,128)} %param.9) | copy-start | bytes 24580
  0.0 17.3 %copy-start = (bf16[1,8,256,128]{3,2,1,0:T(8,128)(2,1)S(1)}, bf16[1,8,256,128]{3,2,1,0:T(8,128)(2,1)}, u32[]{:S(2)}) copy-start(bf16[1,8,256,128]{3,2,1,0:T(8,128)(2,1)} %param.10) | copy-start | bytes 1572868
  2.3 35.1 %all-to-all-start = ((bf16[256,4,256]{2,1,0:T(4,128)(2,1)}), bf16[256,4,256]{2,1,0:T(4,128)(2,1)S(1)}, u32[]{:S(2)}, u32[]{:S(2)}) async-start(bf16[256,4,256]{2,1,0:T(4,128)(2,1)} %bitcast.12), calls=%async_computation | async-start | bytes 1048576 | tf_op jit(solution)/shard_map/all_to_all | solution.py:288
  66.3 7.5 %collective-permute-start = (bf16[64,1024]{1,0:T(8,128)(2,1)S(1)}, bf16[64,1024]{1,0:T(8,128)(2,1)S(1)}, u32[]{:S(2)}, u32[]{:S(2)}) collective-permute-start(bf16[64,1024]{1,0:T(8,128)(2,1)S(1)} %get-tuple-element.17.refs_0_), channel_id=1, source_target_pairs={{0,1},{1,2},{2,3},{3,4},{4,5},{5,6},{6,7},{7,0},{8,9},{9,10},{10,1... | collective-permute-start | bytes 393224 | tf_op jit(solution)/shard_map/ppermute | solution.py:308
  67.3 6.5 %collective-permute-start.8 = (bf16[64,1024]{1,0:T(8,128)(2,1)S(1)}, bf16[64,1024]{1,0:T(8,128)(2,1)S(1)}, u32[]{:S(2)}, u32[]{:S(2)}) collective-permute-start(bf16[64,1024]{1,0:T(8,128)(2,1)S(1)} %get-tuple-element.18.refs_8_), channel_id=1, source_target_pairs={{0,7},{1,0},{2,1},{3,2},{4,3},{5,4},{6,5},{7,6},{8,15},{9,8},{10,9... | collective-permute-start | bytes 393224 | tf_op jit(solution)/shard_map/ppermute | solution.py:308
  69.6 7.6 %collective-permute-start.1 = (bf16[64,1024]{1,0:T(8,128)(2,1)S(1)}, bf16[64,1024]{1,0:T(8,128)(2,1)S(1)}, u32[]{:S(2)}, u32[]{:S(2)}) collective-permute-start(bf16[64,1024]{1,0:T(8,128)(2,1)S(1)} %get-tuple-element.17.refs_0_), channel_id=1, source_target_pairs={{0,7},{1,0},{2,1},{3,2},{4,3},{5,4},{6,5},{7,6},{8,15},{9,8},{10,9... | collective-permute-start | bytes 393224 | tf_op jit(solution)/shard_map/ppermute | solution.py:308
  69.6 9.8 %collective-permute-start.7 = (bf16[64,1024]{1,0:T(8,128)(2,1)S(1)}, bf16[64,1024]{1,0:T(8,128)(2,1)S(1)}, u32[]{:S(2)}, u32[]{:S(2)}) collective-permute-start(bf16[64,1024]{1,0:T(8,128)(2,1)S(1)} %get-tuple-element.18.refs_8_), channel_id=1, source_target_pairs={{0,1},{1,2},{2,3},{3,4},{4,5},{5,6},{6,7},{7,0},{8,9},{9,10},{10,1... | collective-permute-start | bytes 393224 | tf_op jit(solution)/shard_map/ppermute | solution.py:308
  73.8 6.4 %collective-permute-start.2 = (bf16[64,1024]{1,0:T(8,128)(2,1)S(1)}, bf16[64,1024]{1,0:T(8,128)(2,1)S(1)}, u32[]{:S(2)}, u32[]{:S(2)}) collective-permute-start(bf16[64,1024]{1,0:T(8,128)(2,1)S(1)} %collective-permute-done.refs_1_), channel_id=1, source_target_pairs={{0,1},{1,2},{2,3},{3,4},{4,5},{5,6},{6,7},{7,0},{8,9},{9,10},{10,1... | collective-permute-start | bytes 393224 | tf_op jit(solution)/shard_map/ppermute | solution.py:308
  73.8 6.4 %collective-permute-start.10 = (bf16[64,1024]{1,0:T(8,128)(2,1)S(1)}, bf16[64,1024]{1,0:T(8,128)(2,1)S(1)}, u32[]{:S(2)}, u32[]{:S(2)}) collective-permute-start(bf16[64,1024]{1,0:T(8,128)(2,1)S(1)} %collective-permute-done.8.refs_10_), channel_id=1, source_target_pairs={{0,7},{1,0},{2,1},{3,2},{4,3},{5,4},{6,5},{7,6},{8,15},{9,8},{10,9... | collective-permute-start | bytes 393224 | tf_op jit(solution)/shard_map/ppermute | solution.py:308
  77.2 6.7 %collective-permute-start.3 = (bf16[64,1024]{1,0:T(8,128)(2,1)S(1)}, bf16[64,1024]{1,0:T(8,128)(2,1)S(1)}, u32[]{:S(2)}, u32[]{:S(2)}) collective-permute-start(bf16[64,1024]{1,0:T(8,128)(2,1)S(1)} %collective-permute-done.1.refs_2_), channel_id=1, source_target_pairs={{0,7},{1,0},{2,1},{3,2},{4,3},{5,4},{6,5},{7,6},{8,15},{9,8},{10,9... | collective-permute-start | bytes 393224 | tf_op jit(solution)/shard_map/ppermute | solution.py:308
  79.4 7.3 %collective-permute-start.9 = (bf16[64,1024]{1,0:T(8,128)(2,1)S(1)}, bf16[64,1024]{1,0:T(8,128)(2,1)S(1)}, u32[]{:S(2)}, u32[]{:S(2)}) collective-permute-start(bf16[64,1024]{1,0:T(8,128)(2,1)S(1)} %collective-permute-done.7.refs_9_), channel_id=1, source_target_pairs={{0,1},{1,2},{2,3},{3,4},{4,5},{5,6},{6,7},{7,0},{8,9},{9,10},{10,1... | collective-permute-start | bytes 393224 | tf_op jit(solution)/shard_map/ppermute | solution.py:308
  80.2 8.0 %collective-permute-start.4 = (bf16[64,1024]{1,0:T(8,128)(2,1)S(1)}, bf16[64,1024]{1,0:T(8,128)(2,1)S(1)}, u32[]{:S(2)}, u32[]{:S(2)}) collective-permute-start(bf16[64,1024]{1,0:T(8,128)(2,1)S(1)} %collective-permute-done.2.refs_3_), channel_id=1, source_target_pairs={{0,1},{1,2},{2,3},{3,4},{4,5},{5,6},{6,7},{7,0},{8,9},{9,10},{10,1... | collective-permute-start | bytes 393224 | tf_op jit(solution)/shard_map/ppermute | solution.py:308
  80.2 8.0 %collective-permute-start.12 = (bf16[64,1024]{1,0:T(8,128)(2,1)S(1)}, bf16[64,1024]{1,0:T(8,128)(2,1)S(1)}, u32[]{:S(2)}, u32[]{:S(2)}) collective-permute-start(bf16[64,1024]{1,0:T(8,128)(2,1)S(1)} %collective-permute-done.10.refs_12_), channel_id=1, source_target_pairs={{0,7},{1,0},{2,1},{3,2},{4,3},{5,4},{6,5},{7,6},{8,15},{9,8},{10,9... | collective-permute-start | bytes 393224 | tf_op jit(solution)/shard_map/ppermute | solution.py:308
  83.8 7.6 %collective-permute-start.5 = (bf16[64,1024]{1,0:T(8,128)(2,1)S(1)}, bf16[64,1024]{1,0:T(8,128)(2,1)S(1)}, u32[]{:S(2)}, u32[]{:S(2)}) collective-permute-start(bf16[64,1024]{1,0:T(8,128)(2,1)S(1)} %collective-permute-done.3.refs_4_), channel_id=1, source_target_pairs={{0,7},{1,0},{2,1},{3,2},{4,3},{5,4},{6,5},{7,6},{8,15},{9,8},{10,9... | collective-permute-start | bytes 393224 | tf_op jit(solution)/shard_map/ppermute | solution.py:308
  86.8 6.5 %collective-permute-start.11 = (bf16[64,1024]{1,0:T(8,128)(2,1)S(1)}, bf16[64,1024]{1,0:T(8,128)(2,1)S(1)}, u32[]{:S(2)}, u32[]{:S(2)}) collective-permute-start(bf16[64,1024]{1,0:T(8,128)(2,1)S(1)} %collective-permute-done.9.refs_11_), channel_id=1, source_target_pairs={{0,1},{1,2},{2,3},{3,4},{4,5},{5,6},{6,7},{7,0},{8,9},{9,10},{10,1... | collective-permute-start | bytes 393224 | tf_op jit(solution)/shard_map/ppermute | solution.py:308
  88.2 6.5 %collective-permute-start.6 = (bf16[64,1024]{1,0:T(8,128)(2,1)S(1)}, bf16[64,1024]{1,0:T(8,128)(2,1)S(1)}, u32[]{:S(2)}, u32[]{:S(2)}) collective-permute-start(bf16[64,1024]{1,0:T(8,128)(2,1)S(1)} %collective-permute-done.4.refs_5_), channel_id=1, source_target_pairs={{0,1},{1,2},{2,3},{3,4},{4,5},{5,6},{6,7},{7,0},{8,9},{9,10},{10,1... | collective-permute-start | bytes 393224 | tf_op jit(solution)/shard_map/ppermute | solution.py:308
  88.2 6.5 %collective-permute-start.13 = (bf16[64,1024]{1,0:T(8,128)(2,1)S(1)}, bf16[64,1024]{1,0:T(8,128)(2,1)S(1)}, u32[]{:S(2)}, u32[]{:S(2)}) collective-permute-start(bf16[64,1024]{1,0:T(8,128)(2,1)S(1)} %collective-permute-done.12.refs_14_), channel_id=1, source_target_pairs={{0,7},{1,0},{2,1},{3,2},{4,3},{5,4},{6,5},{7,6},{8,15},{9,8},{10,9... | collective-permute-start | bytes 393224 | tf_op jit(solution)/shard_map/ppermute | solution.py:308

commit v6 on v5

--- a/solution.py
+++ b/solution.py
@@ -18,13 +18,29 @@
 VMEM_LIMIT = 20 << 20
 
 
-def scale_kernel(group_ref, pressure_ref, amp_ref, code_ref, out_ref):
-    owners, width = out_ref.shape[0], out_ref.shape[3]
+def scale_kernel(
+    group_ref, pressure_hbm, amp_hbm, code_hbm, out_hbm,
+    pressure_ref, amp_ref, code_ref, held_ref, table_sem, in_sem, out_sem,
+):
+    owners, width = held_ref.shape[1], held_ref.shape[3]
     fl_count = pressure_ref.shape[1]
+    tables = [
+        pltpu.make_async_copy(amp_hbm, amp_ref, table_sem.at[0]),
+        pltpu.make_async_copy(code_hbm, code_ref, table_sem.at[1]),
+    ]
+    arriving = [
+        pltpu.make_async_copy(pressure_hbm.at[:, fl], pressure_ref.at[:, fl], in_sem.at[fl])
+        for fl in range(fl_count)
+    ]
+    for copy in tables + arriving:
+        copy.start()
+    for copy in tables:
+        copy.wait()
     lane = lax.broadcasted_iota(jnp.int32, amp_ref.shape, 1)
     angle = code_ref[...].astype(F32) * (2.0 * math.pi / PHASE_LEVELS)
     cosine, sine = jnp.cos(angle), jnp.sin(angle)
     amp = amp_ref[...]
+    leaving = []
     for fl in range(fl_count):
         chosen = lane == group_ref[0] * fl_count + fl
 
@@ -32,28 +48,39 @@
             return jnp.sum(jnp.where(chosen, table, 0.0), axis=1, keepdims=True)
 
         a, c, s = pick(amp), pick(cosine), pick(sine)
-
+        arriving[fl].wait()
         for g in range(owners):
             cols = pl.ds(g * width, width)
             re = pressure_ref[0, fl, :, cols].astype(F32)
             im = pressure_ref[1, fl, :, cols].astype(F32)
-            out_ref[g, fl] = (a * (re * c - im * s)).astype(BF)
-            out_ref[g, fl_count + fl] = (a * (re * s + im * c)).astype(BF)
+            held_ref[fl, g] = (a * (re * c - im * s)).astype(BF)
+            held_ref[fl_count + fl, g] = (a * (re * s + im * c)).astype(BF)
+        for row in (fl, fl_count + fl):
+            copy = pltpu.make_async_copy(held_ref.at[row], out_hbm.at[row], out_sem.at[row])
+            copy.start()
+            leaving.append(copy)
+    for copy in leaving:
+        copy.wait()
 
 
 def scale_spectra(pressure, spectrum_amp, phase_code, group, owners):
     parts, fl_count, headings, panels = pressure.shape
-    width = panels // owners
+    shape = (parts * fl_count, owners, headings, panels // owners)
     return pl.pallas_call(
         scale_kernel,
-        out_shape=jax.ShapeDtypeStruct((owners, parts * fl_count, headings, width), BF),
-        in_specs=[
-            pl.BlockSpec(memory_space=pltpu.SMEM),
-            pl.BlockSpec(memory_space=pltpu.VMEM),
-            pl.BlockSpec(memory_space=pltpu.VMEM),
-            pl.BlockSpec(memory_space=pltpu.VMEM),
+        out_shape=jax.ShapeDtypeStruct(shape, BF),
+        in_specs=[pl.BlockSpec(memory_space=pltpu.SMEM)]
+        + [pl.BlockSpec(memory_space=pltpu.HBM)] * 3,
+        out_specs=pl.BlockSpec(memory_space=pl.ANY),
+        scratch_shapes=[
+            pltpu.VMEM(pressure.shape, BF),
+            pltpu.VMEM(spectrum_amp.shape, F32),
+            pltpu.VMEM(phase_code.shape, jnp.int32),
+            pltpu.VMEM(shape, BF),
+            pltpu.SemaphoreType.DMA((2,)),
+            pltpu.SemaphoreType.DMA((fl_count,)),
+            pltpu.SemaphoreType.DMA((parts * fl_count,)),
         ],
-        out_specs=pl.BlockSpec(memory_space=pltpu.VMEM),
         cost_estimate=pl.CostEstimate(flops=2_000_000, bytes_accessed=1 << 20, transcendentals=0),
         name="scale",
     )(group.reshape(1), pressure, spectrum_amp, phase_code)
@@ -126,7 +153,7 @@
 
 
 def row_kernel(hot_ref, rank_ref, weight_ref, spectra_ref, out_ref, rows_ref, packed_ref, masked_ref):
-    groups, blocks, headings, width = spectra_ref.shape
+    blocks, groups, headings, width = spectra_ref.shape
     owners, capacity, tiles, _ = out_ref.shape
     lanes = groups * headings
     parts = width // 128
@@ -136,7 +163,7 @@
             slot = k * parts + part
             for g in range(groups):
                 rows_ref[slot, pl.ds(g, headings, stride=groups), :] = (
-                    spectra_ref[g, k, :, part * 128 : (part + 1) * 128].astype(F32)
+                    spectra_ref[k, g, :, part * 128 : (part + 1) * 128].astype(F32)
                 )
             packed_ref[:, slot * 128 : (slot + 1) * 128] = rows_ref[slot].astype(BF)
 
@@ -158,7 +185,7 @@
 
 def gather_rows(hot, rank, weights, spectra):
     blocks, width = rank.shape
-    groups, _, headings, _ = spectra.shape
+    _, groups, headings, _ = spectra.shape
     owners, capacity, tiles, nodes = weights.shape
     lanes = groups * headings
     return pl.pallas_call(
@@ -286,8 +313,8 @@
     capacity = 12
     scaled = scale_spectra(pressure, spectrum_amp, phase_code, group, owners)
     spectra = lax.all_to_all(
-        scaled.reshape(owners * windows, headings, width), ("freq", "node"), 0, 0, tiled=True
-    ).reshape(owners, windows, headings, width)
+        scaled.reshape(windows * owners, headings, width), ("node", "freq"), 0, 0, tiled=True
+    ).reshape(windows, owners, headings, width)
 
     tile_ids = panel_tile.reshape(windows, width)
     weights = patch_weight.reshape(windows * width, 128)

time: 97.8 us -> 97.6 us (level)
  no operation moved by 1% of the time
where the time goes in v6:
time: 97.6 us; the launch traced here: 97 us
  starting transfers between devices  35.2 us (36%)
  blocking collectives  25.6 us (26%)
  waiting for transfers between devices  19.3 us (20%)
  Pallas kernels  13.8 us (14%)
  other arithmetic  2.57 us (3%)
    all_to_all x1, blocking collectives, shards(): got = lax.all_to_all(sent, 'freq', 0, 0, tiled=True)  25.6 us
    ppermute x14, starting transfers between devices, shift(): return lax.ppermute(chunk, 'node', pairs)  20.5 us
    all_to_all x1, starting transfers between devices, shards(): lax.all_to_all(scaled.reshape(windows * owners, headings, width), ('node'...  14.7 us
    all_to_all x1, waiting for transfers between devices, shards(): lax.all_to_all(scaled.reshape(windows * owners, headings, width), ('node'...  11.5 us
    ppermute x14, waiting for transfers between devices, shift(): return lax.ppermute(chunk, 'node', pairs)  7.86 us
    pallas_call x1, Pallas kernels, gather_weights(): pl.pallas_call(weight_kernel, out_shape=(jax.ShapeDtypeStruct((owners, ca...  5.76 us
    pallas_call x1, Pallas kernels, gather_rows(): pl.pallas_call(row_kernel, out_shape=pltpu.VMEM((owners, capacity, tiles,...  2.62 us
    convert_element_type x1, other arithmetic, window_basis(): jnp.where(is_re, jnp.cos(turn_angle), -jnp.sin(turn_angle)).astype(BF)  2.53 us
  transfers between devices with their start and end apart: 15, of which 7 were waited for; matrix products, arithmetic and copies ran while one was open for 3% of the time, Pallas kernels for 6%

profile of v6, /device:TPU:2, one launch (start us, length us, event | category | flops | bytes accessed | tf_op | source)
XLA Modules:
  0.0 97.0 jit_solution(10324494552357338527)
XLA Ops:
  0.0 0.0 copy-start.2
  0.0 0.0 copy-start.1
  0.0 0.0 copy-start
  0.0 2.2 %scale.1 = bf16[8,32,4,256]{3,2,1,0:T(4,128)(2,1)} custom-call(s32[1]{0:T(128)} %bitcast.1.group_ref, bf16[2,4,4,8192]{3,2,1,0:T(4,128)(2,1)} %pressure_hbm.1, f32[4,128]{1,0:T(4,128)} %amp_hbm.1, s32[4,128]{1,0:T(4,128)} %code_hbm.1), custom_call_target="tpu_custom_call" | custom-call | flops 2000000 | bytes 1048576 | tf_op jit(solution)/shard_map/scale/pallas_call | solution.py:69
  2.2 14.7 %all-to-all-start = ((bf16[256,4,256]{2,1,0:T(4,128)(2,1)}), bf16[256,4,256]{2,1,0:T(4,128)(2,1)S(1)}, u32[]{:S(2)}, u32[]{:S(2)}) async-start(bf16[256,4,256]{2,1,0:T(4,128)(2,1)} %bitcast.12), calls=%async_computation | async-start | bytes 1048576 | tf_op jit(solution)/shard_map/all_to_all | solution.py:315
  16.9 0.0 copy-done.2
  16.9 0.1 broadcast_in_dim.14
  17.0 0.1 reshape.63
  17.1 0.1 mul.43
  17.1 0.0 copy-done.1
  17.2 0.0 copy-done
  17.2 5.8 %weight_slots.1 = (bf16[32,12,8,128]{3,2,1,0:T(8,128)(2,1)S(1)}, f32[8,256]{1,0:T(8,128)S(1)}, bf16[256,2048]{1,0:T(8,128)(2,1)S(1)}) custom-call(s32[8,256]{1,0:T(8,128)S(1)} %bitcast.10, bf16[2048,128]{1,0:T(8,128)(2,1)S(1)} %bitcast.11), custom_call_target="tpu_custom_call" | custom-call | flops 1610612736 | bytes 2097152 | tf_op jit(solution)/shard_map/weight_slots/pallas_call | solution.py:137
  23.0 2.5 %select_convert_fusion.basis_ref = bf16[512,256]{1,0:T(8,128)(2,1)S(1)} fusion(s32[512]{0:T(512)S(1)} %iota_add_fusion, s32[256]{0:T(256)S(1)} %multiply_add_fusion, pred[256]{0:T(512)(128)(4,1)S(1)} %broadcast_compare_fusion), kind=kLoop, calls=%fused_computation.8 | loop fusion | flops 2228224 | bytes 265472 | tf_op jit(solution)/shard_map/convert_element_type | solution.py:303
  25.5 11.5 %all-to-all-done = bf16[256,4,256]{2,1,0:T(4,128)(2,1)S(1)} async-done(((bf16[256,4,256]{2,1,0:T(4,128)(2,1)}), bf16[256,4,256]{2,1,0:T(4,128)(2,1)S(1)}, u32[]{:S(2)}, u32[]{:S(2)}) %all-to-all-start) | async-done | bytes 524320 | tf_op jit(solution)/shard_map/all_to_all | solution.py:315
  36.9 2.6 %row_slots.1 = bf16[32,12,8,256]{3,2,1,0:T(8,128)(2,1)S(1)} custom-call(bf16[256,2048]{1,0:T(8,128)(2,1)S(1)} %get-tuple-element.14.hot_ref, f32[8,256]{1,0:T(8,128)S(1)} %get-tuple-element.15.rank_ref, bf16[32,12,8,128]{3,2,1,0:T(8,128)(2,1)S(1)} %get-tuple-element.16.weight_ref, bf16[8,32,4,256]{3,2,1,0:T(4,128)(2,1)S(1)} %bitcast.9), custom_call_target="tpu_custom_call" | custom-call | flops 1610612736 | bytes 3145728 | tf_op jit(solution)/shard_map/row_slots/pallas_call | solution.py:191
  39.6 25.6 %all_to_all.10 = bf16[32,12,8,256]{3,2,1,0:T(8,128)(2,1)S(1)} all-to-all(bf16[32,12,8,256]{3,2,1,0:T(8,128)(2,1)S(1)} %row_slots.1), channel_id=1, replica_groups=mesh['freq'=32,'node'=8] {'freq'}, dimensions={0} | all-to-all | bytes 3145728 | tf_op jit(solution)/shard_map/all_to_all | solution.py:330
  65.2 0.8 node_spectra.1
  66.0 1.1 %collective-permute-start = (bf16[64,1024]{1,0:T(8,128)(2,1)S(1)}, bf16[64,1024]{1,0:T(8,128)(2,1)S(1)}, u32[]{:S(2)}, u32[]{:S(2)}) collective-permute-start(bf16[64,1024]{1,0:T(8,128)(2,1)S(1)} %get-tuple-element.17.refs_0_), channel_id=1, source_target_pairs={{0,1},{1,2},{2,3},{3,4},{4,5},{5,6},{6,7},{7,0},{8,9},{9,10},{10,1... | collective-permute-start | bytes 393224 | tf_op jit(solution)/shard_map/ppermute | solution.py:335
  67.2 2.2 %collective-permute-start.8 = (bf16[64,1024]{1,0:T(8,128)(2,1)S(1)}, bf16[64,1024]{1,0:T(8,128)(2,1)S(1)}, u32[]{:S(2)}, u32[]{:S(2)}) collective-permute-start(bf16[64,1024]{1,0:T(8,128)(2,1)S(1)} %get-tuple-element.18.refs_8_), channel_id=1, source_target_pairs={{0,7},{1,0},{2,1},{3,2},{4,3},{5,4},{6,5},{7,6},{8,15},{9,8},{10,9... | collective-permute-start | bytes 393224 | tf_op jit(solution)/shard_map/ppermute | solution.py:335
  69.3 0.0 collective-permute-start.1
  69.4 2.0 %collective-permute-start.7 = (bf16[64,1024]{1,0:T(8,128)(2,1)S(1)}, bf16[64,1024]{1,0:T(8,128)(2,1)S(1)}, u32[]{:S(2)}, u32[]{:S(2)}) collective-permute-start(bf16[64,1024]{1,0:T(8,128)(2,1)S(1)} %get-tuple-element.18.refs_8_), channel_id=1, source_target_pairs={{0,1},{1,2},{2,3},{3,4},{4,5},{5,6},{6,7},{7,0},{8,9},{9,10},{10,1... | collective-permute-start | bytes 393224 | tf_op jit(solution)/shard_map/ppermute | solution.py:335
  71.4 2.2 %collective-permute-done.refs_1_ = bf16[64,1024]{1,0:T(8,128)(2,1)S(1)} collective-permute-done((bf16[64,1024]{1,0:T(8,128)(2,1)S(1)}, bf16[64,1024]{1,0:T(8,128)(2,1)S(1)}, u32[]{:S(2)}, u32[]{:S(2)}) %collective-permute-start) | collective-permute-done | bytes 131104 | tf_op jit(solution)/shard_map/ppermute | solution.py:335
  73.6 0.0 collective-permute-start.2
  73.6 0.0 collective-permute-done.8.refs_10_
  73.6 3.4 %collective-permute-start.10 = (bf16[64,1024]{1,0:T(8,128)(2,1)S(1)}, bf16[64,1024]{1,0:T(8,128)(2,1)S(1)}, u32[]{:S(2)}, u32[]{:S(2)}) collective-permute-start(bf16[64,1024]{1,0:T(8,128)(2,1)S(1)} %collective-permute-done.8.refs_10_), channel_id=1, source_target_pairs={{0,7},{1,0},{2,1},{3,2},{4,3},{5,4},{6,5},{7,6},{8,15},{9,8},{10,9... | collective-permute-start | bytes 393224 | tf_op jit(solution)/shard_map/ppermute | solution.py:335
  76.9 0.0 collective-permute-done.1.refs_2_
  76.9 2.3 %collective-permute-start.3 = (bf16[64,1024]{1,0:T(8,128)(2,1)S(1)}, bf16[64,1024]{1,0:T(8,128)(2,1)S(1)}, u32[]{:S(2)}, u32[]{:S(2)}) collective-permute-start(bf16[64,1024]{1,0:T(8,128)(2,1)S(1)} %collective-permute-done.1.refs_2_), channel_id=1, source_target_pairs={{0,7},{1,0},{2,1},{3,2},{4,3},{5,4},{6,5},{7,6},{8,15},{9,8},{10,9... | collective-permute-start | bytes 393224 | tf_op jit(solution)/shard_map/ppermute | solution.py:335
  79.2 0.0 collective-permute-done.7.refs_9_
  79.2 0.0 collective-permute-start.9
  79.2 0.7 collective-permute-done.2.refs_3_
  79.9 0.0 collective-permute-start.4
  79.9 0.0 collective-permute-done.10.refs_12_
  79.9 3.7 %collective-permute-start.12 = (bf16[64,1024]{1,0:T(8,128)(2,1)S(1)}, bf16[64,1024]{1,0:T(8,128)(2,1)S(1)}, u32[]{:S(2)}, u32[]{:S(2)}) collective-permute-start(bf16[64,1024]{1,0:T(8,128)(2,1)S(1)} %collective-permute-done.10.refs_12_), channel_id=1, source_target_pairs={{0,7},{1,0},{2,1},{3,2},{4,3},{5,4},{6,5},{7,6},{8,15},{9,8},{10,9... | collective-permute-start | bytes 393224 | tf_op jit(solution)/shard_map/ppermute | solution.py:335
  83.6 0.0 collective-permute-done.3.refs_4_
  83.6 2.6 %collective-permute-start.5 = (bf16[64,1024]{1,0:T(8,128)(2,1)S(1)}, bf16[64,1024]{1,0:T(8,128)(2,1)S(1)}, u32[]{:S(2)}, u32[]{:S(2)}) collective-permute-start(bf16[64,1024]{1,0:T(8,128)(2,1)S(1)} %collective-permute-done.3.refs_4_), channel_id=1, source_target_pairs={{0,7},{1,0},{2,1},{3,2},{4,3},{5,4},{6,5},{7,6},{8,15},{9,8},{10,9... | collective-permute-start | bytes 393224 | tf_op jit(solution)/shard_map/ppermute | solution.py:335
  86.2 0.3 collective-permute-done.9.refs_11_
  86.5 0.0 collective-permute-start.11
  86.5 1.4 %collective-permute-done.4.refs_5_ = bf16[64,1024]{1,0:T(8,128)(2,1)S(1)} collective-permute-done((bf16[64,1024]{1,0:T(8,128)(2,1)S(1)}, bf16[64,1024]{1,0:T(8,128)(2,1)S(1)}, u32[]{:S(2)}, u32[]{:S(2)}) %collective-permute-start.4) | collective-permute-done | bytes 131104 | tf_op jit(solution)/shard_map/ppermute | solution.py:335
  87.9 0.0 collective-permute-start.6
  88.0 0.0 collective-permute-done.12.refs_14_
  88.0 3.2 %collective-permute-start.13 = (bf16[64,1024]{1,0:T(8,128)(2,1)S(1)}, bf16[64,1024]{1,0:T(8,128)(2,1)S(1)}, u32[]{:S(2)}, u32[]{:S(2)}) collective-permute-start(bf16[64,1024]{1,0:T(8,128)(2,1)S(1)} %collective-permute-done.12.refs_14_), channel_id=1, source_target_pairs={{0,7},{1,0},{2,1},{3,2},{4,3},{5,4},{6,5},{7,6},{8,15},{9,8},{10,9... | collective-permute-start | bytes 393224 | tf_op jit(solution)/shard_map/ppermute | solution.py:335
  91.2 0.0 collective-permute-done.5.refs_6_
  91.2 1.8 %collective-permute-done.11.refs_13_ = bf16[64,1024]{1,0:T(8,128)(2,1)S(1)} collective-permute-done((bf16[64,1024]{1,0:T(8,128)(2,1)S(1)}, bf16[64,1024]{1,0:T(8,128)(2,1)S(1)}, u32[]{:S(2)}, u32[]{:S(2)}) %collective-permute-start.11) | collective-permute-done | bytes 131104 | tf_op jit(solution)/shard_map/ppermute | solution.py:335
  93.0 1.4 %collective-permute-done.6.refs_7_ = bf16[64,1024]{1,0:T(8,128)(2,1)S(1)} collective-permute-done((bf16[64,1024]{1,0:T(8,128)(2,1)S(1)}, bf16[64,1024]{1,0:T(8,128)(2,1)S(1)}, u32[]{:S(2)}, u32[]{:S(2)}) %collective-permute-start.6) | collective-permute-done | bytes 131104 | tf_op jit(solution)/shard_map/ppermute | solution.py:335
  94.4 0.0 collective-permute-done.13.refs_15_
  94.4 2.4 %histories.1 = bf16[4,512,1024]{2,1,0:T(8,128)(2,1)} custom-call(bf16[512,256]{1,0:T(8,128)(2,1)S(1)} %select_convert_fusion.basis_ref, bf16[64,1024]{1,0:T(8,128)(2,1)S(1)} %get-tuple-element.17.refs_0_, bf16[64,1024]{1,0:T(8,128)(2,1)S(1)} %collective-permute-done.refs_1_, bf16[64,1024]{1,0:T(8,128)(2,1)S(1)} %collective-permute-done.1.refs_2_, ...), custom_call_target="tpu_custom_call" | custom-call | flops 1073741824 | bytes 6291456 | tf_op jit(solution)/shard_map/histories/pallas_call | solution.py:277
  (6 shorter events, 0.0 us)
Async XLA Ops:
  0.0 16.9 %copy-start.2 = (s32[8]{0:T(128)S(1)}, s32[8]{0:T(128)}, u32[]{:S(2)}) copy-start(s32[8]{0:T(128)} %constant.63.clone) | copy-start | bytes 100
  0.0 17.1 %copy-start.1 = (s32[1,8,256,1]{2,3,1,0:T(1,128)S(1)}, s32[1,8,256,1]{2,3,1,0:T(1,128)}, u32[]{:S(2)}) copy-start(s32[1,8,256,1]{2,3,1,0:T(1,128)} %param.9) | copy-start | bytes 24580
  0.0 17.2 %copy-start = (bf16[1,8,256,128]{3,2,1,0:T(8,128)(2,1)S(1)}, bf16[1,8,256,128]{3,2,1,0:T(8,128)(2,1)}, u32[]{:S(2)}) copy-start(bf16[1,8,256,128]{3,2,1,0:T(8,128)(2,1)} %param.10) | copy-start | bytes 1572868
  2.2 34.8 %all-to-all-start = ((bf16[256,4,256]{2,1,0:T(4,128)(2,1)}), bf16[256,4,256]{2,1,0:T(4,128)(2,1)S(1)}, u32[]{:S(2)}, u32[]{:S(2)}) async-start(bf16[256,4,256]{2,1,0:T(4,128)(2,1)} %bitcast.12), calls=%async_computation | async-start | bytes 1048576 | tf_op jit(solution)/shard_map/all_to_all | solution.py:315
  66.0 7.5 %collective-permute-start = (bf16[64,1024]{1,0:T(8,128)(2,1)S(1)}, bf16[64,1024]{1,0:T(8,128)(2,1)S(1)}, u32[]{:S(2)}, u32[]{:S(2)}) collective-permute-start(bf16[64,1024]{1,0:T(8,128)(2,1)S(1)} %get-tuple-element.17.refs_0_), channel_id=1, source_target_pairs={{0,1},{1,2},{2,3},{3,4},{4,5},{5,6},{6,7},{7,0},{8,9},{9,10},{10,1... | collective-permute-start | bytes 393224 | tf_op jit(solution)/shard_map/ppermute | solution.py:335
  67.2 6.4 %collective-permute-start.8 = (bf16[64,1024]{1,0:T(8,128)(2,1)S(1)}, bf16[64,1024]{1,0:T(8,128)(2,1)S(1)}, u32[]{:S(2)}, u32[]{:S(2)}) collective-permute-start(bf16[64,1024]{1,0:T(8,128)(2,1)S(1)} %get-tuple-element.18.refs_8_), channel_id=1, source_target_pairs={{0,7},{1,0},{2,1},{3,2},{4,3},{5,4},{6,5},{7,6},{8,15},{9,8},{10,9... | collective-permute-start | bytes 393224 | tf_op jit(solution)/shard_map/ppermute | solution.py:335
  69.3 7.6 %collective-permute-start.1 = (bf16[64,1024]{1,0:T(8,128)(2,1)S(1)}, bf16[64,1024]{1,0:T(8,128)(2,1)S(1)}, u32[]{:S(2)}, u32[]{:S(2)}) collective-permute-start(bf16[64,1024]{1,0:T(8,128)(2,1)S(1)} %get-tuple-element.17.refs_0_), channel_id=1, source_target_pairs={{0,7},{1,0},{2,1},{3,2},{4,3},{5,4},{6,5},{7,6},{8,15},{9,8},{10,9... | collective-permute-start | bytes 393224 | tf_op jit(solution)/shard_map/ppermute | solution.py:335
  69.4 9.8 %collective-permute-start.7 = (bf16[64,1024]{1,0:T(8,128)(2,1)S(1)}, bf16[64,1024]{1,0:T(8,128)(2,1)S(1)}, u32[]{:S(2)}, u32[]{:S(2)}) collective-permute-start(bf16[64,1024]{1,0:T(8,128)(2,1)S(1)} %get-tuple-element.18.refs_8_), channel_id=1, source_target_pairs={{0,1},{1,2},{2,3},{3,4},{4,5},{5,6},{6,7},{7,0},{8,9},{9,10},{10,1... | collective-permute-start | bytes 393224 | tf_op jit(solution)/shard_map/ppermute | solution.py:335
  73.6 6.4 %collective-permute-start.2 = (bf16[64,1024]{1,0:T(8,128)(2,1)S(1)}, bf16[64,1024]{1,0:T(8,128)(2,1)S(1)}, u32[]{:S(2)}, u32[]{:S(2)}) collective-permute-start(bf16[64,1024]{1,0:T(8,128)(2,1)S(1)} %collective-permute-done.refs_1_), channel_id=1, source_target_pairs={{0,1},{1,2},{2,3},{3,4},{4,5},{5,6},{6,7},{7,0},{8,9},{9,10},{10,1... | collective-permute-start | bytes 393224 | tf_op jit(solution)/shard_map/ppermute | solution.py:335
  73.6 6.4 %collective-permute-start.10 = (bf16[64,1024]{1,0:T(8,128)(2,1)S(1)}, bf16[64,1024]{1,0:T(8,128)(2,1)S(1)}, u32[]{:S(2)}, u32[]{:S(2)}) collective-permute-start(bf16[64,1024]{1,0:T(8,128)(2,1)S(1)} %collective-permute-done.8.refs_10_), channel_id=1, source_target_pairs={{0,7},{1,0},{2,1},{3,2},{4,3},{5,4},{6,5},{7,6},{8,15},{9,8},{10,9... | collective-permute-start | bytes 393224 | tf_op jit(solution)/shard_map/ppermute | solution.py:335
  76.9 6.7 %collective-permute-start.3 = (bf16[64,1024]{1,0:T(8,128)(2,1)S(1)}, bf16[64,1024]{1,0:T(8,128)(2,1)S(1)}, u32[]{:S(2)}, u32[]{:S(2)}) collective-permute-start(bf16[64,1024]{1,0:T(8,128)(2,1)S(1)} %collective-permute-done.1.refs_2_), channel_id=1, source_target_pairs={{0,7},{1,0},{2,1},{3,2},{4,3},{5,4},{6,5},{7,6},{8,15},{9,8},{10,9... | collective-permute-start | bytes 393224 | tf_op jit(solution)/shard_map/ppermute | solution.py:335
  79.2 7.3 %collective-permute-start.9 = (bf16[64,1024]{1,0:T(8,128)(2,1)S(1)}, bf16[64,1024]{1,0:T(8,128)(2,1)S(1)}, u32[]{:S(2)}, u32[]{:S(2)}) collective-permute-start(bf16[64,1024]{1,0:T(8,128)(2,1)S(1)} %collective-permute-done.7.refs_9_), channel_id=1, source_target_pairs={{0,1},{1,2},{2,3},{3,4},{4,5},{5,6},{6,7},{7,0},{8,9},{9,10},{10,1... | collective-permute-start | bytes 393224 | tf_op jit(solution)/shard_map/ppermute | solution.py:335
  79.9 8.0 %collective-permute-start.4 = (bf16[64,1024]{1,0:T(8,128)(2,1)S(1)}, bf16[64,1024]{1,0:T(8,128)(2,1)S(1)}, u32[]{:S(2)}, u32[]{:S(2)}) collective-permute-start(bf16[64,1024]{1,0:T(8,128)(2,1)S(1)} %collective-permute-done.2.refs_3_), channel_id=1, source_target_pairs={{0,1},{1,2},{2,3},{3,4},{4,5},{5,6},{6,7},{7,0},{8,9},{9,10},{10,1... | collective-permute-start | bytes 393224 | tf_op jit(solution)/shard_map/ppermute | solution.py:335
  79.9 8.0 %collective-permute-start.12 = (bf16[64,1024]{1,0:T(8,128)(2,1)S(1)}, bf16[64,1024]{1,0:T(8,128)(2,1)S(1)}, u32[]{:S(2)}, u32[]{:S(2)}) collective-permute-start(bf16[64,1024]{1,0:T(8,128)(2,1)S(1)} %collective-permute-done.10.refs_12_), channel_id=1, source_target_pairs={{0,7},{1,0},{2,1},{3,2},{4,3},{5,4},{6,5},{7,6},{8,15},{9,8},{10,9... | collective-permute-start | bytes 393224 | tf_op jit(solution)/shard_map/ppermute | solution.py:335
  83.6 7.6 %collective-permute-start.5 = (bf16[64,1024]{1,0:T(8,128)(2,1)S(1)}, bf16[64,1024]{1,0:T(8,128)(2,1)S(1)}, u32[]{:S(2)}, u32[]{:S(2)}) collective-permute-start(bf16[64,1024]{1,0:T(8,128)(2,1)S(1)} %collective-permute-done.3.refs_4_), channel_id=1, source_target_pairs={{0,7},{1,0},{2,1},{3,2},{4,3},{5,4},{6,5},{7,6},{8,15},{9,8},{10,9... | collective-permute-start | bytes 393224 | tf_op jit(solution)/shard_map/ppermute | solution.py:335
  86.5 6.5 %collective-permute-start.11 = (bf16[64,1024]{1,0:T(8,128)(2,1)S(1)}, bf16[64,1024]{1,0:T(8,128)(2,1)S(1)}, u32[]{:S(2)}, u32[]{:S(2)}) collective-permute-start(bf16[64,1024]{1,0:T(8,128)(2,1)S(1)} %collective-permute-done.9.refs_11_), channel_id=1, source_target_pairs={{0,1},{1,2},{2,3},{3,4},{4,5},{5,6},{6,7},{7,0},{8,9},{9,10},{10,1... | collective-permute-start | bytes 393224 | tf_op jit(solution)/shard_map/ppermute | solution.py:335
  87.9 6.5 %collective-permute-start.6 = (bf16[64,1024]{1,0:T(8,128)(2,1)S(1)}, bf16[64,1024]{1,0:T(8,128)(2,1)S(1)}, u32[]{:S(2)}, u32[]{:S(2)}) collective-permute-start(bf16[64,1024]{1,0:T(8,128)(2,1)S(1)} %collective-permute-done.4.refs_5_), channel_id=1, source_target_pairs={{0,1},{1,2},{2,3},{3,4},{4,5},{5,6},{6,7},{7,0},{8,9},{9,10},{10,1... | collective-permute-start | bytes 393224 | tf_op jit(solution)/shard_map/ppermute | solution.py:335
  88.0 6.5 %collective-permute-start.13 = (bf16[64,1024]{1,0:T(8,128)(2,1)S(1)}, bf16[64,1024]{1,0:T(8,128)(2,1)S(1)}, u32[]{:S(2)}, u32[]{:S(2)}) collective-permute-start(bf16[64,1024]{1,0:T(8,128)(2,1)S(1)} %collective-permute-done.12.refs_14_), channel_id=1, source_target_pairs={{0,7},{1,0},{2,1},{3,2},{4,3},{5,4},{6,5},{7,6},{8,15},{9,8},{10,9... | collective-permute-start | bytes 393224 | tf_op jit(solution)/shard_map/ppermute | solution.py:335
